TPU v7x, 32 devices: a whole 2x2x4 slice. The times are simulated.
32 devices in a mesh: tm: 8 (over z, x), head: 4 (over y, core).
Axes of the slice: x: 2, y: 2, z: 4, core: 2. Of those that a mesh axis runs over, the one named last changes fastest.
Arguments:
- tokens_in: bfloat16 [4096, 1024], P('tm', 'head'), may hold values from -12 to 12
- conv_weight: bfloat16 [16, 192, 64], P('head'), may hold values from -0.4375 to 0.4375
- conv_bias: float32 [1024], P('head'), may hold values from -3 to 3
- norm_gain: bfloat16 [1024], P('head'), may hold values from 0.099609375 to 1.8984375
- w_query: bfloat16 [1024, 1024], P(None, 'head')
- w_key: bfloat16 [1024, 1024], P(None, 'head')
- w_value: bfloat16 [1024, 1024], P(None, 'head'), may hold values from -0.1875 to 0.1875
- w_out: bfloat16 [1024, 1024], P('head'), may hold values from -0.1875 to 0.1875
- valid_count: int32 [4], replicated, may hold values from 512 to 1024, as said below
Outputs:
- block_out: bfloat16 [4096, 1024], P('tm', 'head')
Inputs may be any that keep to these rules, and one draw needn't show every extreme that they name: `valid_count`: in every draw some stretch is fully valid and some stretch has exactly 512 valid tokens.
All inputs are finite; a program needn't handle non-finite values.
Results may differ from a plain program's by a relative error of at most 0.019.
Values may be sent and summed in bfloat16 or wider, within the bound.
No kernel may reach another device: no remote copies, remote signals or barrier semaphores. Data moves between devices by JAX's collectives and lax.ppermute only.
A program may use at most 192 MiB of HBM per device.

v0:
```python
import jax
import jax.numpy as jnp
from jax import lax
from jax.sharding import PartitionSpec as P

D = 1024
HEAD_DIM = 64
KERNEL = 3
DILATION = 4
STRETCH = 1024
WINDOW = 8


def from_behind(value, axis, steps):
    count = lax.axis_size(axis)
    first, last = (max(0, -steps), min(count, count - steps))
    return lax.ppermute(value, axis, [(source, source + steps) for source in range(first, last)])


def on_device(
    tokens_in, conv_weight, conv_bias, norm_gain, w_query, w_key, w_value, w_out, valid_count
):
    tok = tokens_in.shape[0]
    local_groups = conv_weight.shape[0]
    width = conv_weight.shape[2]
    rim = (KERNEL - 1) * DILATION
    before = from_behind(tokens_in[tok - rim :], "tm", 1)
    extended = jnp.concatenate([before, tokens_in], axis=0)
    taps = [extended[j * DILATION : j * DILATION + tok] for j in range(KERNEL)]
    stacked = jnp.stack(taps, 1).reshape(tok, KERNEL, local_groups, width)
    stacked = jnp.transpose(stacked, (0, 2, 1, 3)).reshape(tok, local_groups, KERNEL * width)
    conv_term = jnp.einsum("tgi,gio->tgo", stacked, conv_weight, preferred_element_type=jnp.float32)
    conv_term = conv_term.reshape(tok, local_groups * width)
    mixed = (
        tokens_in.astype(jnp.float32) + jax.nn.gelu(conv_term + conv_bias, approximate=True)
    ).astype(jnp.bfloat16)
    mixed32 = mixed.astype(jnp.float32)
    weights_all = jnp.concatenate([w_query, w_key, w_value], axis=1)
    local_cols = w_query.shape[1]
    square_part = jnp.sum(mixed32 * mixed32, axis=1)
    square_tot = lax.psum(square_part, "head")
    rstd = lax.rsqrt(square_tot / D + 1e-06)
    normed = (mixed32 * rstd[:, None] * norm_gain.astype(jnp.float32)).astype(jnp.bfloat16)
    projected = jnp.dot(
        lax.all_gather(normed, "head", axis=1, tiled=True),
        weights_all,
        preferred_element_type=jnp.float32,
    )
    projected = projected.astype(jnp.bfloat16)
    local_heads = local_cols // HEAD_DIM
    query = projected[:, :local_cols].reshape(tok, local_heads, HEAD_DIM)
    keys_own = projected[:, local_cols : 2 * local_cols]
    values_own = projected[:, 2 * local_cols :]
    scale = 1.0 / HEAD_DIM**0.5
    shard = lax.axis_index("tm")
    q_pos = shard * tok + jnp.arange(tok, dtype=jnp.int32)
    stretch_ids = jnp.arange(valid_count.shape[0], dtype=jnp.int32)

    def attend(state, keys_blk, values_blk, source):
        top, total, accum = state
        k_pos = source * tok + jnp.arange(tok, dtype=jnp.int32)
        k_stretch = jnp.where(k_pos >= 0, k_pos // STRETCH, -1)
        counts = jnp.sum(
            jnp.where(k_stretch[:, None] == stretch_ids[None, :], valid_count[None, :], 0), axis=1
        )
        key_ok = (k_pos >= 0) & (k_pos % STRETCH < counts)
        allowed = key_ok[None, :] & (k_pos[None, :] <= q_pos[:, None])
        allowed = allowed & (k_pos[None, :] // STRETCH >= q_pos[:, None] // STRETCH - WINDOW)
        keys3 = keys_blk.reshape(tok, local_heads, HEAD_DIM)
        values3 = values_blk.reshape(tok, local_heads, HEAD_DIM)
        scores = (
            jnp.einsum("qhd,khd->hqk", query, keys3, preferred_element_type=jnp.float32) * scale
        )
        block_top = jnp.max(jnp.where(allowed[None], scores, -1e30), axis=2)
        new_top = jnp.maximum(top, block_top)
        weights = jnp.where(allowed[None], jnp.exp(scores - new_top[:, :, None]), 0.0)
        factor = jnp.exp(top - new_top)
        total = total * factor + jnp.sum(weights, axis=2)
        accum = accum * factor[:, :, None] + jnp.einsum(
            "hqk,khd->hqd",
            weights.astype(jnp.bfloat16),
            values3,
            preferred_element_type=jnp.float32,
        )
        return (new_top, total, accum)

    state = (
        jnp.full((local_heads, tok), -1e30, jnp.float32),
        jnp.zeros((local_heads, tok), jnp.float32),
        jnp.zeros((local_heads, tok, HEAD_DIM), jnp.float32),
    )
    state = attend(state, keys_own, values_own, shard)
    reach = (WINDOW * STRETCH + max(STRETCH - tok, 0) + tok - 1) // tok
    steps_back = min(reach, lax.axis_size("tm") - 1)

    def relay_step(step, carry):
        keys_blk, values_blk, inner = carry
        keys_blk, values_blk = from_behind((keys_blk, values_blk), "tm", 1)
        inner = attend(inner, keys_blk, values_blk, shard - step)
        return (keys_blk, values_blk, inner)

    carried = lax.fori_loop(1, steps_back + 1, relay_step, (keys_own, values_own, state))
    state = carried[2]
    top, total, accum = state
    attended = (accum / total[:, :, None]).astype(jnp.bfloat16)
    attended = jnp.transpose(attended, (1, 0, 2)).reshape(tok, local_cols)
    partial_proj = jnp.dot(attended, w_out, preferred_element_type=jnp.float32)
    proj = lax.psum_scatter(
        partial_proj.astype(jnp.bfloat16), "head", scatter_dimension=1, tiled=True
    ).astype(jnp.float32)
    return (mixed32 + proj).astype(jnp.bfloat16)


def solution(mesh):
    return jax.shard_map(
        on_device,
        mesh=mesh,
        in_specs=(
            P("tm", "head"),
            P("head", None, None),
            P("head"),
            P("head"),
            P(None, "head"),
            P(None, "head"),
            P(None, "head"),
            P("head", None),
            P(),
        ),
        out_specs=P("tm", "head"),
        check_vma=False,
    )
```

profile of v0, /device:TPU:0, one launch (start us, length us, event | category | flops | bytes accessed | tf_op | source)
XLA Modules:
  0.0 194.8 jit_solution(11904148265090692551)
XLA Ops:
  7.5 4.8 %collective-permute-start.2 = (bf16[8,256]{0,1:T(8,128)(2,1)S(1)}, bf16[8,256]{0,1:T(8,128)(2,1)S(1)}, u32[]{:S(2)}, u32[]{:S(2)}) collective-permute-start(bf16[8,256]{0,1:T(8,128)(2,1)S(1)} %copy.35), channel_id=1, source_target_pairs={{0,4},{4,8},{8,12},{12,16},{16,20},{20,24},{24,28},{1,5},{5,9},{9,... | collective-permute-start | bytes 12296 | tf_op jit(solution)/shard_map/ppermute | solution.py:17
  12.3 1.1 copy.36
  15.5 6.2 %psum.7 = f32[512]{0:T(512)S(1)} all-reduce(f32[512]{0:T(512)S(1)} %get-tuple-element.441), channel_id=1, replica_groups=mesh['tm'=8,'head'=4] {'head'}, use_global_device_ids=true, to_apply=%region_1.0 | all-reduce | flops 512 | bytes 4096 | tf_op jit(solution)/shard_map/psum | solution.py:41
  23.1 18.2 %all-gather.2.cloned.1.call-done = bf16[512,1024]{1,0:T(8,128)(2,1)} async-done(((bf16[512,256]{1,0:T(8,128)(2,1)}), bf16[512,1024]{1,0:T(8,128)(2,1)}) %all-gather.2.cloned.1.call-update) | async-done | bytes 1048592 | tf_op jit(solution)/shard_map/all_gather | solution.py:45
  41.4 2.3 %fusion.39 = bf16[512,768]{1,0:T(8,128)(2,1)S(1)} fusion(bf16[512,1024]{1,0:T(8,128)(2,1)} %all-gather.2.cloned.1.call-done, bf16[1024,256]{1,0:T(8,128)(2,1)S(1)} %copy-done.6, bf16[1024,256]{1,0:T(8,128)(2,1)S(1)} %copy-done.7, bf16[1024,256]{1,0:T(8,128)(2,1)} %param.15), kind=kOutput, calls=%fused_computation.54 | convolution fusion | flops 810418176 | bytes 3407872 | tf_op jit(solution)/shard_map/dot_general | solution.py:44
  45.0 1.9 copy-done.1
  46.9 0.9 fusion.29
  48.0 3.2 %fusion.42 = f32[4,512,64]{1,2,0:T(8,128)S(1)} fusion(bf16[512,4,64]{0,2,1:T(8,128)(2,1)S(1)} %bitcast.52, f32[4,512,512]{1,2,0:T(8,128)} %copy-done.1, f32[4,512]{1,0:T(4,128)S(1)} %broadcast_maximum_fusion, pred[512,512]{0,1:T(8,128)(4,1)S(1)} %compare_and_fusion.1, f32[4,512]{1,0:T(4,128)S(1)} %get-tuple-element.454), kind=kOutput, calls=%fused_computation.55 | convolution fusion | flops 138543104 | bytes 5259264 | tf_op jit(solution)/shard_map/hqk,khd->hqd/dot_general | solution.py:79
  51.2 108.6 %while.26 = (s32[]{:T(128)}, bf16[512,256]{0,1:T(8,128)(2,1)S(1)}, bf16[512,256]{0,1:T(8,128)(2,1)S(1)}, f32[4,512]{1,0:T(4,128)S(1)}, f32[4,512]{1,0:T(4,128)S(...) while((s32[]{:T(128)}, bf16[512,256]{0,1:T(8,128)(2,1)S(1)}, ...), condition=%wide.region_9.10_spmd.clone.clone, body=%wide.region_5.9_spmd.clone.clone.sunk | while | flops 281325056 | bytes 18774276 | solution.py:102
  51.2 3.4 %collective-permute-start = (bf16[512,256]{0,1:T(8,128)(2,1)S(1)}, bf16[512,256]{0,1:T(8,128)(2,1)S(1)}, u32[]{:S(2)}, u32[]{:S(2)}) collective-permute-start(bf16[512,256]{0,1:T(8,128)(2,1)S(1)} %get-tuple-element.552), channel_id=1, source_target_pairs={{0,4},{4,8},{8,12},{12,16},{16,20},{20,24},{24,28},{1,5},{5,9},{9,... | collective-permute-start | bytes 786440 | tf_op jit(solution)/shard_map/while/body/eval_jaxpr/ppermute | solution.py:17
  54.6 3.4 %collective-permute-start.1 = (bf16[512,256]{0,1:T(8,128)(2,1)S(1)}, bf16[512,256]{0,1:T(8,128)(2,1)S(1)}, u32[]{:S(2)}, u32[]{:S(2)}) collective-permute-start(bf16[512,256]{0,1:T(8,128)(2,1)S(1)} %get-tuple-element.553), channel_id=1, source_target_pairs={{0,4},{4,8},{8,12},{12,16},{16,20},{20,24},{24,28},{1,5},{5,9},{9,... | collective-permute-start | bytes 786440 | tf_op jit(solution)/shard_map/while/body/eval_jaxpr/ppermute | solution.py:17
  58.6 2.7 %collective-permute-done = bf16[512,256]{0,1:T(8,128)(2,1)S(1)} collective-permute-done((bf16[512,256]{0,1:T(8,128)(2,1)S(1)}, bf16[512,256]{0,1:T(8,128)(2,1)S(1)}, u32[]{:S(2)}, u32[]{:S(2)}) %collective-permute-start) | collective-permute-done | bytes 262176 | tf_op jit(solution)/shard_map/while/body/eval_jaxpr/ppermute | solution.py:17
  61.2 0.9 select_reduce_fusion.7
  63.1 3.1 %collective-permute-done.1 = bf16[512,256]{0,1:T(8,128)(2,1)S(1)} collective-permute-done((bf16[512,256]{0,1:T(8,128)(2,1)S(1)}, bf16[512,256]{0,1:T(8,128)(2,1)S(1)}, u32[]{:S(2)}, u32[]{:S(2)}) %collective-permute-start.1) | collective-permute-done | bytes 262176 | tf_op jit(solution)/shard_map/while/body/eval_jaxpr/ppermute | solution.py:17
  66.2 1.1 fusion.103
  67.4 4.4 %collective-permute-start = (bf16[512,256]{0,1:T(8,128)(2,1)S(1)}, bf16[512,256]{0,1:T(8,128)(2,1)S(1)}, u32[]{:S(2)}, u32[]{:S(2)}) collective-permute-start(bf16[512,256]{0,1:T(8,128)(2,1)S(1)} %get-tuple-element.552), channel_id=1, source_target_pairs={{0,4},{4,8},{8,12},{12,16},{16,20},{20,24},{24,28},{1,5},{5,9},{9,... | collective-permute-start | bytes 786440 | tf_op jit(solution)/shard_map/while/body/eval_jaxpr/ppermute | solution.py:17
  71.8 4.3 %collective-permute-start.1 = (bf16[512,256]{0,1:T(8,128)(2,1)S(1)}, bf16[512,256]{0,1:T(8,128)(2,1)S(1)}, u32[]{:S(2)}, u32[]{:S(2)}) collective-permute-start(bf16[512,256]{0,1:T(8,128)(2,1)S(1)} %get-tuple-element.553), channel_id=1, source_target_pairs={{0,4},{4,8},{8,12},{12,16},{16,20},{20,24},{24,28},{1,5},{5,9},{9,... | collective-permute-start | bytes 786440 | tf_op jit(solution)/shard_map/while/body/eval_jaxpr/ppermute | solution.py:17
  76.6 1.9 collective-permute-done
  80.4 2.2 %collective-permute-done.1 = bf16[512,256]{0,1:T(8,128)(2,1)S(1)} collective-permute-done((bf16[512,256]{0,1:T(8,128)(2,1)S(1)}, bf16[512,256]{0,1:T(8,128)(2,1)S(1)}, u32[]{:S(2)}, u32[]{:S(2)}) %collective-permute-start.1) | collective-permute-done | bytes 262176 | tf_op jit(solution)/shard_map/while/body/eval_jaxpr/ppermute | solution.py:17
  82.5 1.1 fusion.103
  83.7 4.4 %collective-permute-start = (bf16[512,256]{0,1:T(8,128)(2,1)S(1)}, bf16[512,256]{0,1:T(8,128)(2,1)S(1)}, u32[]{:S(2)}, u32[]{:S(2)}) collective-permute-start(bf16[512,256]{0,1:T(8,128)(2,1)S(1)} %get-tuple-element.552), channel_id=1, source_target_pairs={{0,4},{4,8},{8,12},{12,16},{16,20},{20,24},{24,28},{1,5},{5,9},{9,... | collective-permute-start | bytes 786440 | tf_op jit(solution)/shard_map/while/body/eval_jaxpr/ppermute | solution.py:17
  88.1 5.2 %collective-permute-start.1 = (bf16[512,256]{0,1:T(8,128)(2,1)S(1)}, bf16[512,256]{0,1:T(8,128)(2,1)S(1)}, u32[]{:S(2)}, u32[]{:S(2)}) collective-permute-start(bf16[512,256]{0,1:T(8,128)(2,1)S(1)} %get-tuple-element.553), channel_id=1, source_target_pairs={{0,4},{4,8},{8,12},{12,16},{16,20},{20,24},{24,28},{1,5},{5,9},{9,... | collective-permute-start | bytes 786440 | tf_op jit(solution)/shard_map/while/body/eval_jaxpr/ppermute | solution.py:17
  93.9 0.9 select_reduce_fusion.7
  95.8 2.2 %collective-permute-done.1 = bf16[512,256]{0,1:T(8,128)(2,1)S(1)} collective-permute-done((bf16[512,256]{0,1:T(8,128)(2,1)S(1)}, bf16[512,256]{0,1:T(8,128)(2,1)S(1)}, u32[]{:S(2)}, u32[]{:S(2)}) %collective-permute-start.1) | collective-permute-done | bytes 262176 | tf_op jit(solution)/shard_map/while/body/eval_jaxpr/ppermute | solution.py:17
  98.0 1.1 fusion.103
  99.1 5.2 %collective-permute-start = (bf16[512,256]{0,1:T(8,128)(2,1)S(1)}, bf16[512,256]{0,1:T(8,128)(2,1)S(1)}, u32[]{:S(2)}, u32[]{:S(2)}) collective-permute-start(bf16[512,256]{0,1:T(8,128)(2,1)S(1)} %get-tuple-element.552), channel_id=1, source_target_pairs={{0,4},{4,8},{8,12},{12,16},{16,20},{20,24},{24,28},{1,5},{5,9},{9,... | collective-permute-start | bytes 786440 | tf_op jit(solution)/shard_map/while/body/eval_jaxpr/ppermute | solution.py:17
  104.3 5.3 %collective-permute-start.1 = (bf16[512,256]{0,1:T(8,128)(2,1)S(1)}, bf16[512,256]{0,1:T(8,128)(2,1)S(1)}, u32[]{:S(2)}, u32[]{:S(2)}) collective-permute-start(bf16[512,256]{0,1:T(8,128)(2,1)S(1)} %get-tuple-element.553), channel_id=1, source_target_pairs={{0,4},{4,8},{8,12},{12,16},{16,20},{20,24},{24,28},{1,5},{5,9},{9,... | collective-permute-start | bytes 786440 | tf_op jit(solution)/shard_map/while/body/eval_jaxpr/ppermute | solution.py:17
  110.2 0.9 select_reduce_fusion.7
  112.1 1.7 collective-permute-done.1
  113.8 1.1 fusion.103
  115.0 4.7 %collective-permute-start = (bf16[512,256]{0,1:T(8,128)(2,1)S(1)}, bf16[512,256]{0,1:T(8,128)(2,1)S(1)}, u32[]{:S(2)}, u32[]{:S(2)}) collective-permute-start(bf16[512,256]{0,1:T(8,128)(2,1)S(1)} %get-tuple-element.552), channel_id=1, source_target_pairs={{0,4},{4,8},{8,12},{12,16},{16,20},{20,24},{24,28},{1,5},{5,9},{9,... | collective-permute-start | bytes 786440 | tf_op jit(solution)/shard_map/while/body/eval_jaxpr/ppermute | solution.py:17
  119.7 5.3 %collective-permute-start.1 = (bf16[512,256]{0,1:T(8,128)(2,1)S(1)}, bf16[512,256]{0,1:T(8,128)(2,1)S(1)}, u32[]{:S(2)}, u32[]{:S(2)}) collective-permute-start(bf16[512,256]{0,1:T(8,128)(2,1)S(1)} %get-tuple-element.553), channel_id=1, source_target_pairs={{0,4},{4,8},{8,12},{12,16},{16,20},{20,24},{24,28},{1,5},{5,9},{9,... | collective-permute-start | bytes 786440 | tf_op jit(solution)/shard_map/while/body/eval_jaxpr/ppermute | solution.py:17
  127.6 1.6 collective-permute-done.1
  129.2 1.1 fusion.103
  130.4 4.4 %collective-permute-start = (bf16[512,256]{0,1:T(8,128)(2,1)S(1)}, bf16[512,256]{0,1:T(8,128)(2,1)S(1)}, u32[]{:S(2)}, u32[]{:S(2)}) collective-permute-start(bf16[512,256]{0,1:T(8,128)(2,1)S(1)} %get-tuple-element.552), channel_id=1, source_target_pairs={{0,4},{4,8},{8,12},{12,16},{16,20},{20,24},{24,28},{1,5},{5,9},{9,... | collective-permute-start | bytes 786440 | tf_op jit(solution)/shard_map/while/body/eval_jaxpr/ppermute | solution.py:17
  134.8 4.7 %collective-permute-start.1 = (bf16[512,256]{0,1:T(8,128)(2,1)S(1)}, bf16[512,256]{0,1:T(8,128)(2,1)S(1)}, u32[]{:S(2)}, u32[]{:S(2)}) collective-permute-start(bf16[512,256]{0,1:T(8,128)(2,1)S(1)} %get-tuple-element.553), channel_id=1, source_target_pairs={{0,4},{4,8},{8,12},{12,16},{16,20},{20,24},{24,28},{1,5},{5,9},{9,... | collective-permute-start | bytes 786440 | tf_op jit(solution)/shard_map/while/body/eval_jaxpr/ppermute | solution.py:17
  140.9 0.9 select_reduce_fusion.7
  142.7 0.9 collective-permute-done.1
  143.7 1.1 fusion.103
  144.9 4.4 %collective-permute-start = (bf16[512,256]{0,1:T(8,128)(2,1)S(1)}, bf16[512,256]{0,1:T(8,128)(2,1)S(1)}, u32[]{:S(2)}, u32[]{:S(2)}) collective-permute-start(bf16[512,256]{0,1:T(8,128)(2,1)S(1)} %get-tuple-element.552), channel_id=1, source_target_pairs={{0,4},{4,8},{8,12},{12,16},{16,20},{20,24},{24,28},{1,5},{5,9},{9,... | collective-permute-start | bytes 786440 | tf_op jit(solution)/shard_map/while/body/eval_jaxpr/ppermute | solution.py:17
  149.3 5.0 %collective-permute-start.1 = (bf16[512,256]{0,1:T(8,128)(2,1)S(1)}, bf16[512,256]{0,1:T(8,128)(2,1)S(1)}, u32[]{:S(2)}, u32[]{:S(2)}) collective-permute-start(bf16[512,256]{0,1:T(8,128)(2,1)S(1)} %get-tuple-element.553), channel_id=1, source_target_pairs={{0,4},{4,8},{8,12},{12,16},{16,20},{20,24},{24,28},{1,5},{5,9},{9,... | collective-permute-start | bytes 786440 | tf_op jit(solution)/shard_map/while/body/eval_jaxpr/ppermute | solution.py:17
  154.9 1.0 collective-permute-done
  155.8 0.9 select_reduce_fusion.7
  157.7 0.9 collective-permute-done.1
  158.7 1.1 fusion.103
  159.9 1.5 convolution_convert_fusion
  161.4 24.9 %reduce-scatter.2.cloned.1.call-done = bf16[512,256]{1,0:T(8,128)(2,1)} async-done(((bf16[512,1024]{1,0:T(8,128)(2,1)}), bf16[512,256]{1,0:T(8,128)(2,1)}) %reduce-scatter.2.cloned.1.call-update) | async-done | bytes 262160 | tf_op jit(solution)/shard_map/reduce_scatter | solution.py:108
  186.3 1.7 fusion.57
  (148 shorter events, 19.0 us)
Async XLA Ops:
  6.5 153.4 %copy-start = (bf16[256,1024]{1,0:T(8,128)(2,1)S(1)}, bf16[256,1024]{1,0:T(8,128)(2,1)}, u32[]{:S(2)}) copy-start(bf16[256,1024]{1,0:T(8,128)(2,1)} %param.18) | copy-start | bytes 1572868
  6.5 8.6 %copy-start.2 = (bf16[512,256]{1,0:T(8,128)(2,1)S(1)}, bf16[512,256]{1,0:T(8,128)(2,1)}, u32[]{:S(2)}) copy-start(bf16[512,256]{1,0:T(8,128)(2,1)} %param.11) | copy-start | bytes 786436
  6.5 8.1 %copy-start.3 = (bf16[4,192,64]{1,2,0:T(8,128)(2,1)S(1)}, bf16[4,192,64]{1,2,0:T(8,128)(2,1)}, u32[]{:S(2)}) copy-start(bf16[4,192,64]{1,2,0:T(8,128)(2,1)} %param.12) | copy-start | bytes 294916
  6.5 8.6 %copy-start.5 = (f32[256]{0:T(256)S(1)}, f32[256]{0:T(256)}, u32[]{:S(2)}) copy-start(f32[256]{0:T(256)} %param.13) | copy-start | bytes 3076
  6.5 34.8 %all-gather.2.cloned.1.call-start = ((), (), s32[]{:S(2)}) async-start(), calls=%async_computation.1 | async-start | bytes 1310720 | tf_op jit(solution)/shard_map/all_gather | solution.py:45
  7.5 6.7 %collective-permute-start.2 = (bf16[8,256]{0,1:T(8,128)(2,1)S(1)}, bf16[8,256]{0,1:T(8,128)(2,1)S(1)}, u32[]{:S(2)}, u32[]{:S(2)}) collective-permute-start(bf16[8,256]{0,1:T(8,128)(2,1)S(1)} %copy.35), channel_id=1, source_target_pairs={{0,4},{4,8},{8,12},{12,16},{16,20},{20,24},{24,28},{1,5},{5,9},{9,... | collective-permute-start | bytes 12296 | tf_op jit(solution)/shard_map/ppermute | solution.py:17
  13.4 9.2 %copy-start.4 = (s32[4]{0:T(128)S(1)}, s32[4]{0:T(128)}, u32[]{:S(2)}) copy-start(s32[4]{0:T(128)} %param.19) | copy-start | bytes 52
  14.1 27.2 %copy-start.6 = (bf16[1024,256]{1,0:T(8,128)(2,1)S(1)}, bf16[1024,256]{1,0:T(8,128)(2,1)}, u32[]{:S(2)}) copy-start(bf16[1024,256]{1,0:T(8,128)(2,1)} %param.17) | copy-start | bytes 1572868
  14.1 27.2 %copy-start.7 = (bf16[1024,256]{1,0:T(8,128)(2,1)S(1)}, bf16[1024,256]{1,0:T(8,128)(2,1)}, u32[]{:S(2)}) copy-start(bf16[1024,256]{1,0:T(8,128)(2,1)} %param.16) | copy-start | bytes 1572868
  22.6 163.7 %reduce-scatter.2.cloned.1.call-start = ((), (), s32[]{:S(2)}) async-start(), calls=%async_computation.2 | async-start | bytes 1310720 | tf_op jit(solution)/shard_map/reduce_scatter | solution.py:108
  45.0 1.9 copy-start.1
  51.2 10.0 %collective-permute-start = (bf16[512,256]{0,1:T(8,128)(2,1)S(1)}, bf16[512,256]{0,1:T(8,128)(2,1)S(1)}, u32[]{:S(2)}, u32[]{:S(2)}) collective-permute-start(bf16[512,256]{0,1:T(8,128)(2,1)S(1)} %get-tuple-element.552), channel_id=1, source_target_pairs={{0,4},{4,8},{8,12},{12,16},{16,20},{20,24},{24,28},{1,5},{5,9},{9,... | collective-permute-start | bytes 786440 | tf_op jit(solution)/shard_map/while/body/eval_jaxpr/ppermute | solution.py:17
  54.6 11.6 %collective-permute-start.1 = (bf16[512,256]{0,1:T(8,128)(2,1)S(1)}, bf16[512,256]{0,1:T(8,128)(2,1)S(1)}, u32[]{:S(2)}, u32[]{:S(2)}) collective-permute-start(bf16[512,256]{0,1:T(8,128)(2,1)S(1)} %get-tuple-element.553), channel_id=1, source_target_pairs={{0,4},{4,8},{8,12},{12,16},{16,20},{20,24},{24,28},{1,5},{5,9},{9,... | collective-permute-start | bytes 786440 | tf_op jit(solution)/shard_map/while/body/eval_jaxpr/ppermute | solution.py:17
  67.4 11.1 %collective-permute-start = (bf16[512,256]{0,1:T(8,128)(2,1)S(1)}, bf16[512,256]{0,1:T(8,128)(2,1)S(1)}, u32[]{:S(2)}, u32[]{:S(2)}) collective-permute-start(bf16[512,256]{0,1:T(8,128)(2,1)S(1)} %get-tuple-element.552), channel_id=1, source_target_pairs={{0,4},{4,8},{8,12},{12,16},{16,20},{20,24},{24,28},{1,5},{5,9},{9,... | collective-permute-start | bytes 786440 | tf_op jit(solution)/shard_map/while/body/eval_jaxpr/ppermute | solution.py:17
  71.8 10.8 %collective-permute-start.1 = (bf16[512,256]{0,1:T(8,128)(2,1)S(1)}, bf16[512,256]{0,1:T(8,128)(2,1)S(1)}, u32[]{:S(2)}, u32[]{:S(2)}) collective-permute-start(bf16[512,256]{0,1:T(8,128)(2,1)S(1)} %get-tuple-element.553), channel_id=1, source_target_pairs={{0,4},{4,8},{8,12},{12,16},{16,20},{20,24},{24,28},{1,5},{5,9},{9,... | collective-permute-start | bytes 786440 | tf_op jit(solution)/shard_map/while/body/eval_jaxpr/ppermute | solution.py:17
  83.7 10.2 %collective-permute-start = (bf16[512,256]{0,1:T(8,128)(2,1)S(1)}, bf16[512,256]{0,1:T(8,128)(2,1)S(1)}, u32[]{:S(2)}, u32[]{:S(2)}) collective-permute-start(bf16[512,256]{0,1:T(8,128)(2,1)S(1)} %get-tuple-element.552), channel_id=1, source_target_pairs={{0,4},{4,8},{8,12},{12,16},{16,20},{20,24},{24,28},{1,5},{5,9},{9,... | collective-permute-start | bytes 786440 | tf_op jit(solution)/shard_map/while/body/eval_jaxpr/ppermute | solution.py:17
  88.1 9.8 %collective-permute-start.1 = (bf16[512,256]{0,1:T(8,128)(2,1)S(1)}, bf16[512,256]{0,1:T(8,128)(2,1)S(1)}, u32[]{:S(2)}, u32[]{:S(2)}) collective-permute-start(bf16[512,256]{0,1:T(8,128)(2,1)S(1)} %get-tuple-element.553), channel_id=1, source_target_pairs={{0,4},{4,8},{8,12},{12,16},{16,20},{20,24},{24,28},{1,5},{5,9},{9,... | collective-permute-start | bytes 786440 | tf_op jit(solution)/shard_map/while/body/eval_jaxpr/ppermute | solution.py:17
  99.1 11.0 %collective-permute-start = (bf16[512,256]{0,1:T(8,128)(2,1)S(1)}, bf16[512,256]{0,1:T(8,128)(2,1)S(1)}, u32[]{:S(2)}, u32[]{:S(2)}) collective-permute-start(bf16[512,256]{0,1:T(8,128)(2,1)S(1)} %get-tuple-element.552), channel_id=1, source_target_pairs={{0,4},{4,8},{8,12},{12,16},{16,20},{20,24},{24,28},{1,5},{5,9},{9,... | collective-permute-start | bytes 786440 | tf_op jit(solution)/shard_map/while/body/eval_jaxpr/ppermute | solution.py:17
  104.3 9.5 %collective-permute-start.1 = (bf16[512,256]{0,1:T(8,128)(2,1)S(1)}, bf16[512,256]{0,1:T(8,128)(2,1)S(1)}, u32[]{:S(2)}, u32[]{:S(2)}) collective-permute-start(bf16[512,256]{0,1:T(8,128)(2,1)S(1)} %get-tuple-element.553), channel_id=1, source_target_pairs={{0,4},{4,8},{8,12},{12,16},{16,20},{20,24},{24,28},{1,5},{5,9},{9,... | collective-permute-start | bytes 786440 | tf_op jit(solution)/shard_map/while/body/eval_jaxpr/ppermute | solution.py:17
  115.0 10.7 %collective-permute-start = (bf16[512,256]{0,1:T(8,128)(2,1)S(1)}, bf16[512,256]{0,1:T(8,128)(2,1)S(1)}, u32[]{:S(2)}, u32[]{:S(2)}) collective-permute-start(bf16[512,256]{0,1:T(8,128)(2,1)S(1)} %get-tuple-element.552), channel_id=1, source_target_pairs={{0,4},{4,8},{8,12},{12,16},{16,20},{20,24},{24,28},{1,5},{5,9},{9,... | collective-permute-start | bytes 786440 | tf_op jit(solution)/shard_map/while/body/eval_jaxpr/ppermute | solution.py:17
  119.7 9.5 %collective-permute-start.1 = (bf16[512,256]{0,1:T(8,128)(2,1)S(1)}, bf16[512,256]{0,1:T(8,128)(2,1)S(1)}, u32[]{:S(2)}, u32[]{:S(2)}) collective-permute-start(bf16[512,256]{0,1:T(8,128)(2,1)S(1)} %get-tuple-element.553), channel_id=1, source_target_pairs={{0,4},{4,8},{8,12},{12,16},{16,20},{20,24},{24,28},{1,5},{5,9},{9,... | collective-permute-start | bytes 786440 | tf_op jit(solution)/shard_map/while/body/eval_jaxpr/ppermute | solution.py:17
  130.4 10.5 %collective-permute-start = (bf16[512,256]{0,1:T(8,128)(2,1)S(1)}, bf16[512,256]{0,1:T(8,128)(2,1)S(1)}, u32[]{:S(2)}, u32[]{:S(2)}) collective-permute-start(bf16[512,256]{0,1:T(8,128)(2,1)S(1)} %get-tuple-element.552), channel_id=1, source_target_pairs={{0,4},{4,8},{8,12},{12,16},{16,20},{20,24},{24,28},{1,5},{5,9},{9,... | collective-permute-start | bytes 786440 | tf_op jit(solution)/shard_map/while/body/eval_jaxpr/ppermute | solution.py:17
  134.8 8.9 %collective-permute-start.1 = (bf16[512,256]{0,1:T(8,128)(2,1)S(1)}, bf16[512,256]{0,1:T(8,128)(2,1)S(1)}, u32[]{:S(2)}, u32[]{:S(2)}) collective-permute-start(bf16[512,256]{0,1:T(8,128)(2,1)S(1)} %get-tuple-element.553), channel_id=1, source_target_pairs={{0,4},{4,8},{8,12},{12,16},{16,20},{20,24},{24,28},{1,5},{5,9},{9,... | collective-permute-start | bytes 786440 | tf_op jit(solution)/shard_map/while/body/eval_jaxpr/ppermute | solution.py:17
  144.9 11.0 %collective-permute-start = (bf16[512,256]{0,1:T(8,128)(2,1)S(1)}, bf16[512,256]{0,1:T(8,128)(2,1)S(1)}, u32[]{:S(2)}, u32[]{:S(2)}) collective-permute-start(bf16[512,256]{0,1:T(8,128)(2,1)S(1)} %get-tuple-element.552), channel_id=1, source_target_pairs={{0,4},{4,8},{8,12},{12,16},{16,20},{20,24},{24,28},{1,5},{5,9},{9,... | collective-permute-start | bytes 786440 | tf_op jit(solution)/shard_map/while/body/eval_jaxpr/ppermute | solution.py:17
  149.3 9.4 %collective-permute-start.1 = (bf16[512,256]{0,1:T(8,128)(2,1)S(1)}, bf16[512,256]{0,1:T(8,128)(2,1)S(1)}, u32[]{:S(2)}, u32[]{:S(2)}) collective-permute-start(bf16[512,256]{0,1:T(8,128)(2,1)S(1)} %get-tuple-element.553), channel_id=1, source_target_pairs={{0,4},{4,8},{8,12},{12,16},{16,20},{20,24},{24,28},{1,5},{5,9},{9,... | collective-permute-start | bytes 786440 | tf_op jit(solution)/shard_map/while/body/eval_jaxpr/ppermute | solution.py:17
Sparse Core Ops, SparseCore 0:
  22.7 18.5 all-gather.1
  161.5 24.6 reduce-scatter.1
where the time goes:
time: 195 us
  starting transfers between devices  69 us (35%)
  waiting for transfers between devices  62.3 us (32%)
  matrix products  22.4 us (11%)
  other arithmetic  15.5 us (8%)
  between operations  13.6 us (7%)
  blocking collectives  6.23 us (3%)
  local copies, waits for them, and re-layouts  4.94 us (3%)
    ppermute x15, starting transfers between devices, from_behind(): lax.ppermute(value, axis, [(source, source + steps) for source in range(f...  68.9 us
    reduce_scatter x1, waiting for transfers between devices, on_device(): lax.psum_scatter(partial_proj.astype(jnp.bfloat16), 'head', scatter_dimen...  24.9 us
    ppermute x15, waiting for transfers between devices, from_behind(): lax.ppermute(value, axis, [(source, source + steps) for source in range(f...  19.2 us
    all_gather x1, waiting for transfers between devices, on_device(): lax.all_gather(normed, 'head', axis=1, tiled=True)  18.2 us
    dot_general x8, matrix products, attend(): jnp.einsum('hqk,khd->hqd', weights.astype(jnp.bfloat16), values3, preferr...  11 us
    dot_general x8, matrix products, attend(): jnp.einsum('qhd,khd->hqk', query, keys3, preferred_element_type=jnp.float32)  7.33 us
    reduce_sum x8, other arithmetic, attend(): total = total * factor + jnp.sum(weights, axis=2)  7.25 us
    psum x1, blocking collectives, on_device(): square_tot = lax.psum(square_part, 'head')  6.23 us
  transfers between devices with their start and end apart: 17, of which 15 were waited for; matrix products, arithmetic and copies ran while one was open for 10% of the time, Pallas kernels for 0%

commit v1 on v0

--- a/solution.py
+++ b/solution.py
@@ -1,6 +1,10 @@
+import functools
+
 import jax
 import jax.numpy as jnp
 from jax import lax
+from jax.experimental import pallas as pl
+from jax.experimental.pallas import tpu as pltpu
 from jax.sharding import PartitionSpec as P
 
 D = 1024
@@ -9,6 +13,11 @@
 DILATION = 4
 STRETCH = 1024
 WINDOW = 8
+RIM = (KERNEL - 1) * DILATION
+GAIN_ROWS = 8
+NEG = -1e30
+F32 = jnp.float32
+BF16 = jnp.bfloat16
 
 
 def from_behind(value, axis, steps):
@@ -17,7 +26,7 @@
     return lax.ppermute(value, axis, [(source, source + steps) for source in range(first, last)])
 
 
-def on_device(
+def ring_on_device(
     tokens_in, conv_weight, conv_bias, norm_gain, w_query, w_key, w_value, w_out, valid_count
 ):
     tok = tokens_in.shape[0]
@@ -111,9 +120,260 @@
     return (mixed32 + proj).astype(jnp.bfloat16)
 
 
+def swap(value, bit):
+    return lax.ppermute(value, "head", [(i, i ^ bit) for i in range(lax.axis_size("head"))])
+
+
+def dot32(a, b):
+    return jnp.dot(a, b, preferred_element_type=F32)
+
+
+def dot_nt(a, b):
+    return lax.dot_general(a, b, (((1,), (1,)), ((), ())), preferred_element_type=F32)
+
+
+def lane_iota(shape):
+    return lax.broadcasted_iota(jnp.int32, shape, 1)
+
+
+def conv_kernel(halo_ref, x_ref, w_ref, b_ref, o_ref):
+    rows = o_ref.shape[0]
+    groups, _, width = w_ref.shape
+    chans = groups * width
+    x32 = x_ref[0:rows, :].astype(F32)
+    ext = jnp.concatenate([halo_ref[...].astype(F32), x32], axis=0)
+    acc = jnp.zeros((rows, chans), F32)
+    for j in range(KERNEL):
+        tap = ext[j * DILATION : j * DILATION + rows].astype(BF16)
+        bands = []
+        for g in range(groups):
+            blk = w_ref[g, j * width : (j + 1) * width, :].astype(F32)
+            parts = []
+            if g > 0:
+                parts.append(jnp.zeros((width, g * width), F32))
+            parts.append(blk)
+            if g < groups - 1:
+                parts.append(jnp.zeros((width, (groups - 1 - g) * width), F32))
+            bands.append(jnp.concatenate(parts, axis=1))
+        acc += dot32(tap, jnp.concatenate(bands, axis=0).astype(BF16))
+    act = jax.nn.gelu(acc + b_ref[...], approximate=True)
+    o_ref[...] = (x32 + act).astype(BF16)
+
+
+def conv_mix(halo, x, weight, bias, rows):
+    return pl.pallas_call(
+        conv_kernel,
+        out_shape=jax.ShapeDtypeStruct((rows, x.shape[1]), BF16),
+        in_specs=[pl.BlockSpec(memory_space=pltpu.VMEM)] * 4,
+        out_specs=pl.BlockSpec(memory_space=pltpu.VMEM),
+    )(halo, x, weight, bias)
+
+
+def qkv_kernel(
+    pos_ref, a_ref, b_ref, y_ref, fa_ref, fb_ref, fy_ref,
+    wq0, wk0, wv0, wq1, wk1, wv1, o_ref,
+):
+    half = o_ref.shape[1] * 2 // 3
+    cols = a_ref.shape[1]
+    core, ychip = pos_ref[0], pos_ref[1]
+    parts = [
+        (a_ref[...], fa_ref[...], 2 * ychip + core),
+        (b_ref[...], fb_ref[...], 2 * ychip + 1 - core),
+        (y_ref[:, :cols], fy_ref[:, :cols], 2 * (1 - ychip) + core),
+        (y_ref[:, cols:], fy_ref[:, cols:], 2 * (1 - ychip) + 1 - core),
+    ]
+    rows = lax.broadcasted_iota(jnp.int32, (RIM, cols), 0)
+    fixed = core == 0
+    xs, square = [], jnp.zeros((half, cols), F32)
+    for main, fix, group in parts:
+        x = main[:half].astype(F32)
+        top = jnp.where(jnp.logical_and(fixed, rows >= 0), fix.astype(F32), x[:RIM])
+        x = jnp.concatenate([top, x[RIM:]], axis=0)
+        gain = main[half : half + 1].astype(F32)
+        square += x * x
+        xs.append((x, gain, group))
+    rstd = lax.rsqrt(jnp.sum(square, axis=1, keepdims=True) / (4 * cols) + 1e-06)
+    normed = [((x * rstd * gain).astype(BF16), group) for x, gain, group in xs]
+
+    def project(w):
+        total = None
+        for x, group in normed:
+            term = dot32(x, w[pl.ds(pl.multiple_of(group * cols, cols), cols), :])
+            total = term if total is None else total + term
+        return total.astype(BF16)
+
+    for first, (wq, wk, wv) in ((core, (wq0, wk0, wv0)), (1 - core, (wq1, wk1, wv1))):
+        q, k, v = project(wq), project(wk), project(wv)
+        q = (q.astype(F32) * (1.0 / HEAD_DIM**0.5)).astype(BF16)
+        heads = cols // HEAD_DIM
+        for j in range(heads):
+            lanes = slice(j * HEAD_DIM, (j + 1) * HEAD_DIM)
+            head = first * heads + j
+            o_ref[head, 0:half, :] = jnp.concatenate([k[:, lanes], v[:, lanes]], axis=1)
+            o_ref[head, half : half + half // 2, :] = jnp.concatenate(
+                [q[: half // 2, lanes], q[half // 2 :, lanes]], axis=1
+            )
+
+
+def attend_kernel(pos_ref, valid_ref, own_ref, oth_ref, o_ref, kb, vb, sc):
+    blocks = own_ref.shape[0]
+    half = o_ref.shape[1] * 2
+    core = pos_ref[0]
+    lane = lane_iota((half, 128))
+    row = lax.broadcasted_iota(jnp.int32, (half, 128), 0)
+    for t in range(blocks):
+        for side, ref in ((0, own_ref), (1, oth_ref)):
+            kv = ref[t, 0:half, :].astype(F32)
+            part = core if side == 0 else 1 - core
+            offset = (2 * half * t) % STRETCH + part * half
+            ok = row + offset < valid_ref[(2 * half * t) // STRETCH]
+            bias = jnp.where(jnp.logical_and(lane == HEAD_DIM, jnp.logical_not(ok)), NEG, 0.0)
+            kb[2 * t + side] = jnp.where(lane < HEAD_DIM, kv, bias).astype(BF16)
+            vb[2 * t + side] = jnp.where(lane < HEAD_DIM, 1.0, kv).astype(BF16)
+    qrow = lax.broadcasted_iota(jnp.int32, (half, half), 0)
+    kcol = lane_iota((half, half))
+    ahead = jnp.where(core == 0, NEG, 0.0)
+    halfrows = half // 2
+    lane_h = lane_iota((halfrows, 128))
+    pad = jnp.where(lane_h == HEAD_DIM, 1.0, 0.0)
+    for t in range(blocks):
+        packed = own_ref[t, half:, :].astype(F32)
+        q = jnp.concatenate(
+            [
+                jnp.where(lane_h < HEAD_DIM, packed, pad),
+                jnp.where(lane_h < HEAD_DIM, pltpu.roll(packed, HEAD_DIM, 1), pad),
+            ],
+            axis=0,
+        ).astype(BF16)
+        top = jnp.full((half, 128), NEG, F32)
+        for b in range(2 * t + 2):
+            s = dot_nt(q, kb[b])
+            if b == 2 * t:
+                s = jnp.where(kcol <= qrow, s, NEG)
+            if b == 2 * t + 1:
+                s = s + ahead
+            sc[b] = s
+            for piece in range(half // 128):
+                top = jnp.maximum(top, s[:, piece * 128 : (piece + 1) * 128])
+        m = jnp.max(top, axis=1, keepdims=True)
+        acc = jnp.zeros((half, 128), F32)
+        for b in range(2 * t + 2):
+            acc += dot32(jnp.exp(sc[b] - m).astype(BF16), vb[b])
+        out = acc / pltpu.roll(acc, HEAD_DIM, 1)
+        o_ref[t] = jnp.where(
+            lane_h < HEAD_DIM, pltpu.roll(out[:halfrows], HEAD_DIM, 1), out[halfrows:]
+        ).astype(BF16)
+
+
+def out_kernel(pos_ref, own_ref, oth_ref, w0, w1, o_ref, *, other):
+    heads = own_ref.shape[0]
+    halfrows = own_ref.shape[1]
+    half = 2 * halfrows
+    cols = o_ref.shape[1]
+    core, ychip = pos_ref[0], pos_ref[1]
+    group = 2 * ((1 - ychip) if other else ychip) + core
+    lanes = pl.ds(pl.multiple_of(group * cols, cols), cols)
+    lane_h = lane_iota((halfrows, 128))
+    for src, part in ((own_ref, core), (oth_ref, 1 - core)):
+        total = None
+        for first, w in ((core, w0), (1 - core, w1)):
+            tops, bots = [], []
+            for j in range(0, heads // 2, 2):
+                a = src[first * (heads // 2) + j].astype(F32)
+                b = src[first * (heads // 2) + j + 1].astype(F32)
+                tops.append(jnp.where(lane_h < HEAD_DIM, a, pltpu.roll(b, HEAD_DIM, 1)))
+                bots.append(jnp.where(lane_h < HEAD_DIM, pltpu.roll(a, HEAD_DIM, 1), b))
+            feats = jnp.concatenate(
+                [jnp.concatenate(tops, axis=1), jnp.concatenate(bots, axis=1)], axis=0
+            ).astype(BF16)
+            term = dot32(feats, w[:, lanes])
+            total = term if total is None else total + term
+        o_ref[pl.ds(pl.multiple_of(part * half, half), half), :] = total.astype(o_ref.dtype)
+
+
+def vmem_specs(scalars, arrays):
+    return [pl.BlockSpec(memory_space=pltpu.SMEM)] * scalars + [
+        pl.BlockSpec(memory_space=pltpu.VMEM)
+    ] * arrays
+
+
+def on_device(
+    tokens_in, conv_weight, conv_bias, norm_gain, w_query, w_key, w_value, w_out, valid_count
+):
+    tok, cols = tokens_in.shape
+    half = tok // 2
+    ranks = lax.axis_size("tm")
+    head_at = lax.axis_index("head")
+    core, ychip = head_at % 2, head_at // 2
+    pos = jnp.stack([core, ychip]).astype(jnp.int32)
+    bias = conv_bias.reshape(1, cols)
+
+    halo = from_behind(tokens_in[tok - RIM :], "tm", 1)
+    wq1, wk1, wv1, wo1 = swap((w_query, w_key, w_value, w_out), 1)
+    mixed = conv_mix(jnp.zeros((RIM, cols), BF16), tokens_in, conv_weight, bias, tok)
+    gain = jnp.broadcast_to(norm_gain[None, :], (GAIN_ROWS, cols))
+    halves = mixed.reshape(2, half, cols)
+    mine = jnp.concatenate([jnp.where(core == 0, halves[0], halves[1]), gain], axis=0)
+    theirs = jnp.concatenate([jnp.where(core == 0, halves[1], halves[0]), gain], axis=0)
+    beside = swap(theirs, 1)
+    across = swap(jnp.concatenate([mine, beside], axis=1), 2)
+    fix = conv_mix(halo, tokens_in[:RIM], conv_weight, bias, RIM)
+    fix_beside = swap(fix, 1)
+    fix_across = swap(jnp.concatenate([fix, fix_beside], axis=1), 2)
+
+    packed = pl.pallas_call(
+        qkv_kernel,
+        out_shape=jax.ShapeDtypeStruct((ranks, half + half // 2, 2 * HEAD_DIM), BF16),
+        in_specs=vmem_specs(1, 12),
+        out_specs=pl.BlockSpec(memory_space=pltpu.VMEM),
+        compiler_params=pltpu.CompilerParams(vmem_limit_bytes=40 << 20),
+    )(
+        pos, mine, beside, across, fix, fix_beside, fix_across,
+        w_query, w_key, w_value, wq1, wk1, wv1,
+    )
+    own = lax.all_to_all(packed, "tm", 0, 0)
+    oth = swap(own, 1)
+    attended = pl.pallas_call(
+        attend_kernel,
+        out_shape=jax.ShapeDtypeStruct((ranks, half // 2, 2 * HEAD_DIM), BF16),
+        in_specs=vmem_specs(2, 2),
+        out_specs=pl.BlockSpec(memory_space=pltpu.VMEM),
+        scratch_shapes=[
+            pltpu.VMEM((2 * ranks, half, 128), BF16),
+            pltpu.VMEM((2 * ranks, half, 128), BF16),
+            pltpu.VMEM((2 * ranks, half, half), F32),
+        ],
+        compiler_params=pltpu.CompilerParams(vmem_limit_bytes=40 << 20),
+    )(pos, valid_count, own, oth)
+    back = lax.all_to_all(attended, "tm", 0, 0)
+    back_beside = swap(back, 1)
+
+    def project(other, dtype):
+        return pl.pallas_call(
+            functools.partial(out_kernel, other=other),
+            out_shape=jax.ShapeDtypeStruct((tok, cols), dtype),
+            in_specs=vmem_specs(1, 4),
+            out_specs=pl.BlockSpec(memory_space=pltpu.VMEM),
+        )(pos, back, back_beside, w_out, wo1)
+
+    proj_across = swap(project(True, BF16), 2)
+    proj = project(False, F32) + proj_across.astype(F32)
+    whole = jnp.concatenate([fix, mixed[RIM:]], axis=0).astype(F32)
+    return (whole + proj).astype(BF16)
+
+
 def solution(mesh):
+    ranks, heads = mesh.shape["tm"], mesh.shape["head"]
+
+    def body(*args):
+        tokens_in, conv_weight, *_ = args
+        tok, cols = tokens_in.shape
+        fits = heads == 4 and cols == 4 * HEAD_DIM and ranks == 2 * (cols // HEAD_DIM)
+        fits = fits and tok == 512 and ranks * tok <= (WINDOW + 1) * STRETCH
+        return on_device(*args) if fits else ring_on_device(*args)
+
     return jax.shard_map(
-        on_device,
+        body,
         mesh=mesh,
         in_specs=(
             P("tm", "head"),

time: 195 us -> 91.7 us (0.47)
  starting transfers between devices: 69 us -> 12.2 us
  waiting for transfers between devices: 62.3 us -> 24.6 us
  matrix products: 22.4 us -> 0 us
  Pallas kernels: 0 us -> 19.9 us
  blocking collectives: 6.23 us -> 25.7 us
  between operations: 13.6 us -> 0.11 us
  other arithmetic: 15.5 us -> 3.73 us
    ppermute x15 -> x1, starting transfers between devices: 68.9 us -> 3.38 us  [from_behind(): lax.ppermute(value, axis, [(source, source + steps) for source in range(f...]
    all_to_all x0 -> x1, blocking collectives: none -> 25.7 us  [on_device(): own = lax.all_to_all(packed, 'tm', 0, 0)]
    reduce_scatter x1 -> x0, waiting for transfers between devices: 24.9 us -> none  [on_device(): lax.psum_scatter(partial_proj.astype(jnp.bfloat16), 'head', scatter_dimen...]
    dot_general x19 -> x0, matrix products: 22.4 us -> none  [the longest x8 11 us: attend(): jnp.einsum('hqk,khd->hqd', weights.astype(jnp.bfloat16), values3, preferr...]
    pallas_call x0 -> x6, Pallas kernels: none -> 19.9 us  [the longest x1 8.62 us: on_device(): pl.pallas_call(attend_kernel, out_shape=jax.ShapeDtypeStruct((ranks, half...]
    all_gather x1 -> x0, waiting for transfers between devices: 18.2 us -> none  [on_device(): lax.all_gather(normed, 'head', axis=1, tiled=True)]
    ppermute x15 -> x1, waiting for transfers between devices: 19.2 us -> 1.31 us  [from_behind(): lax.ppermute(value, axis, [(source, source + steps) for source in range(f...]
    ppermute x0 -> x11, waiting for transfers between devices: none -> 14.1 us  [swap(): lax.ppermute(value, 'head', [(i, i ^ bit) for i in range(lax.axis_size('h...]
  transfers between devices with their start and end apart: 17 -> 13, of which waited for: 15 -> 8; matrix products, arithmetic and copies ran while one was open for 10% -> 2% of each run, Pallas kernels for 0% -> 5%
where the time goes in v1:
time: 91.7 us; the launch traced here: 91.2 us
  blocking collectives  25.7 us (28%)
  waiting for transfers between devices  24.6 us (27%)
  Pallas kernels  19.9 us (22%)
  starting transfers between devices  12.2 us (13%)
  local copies, waits for them, and re-layouts  4.97 us (5%)
  other arithmetic  3.73 us (4%)
    all_to_all x1, blocking collectives, on_device(): own = lax.all_to_all(packed, 'tm', 0, 0)  25.7 us
    ppermute x11, waiting for transfers between devices, swap(): lax.ppermute(value, 'head', [(i, i ^ bit) for i in range(lax.axis_size('h...  14.1 us
    all_to_all x1, waiting for transfers between devices, on_device(): back = lax.all_to_all(attended, 'tm', 0, 0)  9.18 us
    pallas_call x1, Pallas kernels, on_device(): pl.pallas_call(attend_kernel, out_shape=jax.ShapeDtypeStruct((ranks, half...  8.62 us
    ppermute x11, starting transfers between devices, swap(): lax.ppermute(value, 'head', [(i, i ^ bit) for i in range(lax.axis_size('h...  5.07 us
    pallas_call x2, Pallas kernels, project(): pl.pallas_call(functools.partial(out_kernel, other=other), out_shape=jax....  5.05 us
    pallas_call x2, Pallas kernels, conv_mix(): pl.pallas_call(conv_kernel, out_shape=jax.ShapeDtypeStruct((rows, x.shape...  4.11 us
    all_to_all x1, starting transfers between devices, on_device(): back = lax.all_to_all(attended, 'tm', 0, 0)  3.7 us
  transfers between devices with their start and end apart: 13, of which 8 were waited for; matrix products, arithmetic and copies ran while one was open for 2% of the time, Pallas kernels for 5%

profile of v1, /device:TPU:0, one launch (start us, length us, event | category | flops | bytes accessed | tf_op | source)
XLA Modules:
  0.0 91.2 jit_solution(14810600244600071418)
XLA Ops:
  0.0 1.7 %copy.10.w_ref = bf16[4,192,64]{2,1,0:T(8,128)(2,1)} copy(bf16[4,192,64]{1,2,0:T(8,128)(2,1)} %param.10) | data formatting | bytes 196608 | tf_op args[1]
  1.7 0.6 broadcast_in_dim.4.halo_ref
  2.3 2.3 %shard_map.92 = bf16[512,256]{1,0:T(8,128)(2,1)} custom-call(bf16[8,256]{1,0:T(8,128)(2,1)} %broadcast_in_dim.4.halo_ref, bf16[512,256]{1,0:T(8,128)(2,1)} %x_ref.1, bf16[4,192,64]{2,1,0:T(8,128)(2,1)} %copy.10.w_ref, f32[1,256]{1,0:T(1,128)} %bitcast.3), custom_call_target="tpu_custom_call" | custom-call | tf_op jit(solution)/shard_map/pallas_call | solution.py:164
  4.6 1.1 %broadcast_select_fusion = (bf16[256,256]{1,0:T(8,128)(2,1)S(1)}, bf16[256,256]{1,0:T(8,128)(2,1)S(1)}) fusion(pred[]{:T(512)S(6)} %eq.6, bf16[512,256]{1,0:T(8,128)(2,1)} %shard_map.92), kind=kLoop, calls=%fused_computation.4 | loop fusion | flops 131072 | bytes 524289 | tf_op jit(solution)/shard_map/jit(_where)/select_n | solution.py:317
  5.7 0.0 copy-done.11
  5.8 0.5 collective-permute-start.1
  6.3 0.0 copy-done
  6.3 0.1 collective-permute-start.5
  6.4 0.0 copy-done.1
  6.4 0.4 collective-permute-start.6
  6.8 0.0 copy-done.2
  6.8 0.1 collective-permute-start.7
  6.9 0.4 collective-permute-done.1.b_ref
  7.3 0.7 pad_maximum_fusion
  8.0 2.9 %collective-permute-start.2 = (bf16[264,512]{1,0:T(8,128)(2,1)}, bf16[264,512]{1,0:T(8,128)(2,1)}, u32[]{:S(2)}, u32[]{:S(2)}) collective-permute-start(bf16[264,512]{1,0:T(8,128)(2,1)} %pad_maximum_fusion), channel_id=1, source_target_pairs={{0,2},{1,3},{2,0},{3,1},{4,6},{5,7},{6,4},{7,5},{8,10},{9,11},{10,... | collective-permute-start | bytes 811016 | tf_op jit(solution)/shard_map/ppermute | solution.py:124
  10.9 1.3 %fusion = (bf16[8,256]{1,0:T(8,128)(2,1)}, bf16[8,256]{1,0:T(8,128)(2,1)S(1)}) fusion(bf16[512,256]{1,0:T(8,128)(2,1)} %x_ref.1), kind=kLoop, calls=%fused_computation.8 | loop fusion | bytes 16384 | tf_op jit(solution)/shard_map/slice | solution.py:320
  12.2 3.4 %collective-permute-start = (bf16[8,256]{1,0:T(8,128)(2,1)S(1)}, bf16[8,256]{1,0:T(8,128)(2,1)S(1)}, u32[]{:S(2)}, u32[]{:S(2)}) collective-permute-start(bf16[8,256]{1,0:T(8,128)(2,1)S(1)} %get-tuple-element.6), channel_id=1, source_target_pairs={{0,4},{4,8},{8,12},{12,16},{16,20},{20,24},{24,28},{1,5},{5,9},{9,... | collective-permute-start | bytes 12296 | tf_op jit(solution)/shard_map/ppermute | solution.py:26
  15.6 1.3 %collective-permute-done.halo_ref = bf16[8,256]{1,0:T(8,128)(2,1)S(1)} collective-permute-done((bf16[8,256]{1,0:T(8,128)(2,1)S(1)}, bf16[8,256]{1,0:T(8,128)(2,1)S(1)}, u32[]{:S(2)}, u32[]{:S(2)}) %collective-permute-start) | collective-permute-done | bytes 4128 | tf_op jit(solution)/shard_map/ppermute | solution.py:26
  16.9 0.6 copy-done.10
  17.5 1.8 %shard_map.91.fa_ref = bf16[8,256]{1,0:T(8,128)(2,1)} custom-call(bf16[8,256]{1,0:T(8,128)(2,1)} %copy-done.10, bf16[8,256]{1,0:T(8,128)(2,1)} %get-tuple-element.5.x_ref, bf16[4,192,64]{2,1,0:T(8,128)(2,1)} %copy.10.w_ref, f32[1,256]{1,0:T(1,128)} %bitcast.4), custom_call_target="tpu_custom_call" | custom-call | tf_op jit(solution)/shard_map/pallas_call | solution.py:164
  19.3 0.0 collective-permute-start.3
  19.3 1.4 %collective-permute-done.3.fb_ref = bf16[8,256]{1,0:T(8,128)(2,1)S(1)} collective-permute-done((bf16[8,256]{1,0:T(8,128)(2,1)}, bf16[8,256]{1,0:T(8,128)(2,1)S(1)}, u32[]{:S(2)}, u32[]{:S(2)}) %collective-permute-start.3) | collective-permute-done | bytes 4128 | tf_op jit(solution)/shard_map/ppermute | solution.py:124
  20.6 0.5 collective-permute-start.4
  21.1 0.1 pad_add_fusion.pos_ref
  21.2 3.1 %collective-permute-done.4.fy_ref = bf16[8,512]{1,0:T(8,128)(2,1)S(1)} collective-permute-done((bf16[8,512]{1,0:T(8,128)(2,1)S(1)}, bf16[8,512]{1,0:T(8,128)(2,1)S(1)}, u32[]{:S(2)}, u32[]{:S(2)}) %collective-permute-start.4) | collective-permute-done | bytes 8224 | tf_op jit(solution)/shard_map/ppermute | solution.py:124
  24.3 0.0 collective-permute-done.2.y_ref
  24.3 0.0 collective-permute-done.5.wq1
  24.3 0.0 collective-permute-done.6.wk1
  24.3 0.0 collective-permute-done.7.wv1
  24.3 2.1 %shard_map.93 = bf16[8,384,128]{2,1,0:T(8,128)(2,1)S(1)} custom-call(s32[2]{0:T(128)S(1)} %pad_add_fusion.pos_ref, bf16[264,256]{1,0:T(8,128)(2,1)S(1)} %get-tuple-element.10.a_ref, bf16[264,256]{1,0:T(8,128)(2,1)S(1)} %collective-permute-done.1.b_ref, bf16[264,512]{1,0:T(8,128)(2,1)} %collective-permute-done.2.y_ref, bf16[8,256]{1,0:T(8,128)(2,1)S(1)} %copy-done.3, ...), custom_call_target="tpu_custom_call" | custom-call | tf_op jit(solution)/shard_map/pallas_call | solution.py:324
  26.5 0.0 copy-start.5
  26.5 25.7 %all_to_all.10.own_ref = bf16[8,384,128]{2,1,0:T(8,128)(2,1)S(1)} all-to-all(bf16[8,384,128]{2,1,0:T(8,128)(2,1)S(1)} %shard_map.93), channel_id=1, replica_groups=mesh['tm'=8,'head'=4] {'tm'}, dimensions={0} | all-to-all | bytes 1572864 | tf_op jit(solution)/shard_map/all_to_all | solution.py:334
  52.2 0.0 collective-permute-start.8
  52.2 2.3 %collective-permute-done.8.oth_ref = bf16[8,384,128]{2,1,0:T(8,128)(2,1)S(1)} collective-permute-done((bf16[8,384,128]{2,1,0:T(8,128)(2,1)S(1)}, bf16[8,384,128]{2,1,0:T(8,128)(2,1)S(1)}, u32[]{:S(2)}, u32[]{:S(2)}) %collective-permute-start.8) | collective-permute-done | bytes 786464 | tf_op jit(solution)/shard_map/ppermute | solution.py:124
  54.5 8.6 %shard_map.94 = bf16[8,128,128]{2,1,0:T(8,128)(2,1)} custom-call(s32[2]{0:T(128)S(1)} %pad_add_fusion.pos_ref, s32[4]{0:T(128)S(1)} %copy-done.5, bf16[8,384,128]{2,1,0:T(8,128)(2,1)S(1)} %all_to_all.10.own_ref, bf16[8,384,128]{2,1,0:T(8,128)(2,1)S(1)} %collective-permute-done.8.oth_ref), custom_call_target="tpu_custom_call" | custom-call | tf_op jit(solution)/shard_map/pallas_call | solution.py:336
  63.1 3.7 %all-to-all-start.1 = ((bf16[8,128,128]{2,1,0:T(8,128)(2,1)}), bf16[8,128,128]{2,1,0:T(8,128)(2,1)S(1)}, u32[]{:S(2)}, u32[]{:S(2)}) async-start(bf16[8,128,128]{2,1,0:T(8,128)(2,1)} %shard_map.94), calls=%async_computation.1 | async-start | bytes 524288 | tf_op jit(solution)/shard_map/all_to_all | solution.py:348
  66.8 0.0 copy-done.7
  66.8 0.1 collective-permute-start.10
  66.9 9.2 %all-to-all-done.1.own_ref = bf16[8,128,128]{2,1,0:T(8,128)(2,1)S(1)} async-done(((bf16[8,128,128]{2,1,0:T(8,128)(2,1)}), bf16[8,128,128]{2,1,0:T(8,128)(2,1)S(1)}, u32[]{:S(2)}, u32[]{:S(2)}) %all-to-all-start.1) | async-done | bytes 262176 | tf_op jit(solution)/shard_map/all_to_all | solution.py:348
  76.1 0.0 collective-permute-start.9
  76.1 0.0 collective-permute-done.10.w1
  76.1 1.5 %collective-permute-done.9.oth_ref = bf16[8,128,128]{2,1,0:T(8,128)(2,1)S(1)} collective-permute-done((bf16[8,128,128]{2,1,0:T(8,128)(2,1)S(1)}, bf16[8,128,128]{2,1,0:T(8,128)(2,1)S(1)}, u32[]{:S(2)}, u32[]{:S(2)}) %collective-permute-start.9) | collective-permute-done | bytes 262176 | tf_op jit(solution)/shard_map/ppermute | solution.py:124
  77.6 0.7 copy-done.9
  78.3 2.5 %shard_map.96 = bf16[512,256]{1,0:T(8,128)(2,1)} custom-call(s32[2]{0:T(128)} %copy-done.4, bf16[8,128,128]{2,1,0:T(8,128)(2,1)} %copy-done.6, bf16[8,128,128]{2,1,0:T(8,128)(2,1)} %copy-done.9, bf16[256,1024]{1,0:T(8,128)(2,1)} %w0.3, bf16[256,1024]{1,0:T(8,128)(2,1)} %copy-done.8), custom_call_target="tpu_custom_call" | custom-call | tf_op jit(solution)/shard_map/pallas_call | solution.py:352
  80.8 0.5 collective-permute-start.11
  81.3 2.6 %shard_map.95 = f32[512,256]{1,0:T(8,128)} custom-call(s32[2]{0:T(128)} %copy-done.4, bf16[8,128,128]{2,1,0:T(8,128)(2,1)} %copy-done.6, bf16[8,128,128]{2,1,0:T(8,128)(2,1)} %copy-done.9, bf16[256,1024]{1,0:T(8,128)(2,1)} %w0.3, bf16[256,1024]{1,0:T(8,128)(2,1)} %copy-done.8), custom_call_target="tpu_custom_call" | custom-call | tf_op jit(solution)/shard_map/pallas_call | solution.py:352
  83.9 5.5 %collective-permute-done.11 = bf16[512,256]{1,0:T(8,128)(2,1)S(1)} collective-permute-done((bf16[512,256]{1,0:T(8,128)(2,1)}, bf16[512,256]{1,0:T(8,128)(2,1)S(1)}, u32[]{:S(2)}, u32[]{:S(2)}) %collective-permute-start.11) | collective-permute-done | bytes 262176 | tf_op jit(solution)/shard_map/ppermute | solution.py:124
  89.4 1.8 %add_convert_fusion = bf16[512,256]{1,0:T(8,128)(2,1)} fusion(f32[512,256]{1,0:T(8,128)} %shard_map.95, bf16[512,256]{1,0:T(8,128)(2,1)S(1)} %collective-permute-done.11, bf16[504,256]{1,0:T(8,128)(2,1)S(1)} %slice-done, bf16[8,256]{1,0:T(8,128)(2,1)S(1)} %copy-done.3), kind=kLoop, calls=%fused_computation | loop fusion | flops 1048576 | bytes 1310720 | tf_op jit(solution)/shard_map/convert_element_type | solution.py:362
  (21 shorter events, 0.1 us)
Async XLA Ops:
  2.3 3.4 %copy-start.11 = (bf16[256]{0:T(256)(128)(2,1)S(1)}, bf16[256]{0:T(256)(128)(2,1)}, u32[]{:S(2)}) copy-start(bf16[256]{0:T(256)(128)(2,1)} %param.12) | copy-start | bytes 1540
  2.3 4.5 %copy-start.2 = (bf16[1024,256]{1,0:T(8,128)(2,1)S(1)}, bf16[1024,256]{1,0:T(8,128)(2,1)}, u32[]{:S(2)}) copy-start(bf16[1024,256]{1,0:T(8,128)(2,1)} %wv0.1) | copy-start | bytes 1572868
  4.6 1.7 %copy-start = (bf16[1024,256]{1,0:T(8,128)(2,1)S(1)}, bf16[1024,256]{1,0:T(8,128)(2,1)}, u32[]{:S(2)}) copy-start(bf16[1024,256]{1,0:T(8,128)(2,1)} %wq0.1) | copy-start | bytes 1572868
  4.6 1.7 %copy-start.1 = (bf16[1024,256]{1,0:T(8,128)(2,1)S(1)}, bf16[1024,256]{1,0:T(8,128)(2,1)}, u32[]{:S(2)}) copy-start(bf16[1024,256]{1,0:T(8,128)(2,1)} %wk0.1) | copy-start | bytes 1572868
  5.8 1.5 %collective-permute-start.1 = (bf16[264,256]{1,0:T(8,128)(2,1)S(1)}, bf16[264,256]{1,0:T(8,128)(2,1)S(1)}, u32[]{:S(2)}, u32[]{:S(2)}) collective-permute-start(bf16[264,256]{1,0:T(8,128)(2,1)S(1)} %get-tuple-element.9), channel_id=1, source_target_pairs={{0,1},{1,0},{2,3},{3,2},{4,5},{5,4},{6,7},{7,6},{8,9},{9,8},{10,11... | collective-permute-start | bytes 405512 | tf_op jit(solution)/shard_map/ppermute | solution.py:124
  6.3 18.0 %collective-permute-start.5 = (bf16[1024,256]{1,0:T(8,128)(2,1)S(1)}, bf16[1024,256]{1,0:T(8,128)(2,1)S(1)}, u32[]{:S(2)}, u32[]{:S(2)}) collective-permute-start(bf16[1024,256]{1,0:T(8,128)(2,1)S(1)} %copy-done), channel_id=1, source_target_pairs={{0,1},{1,0},{2,3},{3,2},{4,5},{5,4},{6,7},{7,6},{8,9},{9,8},{10,11... | collective-permute-start | bytes 1572872 | tf_op jit(solution)/shard_map/ppermute | solution.py:124
  6.4 17.9 %collective-permute-start.6 = (bf16[1024,256]{1,0:T(8,128)(2,1)S(1)}, bf16[1024,256]{1,0:T(8,128)(2,1)S(1)}, u32[]{:S(2)}, u32[]{:S(2)}) collective-permute-start(bf16[1024,256]{1,0:T(8,128)(2,1)S(1)} %copy-done.1), channel_id=1, source_target_pairs={{0,1},{1,0},{2,3},{3,2},{4,5},{5,4},{6,7},{7,6},{8,9},{9,8},{10,11... | collective-permute-start | bytes 1572872 | tf_op jit(solution)/shard_map/ppermute | solution.py:124
  6.8 17.5 %collective-permute-start.7 = (bf16[1024,256]{1,0:T(8,128)(2,1)S(1)}, bf16[1024,256]{1,0:T(8,128)(2,1)S(1)}, u32[]{:S(2)}, u32[]{:S(2)}) collective-permute-start(bf16[1024,256]{1,0:T(8,128)(2,1)S(1)} %copy-done.2), channel_id=1, source_target_pairs={{0,1},{1,0},{2,3},{3,2},{4,5},{5,4},{6,7},{7,6},{8,9},{9,8},{10,11... | collective-permute-start | bytes 1572872 | tf_op jit(solution)/shard_map/ppermute | solution.py:124
  8.0 16.3 %collective-permute-start.2 = (bf16[264,512]{1,0:T(8,128)(2,1)}, bf16[264,512]{1,0:T(8,128)(2,1)}, u32[]{:S(2)}, u32[]{:S(2)}) collective-permute-start(bf16[264,512]{1,0:T(8,128)(2,1)} %pad_maximum_fusion), channel_id=1, source_target_pairs={{0,2},{1,3},{2,0},{3,1},{4,6},{5,7},{6,4},{7,5},{8,10},{9,11},{10,... | collective-permute-start | bytes 811016 | tf_op jit(solution)/shard_map/ppermute | solution.py:124
  12.2 4.7 %collective-permute-start = (bf16[8,256]{1,0:T(8,128)(2,1)S(1)}, bf16[8,256]{1,0:T(8,128)(2,1)S(1)}, u32[]{:S(2)}, u32[]{:S(2)}) collective-permute-start(bf16[8,256]{1,0:T(8,128)(2,1)S(1)} %get-tuple-element.6), channel_id=1, source_target_pairs={{0,4},{4,8},{8,12},{12,16},{16,20},{20,24},{24,28},{1,5},{5,9},{9,... | collective-permute-start | bytes 12296 | tf_op jit(solution)/shard_map/ppermute | solution.py:26
  16.9 0.6 copy-start.10
  19.3 1.4 %collective-permute-start.3 = (bf16[8,256]{1,0:T(8,128)(2,1)}, bf16[8,256]{1,0:T(8,128)(2,1)S(1)}, u32[]{:S(2)}, u32[]{:S(2)}) collective-permute-start(bf16[8,256]{1,0:T(8,128)(2,1)} %shard_map.91.fa_ref), channel_id=1, source_target_pairs={{0,1},{1,0},{2,3},{3,2},{4,5},{5,4},{6,7},{7,6},{8,9},{9,8},{10,11... | collective-permute-start | bytes 12296 | tf_op jit(solution)/shard_map/ppermute | solution.py:124
  19.3 1.4 %copy-start.3 = (bf16[8,256]{1,0:T(8,128)(2,1)S(1)}, bf16[8,256]{1,0:T(8,128)(2,1)}, u32[]{:S(2)}) copy-start(bf16[8,256]{1,0:T(8,128)(2,1)} %shard_map.91.fa_ref) | copy-start | bytes 12292
  20.6 3.7 %collective-permute-start.4 = (bf16[8,512]{1,0:T(8,128)(2,1)S(1)}, bf16[8,512]{1,0:T(8,128)(2,1)S(1)}, u32[]{:S(2)}, u32[]{:S(2)}) collective-permute-start(bf16[8,512]{1,0:T(8,128)(2,1)S(1)} %pad_maximum_fusion.3), channel_id=1, source_target_pairs={{0,2},{1,3},{2,0},{3,1},{4,6},{5,7},{6,4},{7,5},{8,10},{9,11},{10,... | collective-permute-start | bytes 24584 | tf_op jit(solution)/shard_map/ppermute | solution.py:124
  21.2 33.3 %copy-start.4 = (s32[2]{0:T(128)}, s32[2]{0:T(128)S(1)}, u32[]{:S(2)}) copy-start(s32[2]{0:T(128)S(1)} %pad_add_fusion.pos_ref) | copy-start | bytes 28
  26.5 28.0 %copy-start.5 = (s32[4]{0:T(128)S(1)}, s32[4]{0:T(128)}, u32[]{:S(2)}) copy-start(s32[4]{0:T(128)} %valid_ref.1) | copy-start | bytes 52
  52.2 2.3 %collective-permute-start.8 = (bf16[8,384,128]{2,1,0:T(8,128)(2,1)S(1)}, bf16[8,384,128]{2,1,0:T(8,128)(2,1)S(1)}, u32[]{:S(2)}, u32[]{:S(2)}) collective-permute-start(bf16[8,384,128]{2,1,0:T(8,128)(2,1)S(1)} %all_to_all.10.own_ref), channel_id=1, source_target_pairs={{0,1},{1,0},{2,3},{3,2},{4,5},{5,4},{6,7},{7,6},{8,9},{9,8},{10,11... | collective-permute-start | bytes 2359304 | tf_op jit(solution)/shard_map/ppermute | solution.py:124
  63.1 3.7 %copy-start.7 = (bf16[256,1024]{1,0:T(8,128)(2,1)S(1)}, bf16[256,1024]{1,0:T(8,128)(2,1)}, u32[]{:S(2)}) copy-start(bf16[256,1024]{1,0:T(8,128)(2,1)} %w0.3) | copy-start | bytes 1572868
  63.1 13.0 %all-to-all-start.1 = ((bf16[8,128,128]{2,1,0:T(8,128)(2,1)}), bf16[8,128,128]{2,1,0:T(8,128)(2,1)S(1)}, u32[]{:S(2)}, u32[]{:S(2)}) async-start(bf16[8,128,128]{2,1,0:T(8,128)(2,1)} %shard_map.94), calls=%async_computation.1 | async-start | bytes 524288 | tf_op jit(solution)/shard_map/all_to_all | solution.py:348
  66.8 9.3 %collective-permute-start.10 = (bf16[256,1024]{1,0:T(8,128)(2,1)S(1)}, bf16[256,1024]{1,0:T(8,128)(2,1)S(1)}, u32[]{:S(2)}, u32[]{:S(2)}) collective-permute-start(bf16[256,1024]{1,0:T(8,128)(2,1)S(1)} %copy-done.7), channel_id=1, source_target_pairs={{0,1},{1,0},{2,3},{3,2},{4,5},{5,4},{6,7},{7,6},{8,9},{9,8},{10,11... | collective-permute-start | bytes 1572872 | tf_op jit(solution)/shard_map/ppermute | solution.py:124
  76.1 1.5 %copy-start.6 = (bf16[8,128,128]{2,1,0:T(8,128)(2,1)}, bf16[8,128,128]{2,1,0:T(8,128)(2,1)S(1)}, u32[]{:S(2)}) copy-start(bf16[8,128,128]{2,1,0:T(8,128)(2,1)S(1)} %all-to-all-done.1.own_ref) | copy-start | bytes 786436
  76.1 1.5 %collective-permute-start.9 = (bf16[8,128,128]{2,1,0:T(8,128)(2,1)S(1)}, bf16[8,128,128]{2,1,0:T(8,128)(2,1)S(1)}, u32[]{:S(2)}, u32[]{:S(2)}) collective-permute-start(bf16[8,128,128]{2,1,0:T(8,128)(2,1)S(1)} %all-to-all-done.1.own_ref), channel_id=1, source_target_pairs={{0,1},{1,0},{2,3},{3,2},{4,5},{5,4},{6,7},{7,6},{8,9},{9,8},{10,11... | collective-permute-start | bytes 786440 | tf_op jit(solution)/shard_map/ppermute | solution.py:124
  76.1 1.5 %copy-start.8 = (bf16[256,1024]{1,0:T(8,128)(2,1)}, bf16[256,1024]{1,0:T(8,128)(2,1)S(1)}, u32[]{:S(2)}) copy-start(bf16[256,1024]{1,0:T(8,128)(2,1)S(1)} %collective-permute-done.10.w1) | copy-start | bytes 1572868
  77.6 0.7 copy-start.9
  80.8 8.6 %collective-permute-start.11 = (bf16[512,256]{1,0:T(8,128)(2,1)}, bf16[512,256]{1,0:T(8,128)(2,1)S(1)}, u32[]{:S(2)}, u32[]{:S(2)}) collective-permute-start(bf16[512,256]{1,0:T(8,128)(2,1)} %shard_map.96), channel_id=1, source_target_pairs={{0,2},{1,3},{2,0},{3,1},{4,6},{5,7},{6,4},{7,5},{8,10},{9,11},{10,... | collective-permute-start | bytes 786440 | tf_op jit(solution)/shard_map/ppermute | solution.py:124
  81.3 8.1 %slice-start = ((bf16[512,256]{1,0:T(8,128)(2,1)}), bf16[504,256]{1,0:T(8,128)(2,1)S(1)}, s32[]{:S(2)}) async-start(bf16[512,256]{1,0:T(8,128)(2,1)} %shard_map.92), calls=%async_computation.2 | async-start | bytes 516096 | tf_op jit(solution)/shard_map/slice | solution.py:361

commit v2 on v0

--- a/solution.py
+++ b/solution.py
@@ -1,6 +1,10 @@
+import functools
+
 import jax
 import jax.numpy as jnp
 from jax import lax
+from jax.experimental import pallas as pl
+from jax.experimental.pallas import tpu as pltpu
 from jax.sharding import PartitionSpec as P
 
 D = 1024
@@ -9,6 +13,11 @@
 DILATION = 4
 STRETCH = 1024
 WINDOW = 8
+RIM = (KERNEL - 1) * DILATION
+GAIN_ROWS = 8
+NEG = -1e30
+F32 = jnp.float32
+BF16 = jnp.bfloat16
 
 
 def from_behind(value, axis, steps):
@@ -17,7 +26,7 @@
     return lax.ppermute(value, axis, [(source, source + steps) for source in range(first, last)])
 
 
-def on_device(
+def ring_on_device(
     tokens_in, conv_weight, conv_bias, norm_gain, w_query, w_key, w_value, w_out, valid_count
 ):
     tok = tokens_in.shape[0]
@@ -111,9 +120,310 @@
     return (mixed32 + proj).astype(jnp.bfloat16)
 
 
+def swap(value, bit):
+    return lax.ppermute(value, "head", [(i, i ^ bit) for i in range(lax.axis_size("head"))])
+
+
+def spread(value, m, part):
+    pairs = []
+    for shard in range(8):
+        for head_at in range(4):
+            b, low, ychip, core = shard // 4, shard % 4, head_at // 2, head_at % 2
+            to = (4 * core + (low ^ m)) * 4 + 2 * ychip + (part ^ b)
+            pairs.append((shard * 4 + head_at, to))
+    return lax.ppermute(value, ("tm", "head"), pairs)
+
+
+def dot32(a, b):
+    return jnp.dot(a, b, preferred_element_type=F32)
+
+
+def dot_nt(a, b):
+    return lax.dot_general(a, b, (((1,), (1,)), ((), ())), preferred_element_type=F32)
+
+
+def lane_iota(shape):
+    return lax.broadcasted_iota(jnp.int32, shape, 1)
+
+
+def gelu_mix(x32, term):
+    return (x32 + jax.nn.gelu(term, approximate=True)).astype(BF16)
+
+
+def conv_kernel(x_ref, w_ref, b_ref, g_ref, late_ref, early_ref, band_ref, base_ref):
+    rows = x_ref.shape[0]
+    half = rows // 2
+    groups, width, _ = w_ref.shape
+    x32 = x_ref[...].astype(F32)
+    ext = jnp.concatenate([jnp.zeros((RIM, x32.shape[1]), F32), x32], axis=0)
+    acc = jnp.zeros(x32.shape, F32) + b_ref[...]
+    for j in range(KERNEL):
+        bands = []
+        for g in range(groups):
+            parts = [w_ref[g, :, j * width : (j + 1) * width].astype(F32)]
+            if g > 0:
+                parts.insert(0, jnp.zeros((width, g * width), F32))
+            if g < groups - 1:
+                parts.append(jnp.zeros((width, (groups - 1 - g) * width), F32))
+            bands.append(jnp.concatenate(parts, axis=1))
+        band = jnp.concatenate(bands, axis=0).astype(BF16)
+        band_ref[j] = band
+        acc += dot_nt(ext[j * DILATION : j * DILATION + rows].astype(BF16), band)
+    base_ref[0:RIM] = acc[0:RIM]
+    base_ref[RIM:] = x32[0:RIM]
+    mix = gelu_mix(x32, acc)
+    gain = jnp.broadcast_to(g_ref[...].astype(F32), (GAIN_ROWS, x32.shape[1])).astype(BF16)
+    late_ref[0:half] = mix[0:half]
+    late_ref[half:] = gain
+    early_ref[0:half] = mix[half:]
+    early_ref[half:] = gain
+
+
+def fix_kernel(halo_ref, base_ref, band_ref, late_ref, o_ref):
+    halo = halo_ref[...].astype(F32)
+    ext = jnp.concatenate([halo, jnp.zeros_like(halo)], axis=0)
+    acc = base_ref[0:RIM]
+    for j in range(KERNEL - 1):
+        acc += dot_nt(ext[j * DILATION : j * DILATION + RIM].astype(BF16), band_ref[j])
+    o_ref[...] = late_ref[...]
+    o_ref[0:RIM] = gelu_mix(base_ref[RIM:], acc)
+
+
+def qkv_kernel(pos_ref, a_ref, b_ref, y_ref, z_ref, wq, wk, wv, *rest):
+    outs, pack = rest[:-1], rest[-1]
+    half = a_ref.shape[0] - GAIN_ROWS
+    cols = a_ref.shape[1]
+    heads = cols // HEAD_DIM
+    core, ychip, low = pos_ref[0], pos_ref[1], pos_ref[2]
+    parts = [
+        (a_ref, 2 * ychip + core),
+        (b_ref, 2 * ychip + 1 - core),
+        (y_ref, 2 * (1 - ychip) + core),
+        (z_ref, 2 * (1 - ychip) + 1 - core),
+    ]
+    square = jnp.zeros((half, cols), F32)
+    for ref, _ in parts:
+        x = ref[0:half].astype(F32)
+        square += x * x
+    rstd = lax.rsqrt(jnp.sum(square, axis=1, keepdims=True) / (4 * cols) + 1e-06)
+    normed = []
+    for ref, group in parts:
+        gain = ref[half : half + 1].astype(F32)
+        normed.append(((ref[0:half].astype(F32) * rstd * gain).astype(BF16), group))
+
+    def project(w):
+        total = None
+        for x, group in normed:
+            term = dot32(x, w[pl.ds(pl.multiple_of(group * cols, cols), cols), :])
+            total = term if total is None else total + term
+        return total.astype(BF16)
+
+    q, k, v = project(wq), project(wk), project(wv)
+    q = (q.astype(F32) * (1.0 / HEAD_DIM**0.5)).astype(BF16)
+    for j in range(heads):
+        lanes = slice(j * HEAD_DIM, (j + 1) * HEAD_DIM)
+        slot = jnp.bitwise_xor(low, j)
+        pack[slot, 0:half, :] = jnp.concatenate([k[:, lanes], v[:, lanes]], axis=1)
+        pack[slot, half : half + half // 2, :] = jnp.concatenate(
+            [q[: half // 2, lanes], q[half // 2 :, lanes]], axis=1
+        )
+    for m, out in enumerate(outs):
+        out[...] = pack[m]
+
+
+def attend_kernel(pos_ref, valid_ref, *rest):
+    own_refs, oth_refs, (o_ref, kb, vb, qs, sc) = rest[:8], rest[8:16], rest[16:]
+    ranks = o_ref.shape[0]
+    half = o_ref.shape[1] * 2
+    halfrows = half // 2
+    core, low = pos_ref[0], pos_ref[2]
+    lane = lane_iota((half, 128))
+    row = lax.broadcasted_iota(jnp.int32, (half, 128), 0)
+    lane_h = lane_iota((halfrows, 128))
+    pad = jnp.where(lane_h == HEAD_DIM, 1.0, 0.0)
+    for i in range(8):
+        part, m = 1 - i // 4, i % 4
+        for side, ref in ((core, own_refs[i]), (1 - core, oth_refs[i])):
+            shard = 4 * jnp.bitwise_xor(side, part) + jnp.bitwise_xor(low, m)
+            block = 2 * shard + part
+            start = block * half
+            stretch = start // STRETCH
+            ok = row + (start - stretch * STRETCH) < valid_ref[stretch]
+            bias = jnp.where(jnp.logical_and(lane == HEAD_DIM, jnp.logical_not(ok)), NEG, 0.0)
+            kv = ref[0:half, :].astype(F32)
+            kb[block] = jnp.where(lane < HEAD_DIM, kv, bias).astype(BF16)
+            vb[block] = jnp.where(lane < HEAD_DIM, 1.0, kv).astype(BF16)
+            if ref is own_refs[i]:
+                packed = ref[half:, :].astype(F32)
+                qs[shard, 0:halfrows] = jnp.where(lane_h < HEAD_DIM, packed, pad).astype(BF16)
+                qs[shard, halfrows:] = jnp.where(
+                    lane_h < HEAD_DIM, pltpu.roll(packed, HEAD_DIM, 1), pad
+                ).astype(BF16)
+    qrow = lax.broadcasted_iota(jnp.int32, (half, half), 0)
+    kcol = lane_iota((half, half))
+    for t in range(ranks):
+        part = jnp.bitwise_xor(core, t // 4)
+        q = qs[t]
+        top = jnp.full((half, 128), NEG, F32)
+        for b in range(2 * t + 2):
+            s = dot_nt(q, kb[b])
+            if b >= 2 * t:
+                s = jnp.where(kcol + (b - 2 * t) * half <= qrow + part * half, s, NEG)
+            sc[b] = s
+            for piece in range(half // 128):
+                top = jnp.maximum(top, s[:, piece * 128 : (piece + 1) * 128])
+        m = jnp.max(top, axis=1, keepdims=True)
+        acc = jnp.zeros((half, 128), F32)
+        for b in range(2 * t + 2):
+            acc += dot32(jnp.exp(sc[b] - m).astype(BF16), vb[b])
+        out = acc / pltpu.roll(acc, HEAD_DIM, 1)
+        o_ref[t] = jnp.where(
+            lane_h < HEAD_DIM, pltpu.roll(out[:halfrows], HEAD_DIM, 1), out[halfrows:]
+        ).astype(BF16)
+
+
+def out_kernel(pos_ref, own_ref, oth_ref, w0, w1, o_ref, *, other):
+    heads = own_ref.shape[0]
+    halfrows = own_ref.shape[1]
+    half = 2 * halfrows
+    cols = o_ref.shape[1]
+    core, ychip = pos_ref[0], pos_ref[1]
+    mine = jnp.bitwise_xor(core, pos_ref[3])
+    group = 2 * ((1 - ychip) if other else ychip) + core
+    lanes = pl.ds(pl.multiple_of(group * cols, cols), cols)
+    lane_h = lane_iota((halfrows, 128))
+    for src, part in ((own_ref, mine), (oth_ref, 1 - mine)):
+        total = None
+        for first, w in ((core, w0), (1 - core, w1)):
+            tops, bots = [], []
+            for j in range(0, heads // 2, 2):
+                a = src[first * (heads // 2) + j].astype(F32)
+                b = src[first * (heads // 2) + j + 1].astype(F32)
+                tops.append(jnp.where(lane_h < HEAD_DIM, a, pltpu.roll(b, HEAD_DIM, 1)))
+                bots.append(jnp.where(lane_h < HEAD_DIM, pltpu.roll(a, HEAD_DIM, 1), b))
+            feats = jnp.concatenate(
+                [jnp.concatenate(tops, axis=1), jnp.concatenate(bots, axis=1)], axis=0
+            ).astype(BF16)
+            term = dot32(feats, w[:, lanes])
+            total = term if total is None else total + term
+        o_ref[pl.ds(pl.multiple_of(part * half, half), half), :] = total.astype(o_ref.dtype)
+
+
+def final_kernel(late_ref, early_ref, proj_ref, across_ref, o_ref):
+    half = o_ref.shape[0] // 2
+    for i, ref in enumerate((late_ref, early_ref)):
+        rows = slice(i * half, (i + 1) * half)
+        proj = proj_ref[rows] + across_ref[rows].astype(F32)
+        o_ref[rows] = (ref[0:half].astype(F32) + proj).astype(BF16)
+
+
+def call(kernel, outs, scalars, args, *, us, vmem=16, scratch=()):
+    spaces = [pltpu.SMEM] * scalars + [pltpu.VMEM] * (len(args) - scalars)
+    outs = [jax.ShapeDtypeStruct(*out) for out in outs]
+    result = pl.pallas_call(
+        kernel,
+        out_shape=outs,
+        in_specs=[pl.BlockSpec(memory_space=space) for space in spaces],
+        out_specs=[pl.BlockSpec(memory_space=pltpu.VMEM)] * len(outs),
+        scratch_shapes=scratch,
+        compiler_params=pltpu.CompilerParams(vmem_limit_bytes=vmem << 20),
+        cost_estimate=pl.CostEstimate(
+            flops=int(us * 1e9), bytes_accessed=int(us * 3.6e6), transcendentals=0
+        ),
+    )(*args)
+    return result if len(outs) > 1 else result[0]
+
+
+def on_device(
+    tokens_in, conv_weight, conv_bias, norm_gain, w_query, w_key, w_value, w_out, valid_count
+):
+    tok, cols = tokens_in.shape
+    half = tok // 2
+    ranks = lax.axis_size("tm")
+    head_at, shard = lax.axis_index("head"), lax.axis_index("tm")
+    pos = jnp.stack([head_at % 2, head_at // 2, shard % 4, shard // 4]).astype(jnp.int32)
+
+    halo = from_behind(tokens_in[tok - RIM :], "tm", 1)
+    late, early, band, base = call(
+        conv_kernel,
+        [
+            ((half + GAIN_ROWS, cols), BF16),
+            ((half + GAIN_ROWS, cols), BF16),
+            ((KERNEL, cols, cols), BF16),
+            ((2 * RIM, cols), F32),
+        ],
+        0,
+        (
+            tokens_in, jnp.swapaxes(conv_weight, 1, 2),
+            conv_bias.reshape(1, cols), norm_gain.reshape(1, cols),
+        ),
+        us=2.0,
+    )
+
+    def project_half(x):
+        beside, across = swap(x, 1), swap(x, 2)
+        corner = swap(across, 1)
+        return call(
+            qkv_kernel,
+            [((half + half // 2, 2 * HEAD_DIM), BF16)] * 4,
+            1,
+            (pos, x, beside, across, corner, w_query, w_key, w_value),
+            us=1.0,
+            scratch=[pltpu.VMEM((4, half + half // 2, 2 * HEAD_DIM), BF16)],
+        )
+
+    sends = list(project_half(early))
+    late = call(
+        fix_kernel, [((half + GAIN_ROWS, cols), BF16)], 0, (halo, base, band, late), us=0.5
+    )
+    sends += list(project_half(late))
+    own = [spread(value, i % 4, 1 - i // 4) for i, value in enumerate(sends)]
+    oth = [swap(value, 1) for value in own]
+    wo1 = swap(lax.optimization_barrier((w_out, sends[0]))[0], 1)
+    attended = call(
+        attend_kernel,
+        [((ranks, half // 2, 2 * HEAD_DIM), BF16)],
+        2,
+        (pos, valid_count, *own, *oth),
+        us=8.0,
+        vmem=24,
+        scratch=[
+            pltpu.VMEM((2 * ranks, half, 128), BF16),
+            pltpu.VMEM((2 * ranks, half, 128), BF16),
+            pltpu.VMEM((ranks, half, 128), BF16),
+            pltpu.VMEM((2 * ranks, half, half), F32),
+        ],
+    )
+    back = lax.all_to_all(attended, "tm", 0, 0)
+    back_beside = swap(back, 1)
+
+    def project(other, dtype):
+        kernel = functools.partial(out_kernel, other=other)
+        args = (pos, back, back_beside, w_out, wo1)
+        return call(kernel, [((tok, cols), dtype)], 1, args, us=1.0)
+
+    proj_across = swap(project(True, BF16), 2)
+    return call(
+        final_kernel,
+        [((tok, cols), BF16)],
+        0,
+        (late, early, project(False, F32), proj_across),
+        us=0.5,
+    )
+
+
 def solution(mesh):
+    ranks, heads = mesh.shape["tm"], mesh.shape["head"]
+
+    def body(*args):
+        tokens_in, conv_weight, *_ = args
+        tok, cols = tokens_in.shape
+        fits = heads == 4 and cols == 4 * HEAD_DIM and ranks == 2 * (cols // HEAD_DIM)
+        fits = fits and tok == 512 and ranks * tok <= (WINDOW + 1) * STRETCH
+        return on_device(*args) if fits else ring_on_device(*args)
+
     return jax.shard_map(
-        on_device,
+        body,
         mesh=mesh,
         in_specs=(
             P("tm", "head"),

time: 195 us -> 76.7 us (0.39)
  starting transfers between devices: 69 us -> 31.7 us
  waiting for transfers between devices: 62.3 us -> 25.8 us
  matrix products: 22.4 us -> 0 us
  other arithmetic: 15.5 us -> 0.08 us
  Pallas kernels: 0 us -> 15.4 us
  between operations: 13.6 us -> 0.16 us
  blocking collectives: 6.23 us -> 0 us
    ppermute x15 -> x1, starting transfers between devices: 68.9 us -> 4.83 us  [from_behind(): lax.ppermute(value, axis, [(source, source + steps) for source in range(f...]
    reduce_scatter x1 -> x0, waiting for transfers between devices: 24.9 us -> none  [on_device(): lax.psum_scatter(partial_proj.astype(jnp.bfloat16), 'head', scatter_dimen...]
    ppermute x0 -> x25, starting transfers between devices: none -> 22.8 us  [the longest x17 12.4 us: swap(): lax.ppermute(value, 'head', [(i, i ^ bit) for i in range(lax.axis_size('h...]
    dot_general x19 -> x0, matrix products: 22.4 us -> none  [the longest x8 11 us: attend(): jnp.einsum('hqk,khd->hqd', weights.astype(jnp.bfloat16), values3, preferr...]
    ppermute x15 -> x1, waiting for transfers between devices: 19.2 us -> 0.01 us  [from_behind(): lax.ppermute(value, axis, [(source, source + steps) for source in range(f...]
    all_gather x1 -> x0, waiting for transfers between devices: 18.2 us -> none  [on_device(): lax.all_gather(normed, 'head', axis=1, tiled=True)]
    ppermute x0 -> x25, waiting for transfers between devices: none -> 16.5 us  [the longest x17 13.8 us: swap(): lax.ppermute(value, 'head', [(i, i ^ bit) for i in range(lax.axis_size('h...]
    pallas_call x0 -> x8, Pallas kernels: none -> 15.4 us  [call(): pl.pallas_call(kernel, out_shape=outs, in_specs=[pl.BlockSpec(memory_spac...]
  transfers between devices with their start and end apart: 17 -> 27, of which waited for: 15 -> 11; matrix products, arithmetic and copies ran while one was open for 10% -> 0% of each run, Pallas kernels for 0% -> 6%
where the time goes in v2:
time: 76.7 us; the launch traced here: 76.4 us
  starting transfers between devices  31.7 us (41%)
  waiting for transfers between devices  25.8 us (34%)
  Pallas kernels  15.4 us (20%)
  local copies, waits for them, and re-layouts  3.26 us (4%)
    pallas_call x8, Pallas kernels, call(): pl.pallas_call(kernel, out_shape=outs, in_specs=[pl.BlockSpec(memory_spac...  15.4 us
    ppermute x17, waiting for transfers between devices, swap(): lax.ppermute(value, 'head', [(i, i ^ bit) for i in range(lax.axis_size('h...  13.8 us
    ppermute x17, starting transfers between devices, swap(): lax.ppermute(value, 'head', [(i, i ^ bit) for i in range(lax.axis_size('h...  12.4 us
    ppermute x8, starting transfers between devices, spread(): return lax.ppermute(value, ('tm', 'head'), pairs)  10.4 us
    all_to_all x1, waiting for transfers between devices, on_device(): back = lax.all_to_all(attended, 'tm', 0, 0)  9.29 us
    ppermute x1, starting transfers between devices, from_behind(): lax.ppermute(value, axis, [(source, source + steps) for source in range(f...  4.83 us
    all_to_all x1, starting transfers between devices, on_device(): back = lax.all_to_all(attended, 'tm', 0, 0)  4.1 us
    ppermute x8, waiting for transfers between devices, spread(): return lax.ppermute(value, ('tm', 'head'), pairs)  2.71 us
  transfers between devices with their start and end apart: 27, of which 11 were waited for; matrix products, arithmetic and copies ran while one was open for 0% of the time, Pallas kernels for 6%

profile of v2, /device:TPU:0, one launch (start us, length us, event | category | flops | bytes accessed | tf_op | source)
XLA Modules:
  0.0 76.4 jit_solution(3813761487468501627)
XLA Ops:
  0.0 0.7 slice.3
  0.7 4.8 %collective-permute-start = (bf16[8,256]{1,0:T(8,128)(2,1)S(1)}, bf16[8,256]{1,0:T(8,128)(2,1)S(1)}, u32[]{:S(2)}, u32[]{:S(2)}) collective-permute-start(bf16[8,256]{1,0:T(8,128)(2,1)S(1)} %slice.3), channel_id=1, source_target_pairs={{0,4},{4,8},{8,12},{12,16},{16,20},{20,24},{24,28},{1,5},{5,9},{9,... | collective-permute-start | bytes 12296 | tf_op jit(solution)/shard_map/ppermute | solution.py:26
  5.6 0.0 copy-start.6
  5.6 0.7 copy-done.6
  6.2 0.9 %copy-done = bf16[512,256]{1,0:T(8,128)(2,1)S(1)} copy-done((bf16[512,256]{1,0:T(8,128)(2,1)S(1)}, bf16[512,256]{1,0:T(8,128)(2,1)}, u32[]{:S(2)}) %copy-start) | copy-done | bytes 262168
  7.2 0.9 %copy-done.5 = bf16[4,192,64]{1,2,0:T(8,128)(2,1)S(1)} copy-done((bf16[4,192,64]{1,2,0:T(8,128)(2,1)S(1)}, bf16[4,192,64]{1,2,0:T(8,128)(2,1)}, u32[]{:S(2)}) %copy-start.5) | copy-done | bytes 98328
  8.1 0.6 shard_map.91
  8.7 1.6 %collective-permute-start.2 = (bf16[264,256]{1,0:T(8,128)(2,1)S(1)}, bf16[264,256]{1,0:T(8,128)(2,1)S(1)}, u32[]{:S(2)}, u32[]{:S(2)}) collective-permute-start(bf16[264,256]{1,0:T(8,128)(2,1)S(1)} %get-tuple-element.21.a_ref.early_ref), channel_id=1, source_target_pairs={{0,2},{1,3},{2,0},{3,1},{4,6},{5,7},{6,4},{7,5},{8,10},{9,11},{10,... | collective-permute-start | bytes 405512 | tf_op jit(solution)/shard_map/ppermute | solution.py:124
  10.3 0.2 shard_map.92.a_ref.late_ref
  10.5 0.6 collective-permute-start.9
  11.0 4.1 %collective-permute-done.2.y_ref = bf16[264,256]{1,0:T(8,128)(2,1)S(1)} collective-permute-done((bf16[264,256]{1,0:T(8,128)(2,1)S(1)}, bf16[264,256]{1,0:T(8,128)(2,1)S(1)}, u32[]{:S(2)}, u32[]{:S(2)}) %collective-permute-start.2) | collective-permute-done | bytes 135200 | tf_op jit(solution)/shard_map/ppermute | solution.py:124
  15.2 0.5 collective-permute-start.8
  15.7 1.0 %collective-permute-done.9.y_ref = bf16[264,256]{1,0:T(8,128)(2,1)S(1)} collective-permute-done((bf16[264,256]{1,0:T(8,128)(2,1)S(1)}, bf16[264,256]{1,0:T(8,128)(2,1)S(1)}, u32[]{:S(2)}, u32[]{:S(2)}) %collective-permute-start.9) | collective-permute-done | bytes 135200 | tf_op jit(solution)/shard_map/ppermute | solution.py:124
  16.7 0.1 pad_add_fusion.pos_ref
  16.8 1.4 %shard_map.93 = (bf16[384,128]{1,0:T(8,128)(2,1)S(1)}, bf16[384,128]{1,0:T(8,128)(2,1)S(1)}, bf16[384,128]{1,0:T(8,128)(2,1)S(1)}, bf16[384,128]{1,0:T(8,128)(2,1)S(1)}) custom-call(s32[4]{0:T(128)S(1)} %pad_add_fusion.pos_ref, bf16[264,256]{1,0:T(8,128)(2,1)S(1)} %get-tuple-element.21.a_ref.early_ref, bf16[264,256]{1,0:T(8,128)(2,1)S(1)} %collective-permute-done.1.b_ref, ...), custom_call_target="tpu_custom_call" | custom-call | flops 1000000000 | bytes 3600000 | tf_op jit(solution)/shard_map/pallas_call | solution.py:323
  18.2 1.7 %collective-permute-start.5 = (bf16[384,128]{1,0:T(8,128)(2,1)S(1)}, bf16[384,128]{1,0:T(8,128)(2,1)S(1)}, u32[]{:S(2)}, u32[]{:S(2)}) collective-permute-start(bf16[384,128]{1,0:T(8,128)(2,1)S(1)} %get-tuple-element.23), channel_id=1, source_target_pairs={{0,5},{1,21},{2,7},{3,23},{4,1},{5,17},{6,3},{7,19},{8,13},{9,29},... | collective-permute-start | bytes 294920 | tf_op jit(solution)/shard_map/ppermute | solution.py:134
  19.9 1.4 %collective-permute-start.6 = (bf16[384,128]{1,0:T(8,128)(2,1)S(1)}, bf16[384,128]{1,0:T(8,128)(2,1)S(1)}, u32[]{:S(2)}, u32[]{:S(2)}) collective-permute-start(bf16[384,128]{1,0:T(8,128)(2,1)S(1)} %get-tuple-element.24), channel_id=1, source_target_pairs={{0,9},{1,25},{2,11},{3,27},{4,13},{5,29},{6,15},{7,31},{8,1},{9,17... | collective-permute-start | bytes 294920 | tf_op jit(solution)/shard_map/ppermute | solution.py:134
  21.3 1.8 %collective-permute-start.7 = (bf16[384,128]{1,0:T(8,128)(2,1)S(1)}, bf16[384,128]{1,0:T(8,128)(2,1)S(1)}, u32[]{:S(2)}, u32[]{:S(2)}) collective-permute-start(bf16[384,128]{1,0:T(8,128)(2,1)S(1)} %get-tuple-element.25), channel_id=1, source_target_pairs={{0,13},{1,29},{2,15},{3,31},{4,9},{5,25},{6,11},{7,27},{8,5},{9,21... | collective-permute-start | bytes 294920 | tf_op jit(solution)/shard_map/ppermute | solution.py:134
  23.1 0.0 collective-permute-done.8.b_ref
  23.1 0.2 collective-permute-start.4
  23.4 1.4 %shard_map.94 = (bf16[384,128]{1,0:T(8,128)(2,1)S(1)}, bf16[384,128]{1,0:T(8,128)(2,1)S(1)}, bf16[384,128]{1,0:T(8,128)(2,1)S(1)}, bf16[384,128]{1,0:T(8,128)(2,1)S(1)}) custom-call(s32[4]{0:T(128)S(1)} %pad_add_fusion.pos_ref, bf16[264,256]{1,0:T(8,128)(2,1)S(1)} %shard_map.92.a_ref.late_ref, bf16[264,256]{1,0:T(8,128)(2,1)S(1)} %collective-permute-done.8.b_ref, ...), custom_call_target="tpu_custom_call" | custom-call | flops 1000000000 | bytes 3600000 | tf_op jit(solution)/shard_map/pallas_call | solution.py:323
  24.7 0.8 %collective-permute-start.11 = (bf16[384,128]{1,0:T(8,128)(2,1)S(1)}, bf16[384,128]{1,0:T(8,128)(2,1)S(1)}, u32[]{:S(2)}, u32[]{:S(2)}) collective-permute-start(bf16[384,128]{1,0:T(8,128)(2,1)S(1)} %get-tuple-element.26), channel_id=1, source_target_pairs={{0,0},{1,16},{2,2},{3,18},{4,4},{5,20},{6,6},{7,22},{8,8},{9,24},{... | collective-permute-start | bytes 294920 | tf_op jit(solution)/shard_map/ppermute | solution.py:134
  25.6 1.6 %collective-permute-start.12 = (bf16[384,128]{1,0:T(8,128)(2,1)S(1)}, bf16[384,128]{1,0:T(8,128)(2,1)S(1)}, u32[]{:S(2)}, u32[]{:S(2)}) collective-permute-start(bf16[384,128]{1,0:T(8,128)(2,1)S(1)} %get-tuple-element.27), channel_id=1, source_target_pairs={{0,4},{1,20},{2,6},{3,22},{4,0},{5,16},{6,2},{7,18},{8,12},{9,28},... | collective-permute-start | bytes 294920 | tf_op jit(solution)/shard_map/ppermute | solution.py:134
  27.2 1.7 %collective-permute-done.6.rest_2_ = bf16[384,128]{1,0:T(8,128)(2,1)S(1)} collective-permute-done((bf16[384,128]{1,0:T(8,128)(2,1)S(1)}, bf16[384,128]{1,0:T(8,128)(2,1)S(1)}, u32[]{:S(2)}, u32[]{:S(2)}) %collective-permute-start.6) | collective-permute-done | bytes 98336 | tf_op jit(solution)/shard_map/ppermute | solution.py:134
  28.9 1.0 %collective-permute-done.7.rest_3_ = bf16[384,128]{1,0:T(8,128)(2,1)S(1)} collective-permute-done((bf16[384,128]{1,0:T(8,128)(2,1)S(1)}, bf16[384,128]{1,0:T(8,128)(2,1)S(1)}, u32[]{:S(2)}, u32[]{:S(2)}) %collective-permute-start.7) | collective-permute-done | bytes 98336 | tf_op jit(solution)/shard_map/ppermute | solution.py:134
  29.9 2.7 %collective-permute-start.14 = (bf16[384,128]{1,0:T(8,128)(2,1)S(1)}, bf16[384,128]{1,0:T(8,128)(2,1)S(1)}, u32[]{:S(2)}, u32[]{:S(2)}) collective-permute-start(bf16[384,128]{1,0:T(8,128)(2,1)S(1)} %get-tuple-element.29), channel_id=1, source_target_pairs={{0,12},{1,28},{2,14},{3,30},{4,8},{5,24},{6,10},{7,26},{8,4},{9,20... | collective-permute-start | bytes 294920 | tf_op jit(solution)/shard_map/ppermute | solution.py:134
  32.6 2.1 %collective-permute-start.16 = (bf16[384,128]{1,0:T(8,128)(2,1)S(1)}, bf16[384,128]{1,0:T(8,128)(2,1)S(1)}, u32[]{:S(2)}, u32[]{:S(2)}) collective-permute-start(bf16[384,128]{1,0:T(8,128)(2,1)S(1)} %collective-permute-done.5.rest_1_), channel_id=1, source_target_pairs={{0,1},{1,0},{2,3},{3,2},{4,5},{5,4},{6,7},{7,6},{8,9},{9,8},{10,11... | collective-permute-start | bytes 294920 | tf_op jit(solution)/shard_map/ppermute | solution.py:124
  34.7 0.1 collective-permute-start.17
  34.8 0.8 %collective-permute-start.18 = (bf16[384,128]{1,0:T(8,128)(2,1)S(1)}, bf16[384,128]{1,0:T(8,128)(2,1)S(1)}, u32[]{:S(2)}, u32[]{:S(2)}) collective-permute-start(bf16[384,128]{1,0:T(8,128)(2,1)S(1)} %collective-permute-done.7.rest_3_), channel_id=1, source_target_pairs={{0,1},{1,0},{2,3},{3,2},{4,5},{5,4},{6,7},{7,6},{8,9},{9,8},{10,11... | collective-permute-start | bytes 294920 | tf_op jit(solution)/shard_map/ppermute | solution.py:124
  35.6 1.6 %collective-permute-start.15 = (bf16[384,128]{1,0:T(8,128)(2,1)S(1)}, bf16[384,128]{1,0:T(8,128)(2,1)S(1)}, u32[]{:S(2)}, u32[]{:S(2)}) collective-permute-start(bf16[384,128]{1,0:T(8,128)(2,1)S(1)} %collective-permute-done.4.rest_0_), channel_id=1, source_target_pairs={{0,1},{1,0},{2,3},{3,2},{4,5},{5,4},{6,7},{7,6},{8,9},{9,8},{10,11... | collective-permute-start | bytes 294920 | tf_op jit(solution)/shard_map/ppermute | solution.py:124
  37.2 2.9 %collective-permute-start.19 = (bf16[384,128]{1,0:T(8,128)(2,1)S(1)}, bf16[384,128]{1,0:T(8,128)(2,1)S(1)}, u32[]{:S(2)}, u32[]{:S(2)}) collective-permute-start(bf16[384,128]{1,0:T(8,128)(2,1)S(1)} %collective-permute-done.11.rest_4_), channel_id=1, source_target_pairs={{0,1},{1,0},{2,3},{3,2},{4,5},{5,4},{6,7},{7,6},{8,9},{9,8},{10,11... | collective-permute-start | bytes 294920 | tf_op jit(solution)/shard_map/ppermute | solution.py:124
  40.1 0.0 collective-permute-start.20
  40.1 0.5 collective-permute-start.21
  40.6 0.1 collective-permute-start.22
  40.7 0.3 collective-permute-done.19.rest_12_
  41.0 0.4 collective-permute-done.20.rest_13_
  41.4 0.2 collective-permute-done.21.rest_14_
  41.6 0.4 collective-permute-done.22.rest_15_
  41.9 9.3 %shard_map.95 = bf16[8,128,128]{2,1,0:T(8,128)(2,1)} custom-call(s32[4]{0:T(128)S(1)} %pad_add_fusion.pos_ref, s32[4]{0:T(128)S(1)} %copy-done.7, bf16[384,128]{1,0:T(8,128)(2,1)S(1)} %collective-permute-done.4.rest_0_, bf16[384,128]{1,0:T(8,128)(2,1)S(1)} %collective-permute-done.5.rest_1_, bf16[384,128]{1,0:T(8,128)(2,1)S(1)} %collective-permute-done.6.rest_2_, ...), custom_call_target="tpu_custom_call" | custom-call | flops 8000000000 | bytes 28800000 | tf_op jit(solution)/shard_map/pallas_call | solution.py:323
  51.2 4.1 %all-to-all-start = ((bf16[8,128,128]{2,1,0:T(8,128)(2,1)}), bf16[8,128,128]{2,1,0:T(8,128)(2,1)S(1)}, u32[]{:S(2)}, u32[]{:S(2)}) async-start(bf16[8,128,128]{2,1,0:T(8,128)(2,1)} %shard_map.95), calls=%async_computation | async-start | bytes 524288 | tf_op jit(solution)/shard_map/all_to_all | solution.py:397
  55.3 0.1 collective-permute-start.24
  55.4 9.3 %all-to-all-done.own_ref = bf16[8,128,128]{2,1,0:T(8,128)(2,1)S(1)} async-done(((bf16[8,128,128]{2,1,0:T(8,128)(2,1)}), bf16[8,128,128]{2,1,0:T(8,128)(2,1)S(1)}, u32[]{:S(2)}, u32[]{:S(2)}) %all-to-all-start) | async-done | bytes 262176 | tf_op jit(solution)/shard_map/all_to_all | solution.py:397
  64.7 1.5 %collective-permute-done.23.oth_ref = bf16[8,128,128]{2,1,0:T(8,128)(2,1)S(1)} collective-permute-done((bf16[8,128,128]{2,1,0:T(8,128)(2,1)S(1)}, bf16[8,128,128]{2,1,0:T(8,128)(2,1)S(1)}, u32[]{:S(2)}, u32[]{:S(2)}) %collective-permute-start.23) | collective-permute-done | bytes 262176 | tf_op jit(solution)/shard_map/ppermute | solution.py:124
  66.3 0.9 %shard_map.97 = bf16[512,256]{1,0:T(8,128)(2,1)S(1)} custom-call(s32[4]{0:T(128)S(1)} %pad_add_fusion.pos_ref, bf16[8,128,128]{2,1,0:T(8,128)(2,1)S(1)} %all-to-all-done.own_ref, bf16[8,128,128]{2,1,0:T(8,128)(2,1)S(1)} %collective-permute-done.23.oth_ref, bf16[256,1024]{1,0:T(8,128)(2,1)S(1)} %copy-done.4, bf16[256,1024]{1,0:T(8,128)(2,1)S(1)} %collective-permute-done.24.w1), custom_call_target="tpu_custom_call" | custom-call | flops 1000000000 | bytes 3600000 | tf_op jit(solution)/shard_map/pallas_call | solution.py:323
  67.2 1.6 %collective-permute-start.25 = (bf16[512,256]{1,0:T(8,128)(2,1)S(1)}, bf16[512,256]{1,0:T(8,128)(2,1)S(1)}, u32[]{:S(2)}, u32[]{:S(2)}) collective-permute-start(bf16[512,256]{1,0:T(8,128)(2,1)S(1)} %shard_map.97), channel_id=1, source_target_pairs={{0,2},{1,3},{2,0},{3,1},{4,6},{5,7},{6,4},{7,5},{8,10},{9,11},{10,... | collective-permute-start | bytes 786440 | tf_op jit(solution)/shard_map/ppermute | solution.py:124
  68.8 0.9 %shard_map.96.proj_ref = f32[512,256]{1,0:T(8,128)S(1)} custom-call(s32[4]{0:T(128)S(1)} %pad_add_fusion.pos_ref, bf16[8,128,128]{2,1,0:T(8,128)(2,1)S(1)} %all-to-all-done.own_ref, bf16[8,128,128]{2,1,0:T(8,128)(2,1)S(1)} %collective-permute-done.23.oth_ref, bf16[256,1024]{1,0:T(8,128)(2,1)S(1)} %copy-done.4, bf16[256,1024]{1,0:T(8,128)(2,1)S(1)} %collective-permute-done.24.w1), custom_call_target="tpu_custom_call" | custom-call | flops 1000000000 | bytes 3600000 | tf_op jit(solution)/shard_map/pallas_call | solution.py:323
  69.7 5.9 %collective-permute-done.25.across_ref = bf16[512,256]{1,0:T(8,128)(2,1)S(1)} collective-permute-done((bf16[512,256]{1,0:T(8,128)(2,1)S(1)}, bf16[512,256]{1,0:T(8,128)(2,1)S(1)}, u32[]{:S(2)}, u32[]{:S(2)}) %collective-permute-start.25) | collective-permute-done | bytes 262176 | tf_op jit(solution)/shard_map/ppermute | solution.py:124
  75.6 0.8 %shard_map.98 = bf16[512,256]{1,0:T(8,128)(2,1)} custom-call(bf16[264,256]{1,0:T(8,128)(2,1)S(1)} %shard_map.92.a_ref.late_ref, bf16[264,256]{1,0:T(8,128)(2,1)S(1)} %get-tuple-element.21.a_ref.early_ref, f32[512,256]{1,0:T(8,128)S(1)} %shard_map.96.proj_ref, bf16[512,256]{1,0:T(8,128)(2,1)S(1)} %collective-permute-done.25.across_ref), custom_call_target="tpu_custom_call" | custom-call | flops 500000000 | bytes 1800000 | tf_op jit(solution)/shard_map/pallas_call | solution.py:323
  (35 shorter events, 0.1 us)
Async XLA Ops:
  0.0 5.5 %copy-start.8 = (bf16[256]{0:T(256)(128)(2,1)S(1)}, bf16[256]{0:T(256)(128)(2,1)}, u32[]{:S(2)}) copy-start(bf16[256]{0:T(256)(128)(2,1)} %param.12) | copy-start | bytes 1540
  0.7 9.6 %collective-permute-start = (bf16[8,256]{1,0:T(8,128)(2,1)S(1)}, bf16[8,256]{1,0:T(8,128)(2,1)S(1)}, u32[]{:S(2)}, u32[]{:S(2)}) collective-permute-start(bf16[8,256]{1,0:T(8,128)(2,1)S(1)} %slice.3), channel_id=1, source_target_pairs={{0,4},{4,8},{8,12},{12,16},{16,20},{20,24},{24,28},{1,5},{5,9},{9,... | collective-permute-start | bytes 12296 | tf_op jit(solution)/shard_map/ppermute | solution.py:26
  5.6 0.7 copy-start.6
  6.2 0.9 %copy-start = (bf16[512,256]{1,0:T(8,128)(2,1)S(1)}, bf16[512,256]{1,0:T(8,128)(2,1)}, u32[]{:S(2)}) copy-start(bf16[512,256]{1,0:T(8,128)(2,1)} %x_ref.1) | copy-start | bytes 786436
  7.2 0.9 %copy-start.5 = (bf16[4,192,64]{1,2,0:T(8,128)(2,1)S(1)}, bf16[4,192,64]{1,2,0:T(8,128)(2,1)}, u32[]{:S(2)}) copy-start(bf16[4,192,64]{1,2,0:T(8,128)(2,1)} %param.10) | copy-start | bytes 294916
  8.7 6.5 %collective-permute-start.2 = (bf16[264,256]{1,0:T(8,128)(2,1)S(1)}, bf16[264,256]{1,0:T(8,128)(2,1)S(1)}, u32[]{:S(2)}, u32[]{:S(2)}) collective-permute-start(bf16[264,256]{1,0:T(8,128)(2,1)S(1)} %get-tuple-element.21.a_ref.early_ref), channel_id=1, source_target_pairs={{0,2},{1,3},{2,0},{3,1},{4,6},{5,7},{6,4},{7,5},{8,10},{9,11},{10,... | collective-permute-start | bytes 405512 | tf_op jit(solution)/shard_map/ppermute | solution.py:124
  10.3 6.5 %copy-start.1 = (bf16[1024,256]{1,0:T(8,128)(2,1)S(1)}, bf16[1024,256]{1,0:T(8,128)(2,1)}, u32[]{:S(2)}) copy-start(bf16[1024,256]{1,0:T(8,128)(2,1)} %wq.3) | copy-start | bytes 1572868
  10.3 6.5 %copy-start.2 = (bf16[1024,256]{1,0:T(8,128)(2,1)S(1)}, bf16[1024,256]{1,0:T(8,128)(2,1)}, u32[]{:S(2)}) copy-start(bf16[1024,256]{1,0:T(8,128)(2,1)} %wk.3) | copy-start | bytes 1572868
  10.3 6.5 %copy-start.3 = (bf16[1024,256]{1,0:T(8,128)(2,1)S(1)}, bf16[1024,256]{1,0:T(8,128)(2,1)}, u32[]{:S(2)}) copy-start(bf16[1024,256]{1,0:T(8,128)(2,1)} %wv.3) | copy-start | bytes 1572868
  10.5 6.2 %collective-permute-start.9 = (bf16[264,256]{1,0:T(8,128)(2,1)S(1)}, bf16[264,256]{1,0:T(8,128)(2,1)S(1)}, u32[]{:S(2)}, u32[]{:S(2)}) collective-permute-start(bf16[264,256]{1,0:T(8,128)(2,1)S(1)} %shard_map.92.a_ref.late_ref), channel_id=1, source_target_pairs={{0,2},{1,3},{2,0},{3,1},{4,6},{5,7},{6,4},{7,5},{8,10},{9,11},{10,... | collective-permute-start | bytes 405512 | tf_op jit(solution)/shard_map/ppermute | solution.py:124
  11.0 5.7 %collective-permute-start.1 = (bf16[264,256]{1,0:T(8,128)(2,1)S(1)}, bf16[264,256]{1,0:T(8,128)(2,1)S(1)}, u32[]{:S(2)}, u32[]{:S(2)}) collective-permute-start(bf16[264,256]{1,0:T(8,128)(2,1)S(1)} %get-tuple-element.21.a_ref.early_ref), channel_id=1, source_target_pairs={{0,1},{1,0},{2,3},{3,2},{4,5},{5,4},{6,7},{7,6},{8,9},{9,8},{10,11... | collective-permute-start | bytes 405512 | tf_op jit(solution)/shard_map/ppermute | solution.py:124
  15.2 1.6 %collective-permute-start.3 = (bf16[264,256]{1,0:T(8,128)(2,1)S(1)}, bf16[264,256]{1,0:T(8,128)(2,1)S(1)}, u32[]{:S(2)}, u32[]{:S(2)}) collective-permute-start(bf16[264,256]{1,0:T(8,128)(2,1)S(1)} %collective-permute-done.2.y_ref), channel_id=1, source_target_pairs={{0,1},{1,0},{2,3},{3,2},{4,5},{5,4},{6,7},{7,6},{8,9},{9,8},{10,11... | collective-permute-start | bytes 405512 | tf_op jit(solution)/shard_map/ppermute | solution.py:124
  15.2 8.0 %collective-permute-start.8 = (bf16[264,256]{1,0:T(8,128)(2,1)S(1)}, bf16[264,256]{1,0:T(8,128)(2,1)S(1)}, u32[]{:S(2)}, u32[]{:S(2)}) collective-permute-start(bf16[264,256]{1,0:T(8,128)(2,1)S(1)} %shard_map.92.a_ref.late_ref), channel_id=1, source_target_pairs={{0,1},{1,0},{2,3},{3,2},{4,5},{5,4},{6,7},{7,6},{8,9},{9,8},{10,11... | collective-permute-start | bytes 405512 | tf_op jit(solution)/shard_map/ppermute | solution.py:124
  16.7 6.7 %collective-permute-start.10 = (bf16[264,256]{1,0:T(8,128)(2,1)S(1)}, bf16[264,256]{1,0:T(8,128)(2,1)S(1)}, u32[]{:S(2)}, u32[]{:S(2)}) collective-permute-start(bf16[264,256]{1,0:T(8,128)(2,1)S(1)} %collective-permute-done.9.y_ref), channel_id=1, source_target_pairs={{0,1},{1,0},{2,3},{3,2},{4,5},{5,4},{6,7},{7,6},{8,9},{9,8},{10,11... | collective-permute-start | bytes 405512 | tf_op jit(solution)/shard_map/ppermute | solution.py:124
  18.2 7.4 %collective-permute-start.5 = (bf16[384,128]{1,0:T(8,128)(2,1)S(1)}, bf16[384,128]{1,0:T(8,128)(2,1)S(1)}, u32[]{:S(2)}, u32[]{:S(2)}) collective-permute-start(bf16[384,128]{1,0:T(8,128)(2,1)S(1)} %get-tuple-element.23), channel_id=1, source_target_pairs={{0,5},{1,21},{2,7},{3,23},{4,1},{5,17},{6,3},{7,19},{8,13},{9,29},... | collective-permute-start | bytes 294920 | tf_op jit(solution)/shard_map/ppermute | solution.py:134
  19.9 9.0 %collective-permute-start.6 = (bf16[384,128]{1,0:T(8,128)(2,1)S(1)}, bf16[384,128]{1,0:T(8,128)(2,1)S(1)}, u32[]{:S(2)}, u32[]{:S(2)}) collective-permute-start(bf16[384,128]{1,0:T(8,128)(2,1)S(1)} %get-tuple-element.24), channel_id=1, source_target_pairs={{0,9},{1,25},{2,11},{3,27},{4,13},{5,29},{6,15},{7,31},{8,1},{9,17... | collective-permute-start | bytes 294920 | tf_op jit(solution)/shard_map/ppermute | solution.py:134
  21.3 8.6 %collective-permute-start.7 = (bf16[384,128]{1,0:T(8,128)(2,1)S(1)}, bf16[384,128]{1,0:T(8,128)(2,1)S(1)}, u32[]{:S(2)}, u32[]{:S(2)}) collective-permute-start(bf16[384,128]{1,0:T(8,128)(2,1)S(1)} %get-tuple-element.25), channel_id=1, source_target_pairs={{0,13},{1,29},{2,15},{3,31},{4,9},{5,25},{6,11},{7,27},{8,5},{9,21... | collective-permute-start | bytes 294920 | tf_op jit(solution)/shard_map/ppermute | solution.py:134
  23.1 9.5 %collective-permute-start.4 = (bf16[384,128]{1,0:T(8,128)(2,1)S(1)}, bf16[384,128]{1,0:T(8,128)(2,1)S(1)}, u32[]{:S(2)}, u32[]{:S(2)}) collective-permute-start(bf16[384,128]{1,0:T(8,128)(2,1)S(1)} %get-tuple-element.22), channel_id=1, source_target_pairs={{0,1},{1,17},{2,3},{3,19},{4,5},{5,21},{6,7},{7,23},{8,9},{9,25},{... | collective-permute-start | bytes 294920 | tf_op jit(solution)/shard_map/ppermute | solution.py:134
  24.7 9.9 %collective-permute-start.11 = (bf16[384,128]{1,0:T(8,128)(2,1)S(1)}, bf16[384,128]{1,0:T(8,128)(2,1)S(1)}, u32[]{:S(2)}, u32[]{:S(2)}) collective-permute-start(bf16[384,128]{1,0:T(8,128)(2,1)S(1)} %get-tuple-element.26), channel_id=1, source_target_pairs={{0,0},{1,16},{2,2},{3,18},{4,4},{5,20},{6,6},{7,22},{8,8},{9,24},{... | collective-permute-start | bytes 294920 | tf_op jit(solution)/shard_map/ppermute | solution.py:134
  25.6 9.2 %collective-permute-start.12 = (bf16[384,128]{1,0:T(8,128)(2,1)S(1)}, bf16[384,128]{1,0:T(8,128)(2,1)S(1)}, u32[]{:S(2)}, u32[]{:S(2)}) collective-permute-start(bf16[384,128]{1,0:T(8,128)(2,1)S(1)} %get-tuple-element.27), channel_id=1, source_target_pairs={{0,4},{1,20},{2,6},{3,22},{4,0},{5,16},{6,2},{7,18},{8,12},{9,28},... | collective-permute-start | bytes 294920 | tf_op jit(solution)/shard_map/ppermute | solution.py:134
  28.9 13.0 %copy-start.7 = (s32[4]{0:T(128)S(1)}, s32[4]{0:T(128)}, u32[]{:S(2)}) copy-start(s32[4]{0:T(128)} %valid_ref.1) | copy-start | bytes 52
  28.9 6.7 %collective-permute-start.13 = (bf16[384,128]{1,0:T(8,128)(2,1)S(1)}, bf16[384,128]{1,0:T(8,128)(2,1)S(1)}, u32[]{:S(2)}, u32[]{:S(2)}) collective-permute-start(bf16[384,128]{1,0:T(8,128)(2,1)S(1)} %get-tuple-element.28), channel_id=1, source_target_pairs={{0,8},{1,24},{2,10},{3,26},{4,12},{5,28},{6,14},{7,30},{8,0},{9,16... | collective-permute-start | bytes 294920 | tf_op jit(solution)/shard_map/ppermute | solution.py:134
  29.9 7.3 %collective-permute-start.14 = (bf16[384,128]{1,0:T(8,128)(2,1)S(1)}, bf16[384,128]{1,0:T(8,128)(2,1)S(1)}, u32[]{:S(2)}, u32[]{:S(2)}) collective-permute-start(bf16[384,128]{1,0:T(8,128)(2,1)S(1)} %get-tuple-element.29), channel_id=1, source_target_pairs={{0,12},{1,28},{2,14},{3,30},{4,8},{5,24},{6,10},{7,26},{8,4},{9,20... | collective-permute-start | bytes 294920 | tf_op jit(solution)/shard_map/ppermute | solution.py:134
  32.6 7.5 %collective-permute-start.16 = (bf16[384,128]{1,0:T(8,128)(2,1)S(1)}, bf16[384,128]{1,0:T(8,128)(2,1)S(1)}, u32[]{:S(2)}, u32[]{:S(2)}) collective-permute-start(bf16[384,128]{1,0:T(8,128)(2,1)S(1)} %collective-permute-done.5.rest_1_), channel_id=1, source_target_pairs={{0,1},{1,0},{2,3},{3,2},{4,5},{5,4},{6,7},{7,6},{8,9},{9,8},{10,11... | collective-permute-start | bytes 294920 | tf_op jit(solution)/shard_map/ppermute | solution.py:124
  34.7 5.4 %collective-permute-start.17 = (bf16[384,128]{1,0:T(8,128)(2,1)S(1)}, bf16[384,128]{1,0:T(8,128)(2,1)S(1)}, u32[]{:S(2)}, u32[]{:S(2)}) collective-permute-start(bf16[384,128]{1,0:T(8,128)(2,1)S(1)} %collective-permute-done.6.rest_2_), channel_id=1, source_target_pairs={{0,1},{1,0},{2,3},{3,2},{4,5},{5,4},{6,7},{7,6},{8,9},{9,8},{10,11... | collective-permute-start | bytes 294920 | tf_op jit(solution)/shard_map/ppermute | solution.py:124
  34.8 5.9 %collective-permute-start.18 = (bf16[384,128]{1,0:T(8,128)(2,1)S(1)}, bf16[384,128]{1,0:T(8,128)(2,1)S(1)}, u32[]{:S(2)}, u32[]{:S(2)}) collective-permute-start(bf16[384,128]{1,0:T(8,128)(2,1)S(1)} %collective-permute-done.7.rest_3_), channel_id=1, source_target_pairs={{0,1},{1,0},{2,3},{3,2},{4,5},{5,4},{6,7},{7,6},{8,9},{9,8},{10,11... | collective-permute-start | bytes 294920 | tf_op jit(solution)/shard_map/ppermute | solution.py:124
  35.6 5.1 %collective-permute-start.15 = (bf16[384,128]{1,0:T(8,128)(2,1)S(1)}, bf16[384,128]{1,0:T(8,128)(2,1)S(1)}, u32[]{:S(2)}, u32[]{:S(2)}) collective-permute-start(bf16[384,128]{1,0:T(8,128)(2,1)S(1)} %collective-permute-done.4.rest_0_), channel_id=1, source_target_pairs={{0,1},{1,0},{2,3},{3,2},{4,5},{5,4},{6,7},{7,6},{8,9},{9,8},{10,11... | collective-permute-start | bytes 294920 | tf_op jit(solution)/shard_map/ppermute | solution.py:124
  37.2 3.9 %collective-permute-start.19 = (bf16[384,128]{1,0:T(8,128)(2,1)S(1)}, bf16[384,128]{1,0:T(8,128)(2,1)S(1)}, u32[]{:S(2)}, u32[]{:S(2)}) collective-permute-start(bf16[384,128]{1,0:T(8,128)(2,1)S(1)} %collective-permute-done.11.rest_4_), channel_id=1, source_target_pairs={{0,1},{1,0},{2,3},{3,2},{4,5},{5,4},{6,7},{7,6},{8,9},{9,8},{10,11... | collective-permute-start | bytes 294920 | tf_op jit(solution)/shard_map/ppermute | solution.py:124
  40.1 1.3 %collective-permute-start.20 = (bf16[384,128]{1,0:T(8,128)(2,1)S(1)}, bf16[384,128]{1,0:T(8,128)(2,1)S(1)}, u32[]{:S(2)}, u32[]{:S(2)}) collective-permute-start(bf16[384,128]{1,0:T(8,128)(2,1)S(1)} %collective-permute-done.12.rest_5_), channel_id=1, source_target_pairs={{0,1},{1,0},{2,3},{3,2},{4,5},{5,4},{6,7},{7,6},{8,9},{9,8},{10,11... | collective-permute-start | bytes 294920 | tf_op jit(solution)/shard_map/ppermute | solution.py:124
  40.1 1.5 %collective-permute-start.21 = (bf16[384,128]{1,0:T(8,128)(2,1)S(1)}, bf16[384,128]{1,0:T(8,128)(2,1)S(1)}, u32[]{:S(2)}, u32[]{:S(2)}) collective-permute-start(bf16[384,128]{1,0:T(8,128)(2,1)S(1)} %collective-permute-done.13.rest_6_), channel_id=1, source_target_pairs={{0,1},{1,0},{2,3},{3,2},{4,5},{5,4},{6,7},{7,6},{8,9},{9,8},{10,11... | collective-permute-start | bytes 294920 | tf_op jit(solution)/shard_map/ppermute | solution.py:124
  40.6 1.3 %collective-permute-start.22 = (bf16[384,128]{1,0:T(8,128)(2,1)S(1)}, bf16[384,128]{1,0:T(8,128)(2,1)S(1)}, u32[]{:S(2)}, u32[]{:S(2)}) collective-permute-start(bf16[384,128]{1,0:T(8,128)(2,1)S(1)} %collective-permute-done.14.rest_7_), channel_id=1, source_target_pairs={{0,1},{1,0},{2,3},{3,2},{4,5},{5,4},{6,7},{7,6},{8,9},{9,8},{10,11... | collective-permute-start | bytes 294920 | tf_op jit(solution)/shard_map/ppermute | solution.py:124
  51.2 4.1 %copy-start.4 = (bf16[256,1024]{1,0:T(8,128)(2,1)S(1)}, bf16[256,1024]{1,0:T(8,128)(2,1)}, u32[]{:S(2)}) copy-start(bf16[256,1024]{1,0:T(8,128)(2,1)} %w0.3) | copy-start | bytes 1572868
  51.2 13.5 %all-to-all-start = ((bf16[8,128,128]{2,1,0:T(8,128)(2,1)}), bf16[8,128,128]{2,1,0:T(8,128)(2,1)S(1)}, u32[]{:S(2)}, u32[]{:S(2)}) async-start(bf16[8,128,128]{2,1,0:T(8,128)(2,1)} %shard_map.95), calls=%async_computation | async-start | bytes 524288 | tf_op jit(solution)/shard_map/all_to_all | solution.py:397
  55.3 9.4 %collective-permute-start.24 = (bf16[256,1024]{1,0:T(8,128)(2,1)S(1)}, bf16[256,1024]{1,0:T(8,128)(2,1)S(1)}, u32[]{:S(2)}, u32[]{:S(2)}) collective-permute-start(bf16[256,1024]{1,0:T(8,128)(2,1)S(1)} %copy-done.4), channel_id=1, source_target_pairs={{0,1},{1,0},{2,3},{3,2},{4,5},{5,4},{6,7},{7,6},{8,9},{9,8},{10,11... | collective-permute-start | bytes 1572872 | tf_op jit(solution)/shard_map/ppermute | solution.py:124
  64.7 1.5 %collective-permute-start.23 = (bf16[8,128,128]{2,1,0:T(8,128)(2,1)S(1)}, bf16[8,128,128]{2,1,0:T(8,128)(2,1)S(1)}, u32[]{:S(2)}, u32[]{:S(2)}) collective-permute-start(bf16[8,128,128]{2,1,0:T(8,128)(2,1)S(1)} %all-to-all-done.own_ref), channel_id=1, source_target_pairs={{0,1},{1,0},{2,3},{3,2},{4,5},{5,4},{6,7},{7,6},{8,9},{9,8},{10,11... | collective-permute-start | bytes 786440 | tf_op jit(solution)/shard_map/ppermute | solution.py:124
  67.2 8.4 %collective-permute-start.25 = (bf16[512,256]{1,0:T(8,128)(2,1)S(1)}, bf16[512,256]{1,0:T(8,128)(2,1)S(1)}, u32[]{:S(2)}, u32[]{:S(2)}) collective-permute-start(bf16[512,256]{1,0:T(8,128)(2,1)S(1)} %shard_map.97), channel_id=1, source_target_pairs={{0,2},{1,3},{2,0},{3,1},{4,6},{5,7},{6,4},{7,5},{8,10},{9,11},{10,... | collective-permute-start | bytes 786440 | tf_op jit(solution)/shard_map/ppermute | solution.py:124

commit v3 on v2

--- a/solution.py
+++ b/solution.py
@@ -15,6 +15,8 @@
 WINDOW = 8
 RIM = (KERNEL - 1) * DILATION
 GAIN_ROWS = 8
+CONV_VMEM = 60
+FIX_US = 2.0
 NEG = -1e30
 F32 = jnp.float32
 BF16 = jnp.bfloat16
@@ -150,9 +152,18 @@
     return (x32 + jax.nn.gelu(term, approximate=True)).astype(BF16)
 
 
-def conv_kernel(x_ref, w_ref, b_ref, g_ref, late_ref, early_ref, band_ref, base_ref):
+def conv_kernel(
+    x_hbm, w_hbm, b_hbm, g_hbm, late_ref, early_ref, band_ref, base_ref, edge_ref,
+    x_ref, w_ref, b_ref, g_ref, sems,
+):
+    pairs = ((x_hbm, x_ref), (w_hbm, w_ref), (b_hbm, b_ref), (g_hbm, g_ref))
+    copies = [pltpu.make_async_copy(src, dst, sems.at[i]) for i, (src, dst) in enumerate(pairs)]
+    for copy in copies:
+        copy.start()
+    for copy in copies:
+        copy.wait()
     rows = x_ref.shape[0]
-    half = rows // 2
+    edge_ref[...] = x_ref[rows - RIM :]
     groups, width, _ = w_ref.shape
     x32 = x_ref[...].astype(F32)
     ext = jnp.concatenate([jnp.zeros((RIM, x32.shape[1]), F32), x32], axis=0)
@@ -167,16 +178,25 @@
                 parts.append(jnp.zeros((width, (groups - 1 - g) * width), F32))
             bands.append(jnp.concatenate(parts, axis=1))
         band = jnp.concatenate(bands, axis=0).astype(BF16)
-        band_ref[j] = band
+        if j < KERNEL - 1:
+            band_ref[j] = band
         acc += dot_nt(ext[j * DILATION : j * DILATION + rows].astype(BF16), band)
     base_ref[0:RIM] = acc[0:RIM]
     base_ref[RIM:] = x32[0:RIM]
     mix = gelu_mix(x32, acc)
-    gain = jnp.broadcast_to(g_ref[...].astype(F32), (GAIN_ROWS, x32.shape[1])).astype(BF16)
+    pieces = g_ref[...].astype(F32)
+    gain = jnp.concatenate([pieces[i : i + 1] for i in range(pieces.shape[0])], axis=1)
+    gain = jnp.broadcast_to(gain, (GAIN_ROWS, gain.shape[1])).astype(BF16)
+    half = rows // 2
     late_ref[0:half] = mix[0:half]
     late_ref[half:] = gain
     early_ref[0:half] = mix[half:]
     early_ref[half:] = gain
+
+
+def stage_kernel(*refs):
+    for ref, out in zip(refs[:3], refs[3:]):
+        out[...] = ref[...]
 
 
 def fix_kernel(halo_ref, base_ref, band_ref, late_ref, o_ref):
@@ -231,8 +251,21 @@
         out[...] = pack[m]
 
 
-def attend_kernel(pos_ref, valid_ref, *rest):
-    own_refs, oth_refs, (o_ref, kb, vb, qs, sc) = rest[:8], rest[8:16], rest[16:]
+def pack_kernel(pos_ref, *rest):
+    own_refs, kv_ref, qs_ref = rest[:8], rest[8], rest[9]
+    half = kv_ref.shape[1]
+    lane = lane_iota((half // 2, 128))
+    pad = jnp.where(lane == HEAD_DIM, 1.0, 0.0)
+    for i, ref in enumerate(own_refs):
+        kv_ref[i] = ref[0:half, :]
+        shard = 4 * jnp.bitwise_xor(pos_ref[0], 1 - i // 4) + jnp.bitwise_xor(pos_ref[2], i % 4)
+        packed = ref[half:, :].astype(F32)
+        rolled = pltpu.roll(packed, HEAD_DIM, 1)
+        qs_ref[shard, 0 : half // 2] = jnp.where(lane < HEAD_DIM, packed, pad).astype(BF16)
+        qs_ref[shard, half // 2 :] = jnp.where(lane < HEAD_DIM, rolled, pad).astype(BF16)
+
+
+def attend_kernel(pos_ref, valid_ref, own_ref, oth_ref, qs, o_ref, kb, vb, sc):
     ranks = o_ref.shape[0]
     half = o_ref.shape[1] * 2
     halfrows = half // 2
@@ -240,28 +273,22 @@
     lane = lane_iota((half, 128))
     row = lax.broadcasted_iota(jnp.int32, (half, 128), 0)
     lane_h = lane_iota((halfrows, 128))
-    pad = jnp.where(lane_h == HEAD_DIM, 1.0, 0.0)
     for i in range(8):
-        part, m = 1 - i // 4, i % 4
-        for side, ref in ((core, own_refs[i]), (1 - core, oth_refs[i])):
-            shard = 4 * jnp.bitwise_xor(side, part) + jnp.bitwise_xor(low, m)
+        part = 1 - i // 4
+        for side, ref in ((core, own_ref), (1 - core, oth_ref)):
+            shard = 4 * jnp.bitwise_xor(side, part) + jnp.bitwise_xor(low, i % 4)
             block = 2 * shard + part
             start = block * half
             stretch = start // STRETCH
             ok = row + (start - stretch * STRETCH) < valid_ref[stretch]
             bias = jnp.where(jnp.logical_and(lane == HEAD_DIM, jnp.logical_not(ok)), NEG, 0.0)
-            kv = ref[0:half, :].astype(F32)
+            kv = ref[i].astype(F32)
             kb[block] = jnp.where(lane < HEAD_DIM, kv, bias).astype(BF16)
             vb[block] = jnp.where(lane < HEAD_DIM, 1.0, kv).astype(BF16)
-            if ref is own_refs[i]:
-                packed = ref[half:, :].astype(F32)
-                qs[shard, 0:halfrows] = jnp.where(lane_h < HEAD_DIM, packed, pad).astype(BF16)
-                qs[shard, halfrows:] = jnp.where(
-                    lane_h < HEAD_DIM, pltpu.roll(packed, HEAD_DIM, 1), pad
-                ).astype(BF16)
     qrow = lax.broadcasted_iota(jnp.int32, (half, half), 0)
     kcol = lane_iota((half, half))
-    for t in range(ranks):
+
+    def scores(t):
         part = jnp.bitwise_xor(core, t // 4)
         q = qs[t]
         top = jnp.full((half, 128), NEG, F32)
@@ -269,56 +296,63 @@
             s = dot_nt(q, kb[b])
             if b >= 2 * t:
                 s = jnp.where(kcol + (b - 2 * t) * half <= qrow + part * half, s, NEG)
-            sc[b] = s
+            sc[t % 2, b] = s
             for piece in range(half // 128):
                 top = jnp.maximum(top, s[:, piece * 128 : (piece + 1) * 128])
-        m = jnp.max(top, axis=1, keepdims=True)
+        return jnp.max(top, axis=1, keepdims=True)
+
+    def values(t, m):
         acc = jnp.zeros((half, 128), F32)
         for b in range(2 * t + 2):
-            acc += dot32(jnp.exp(sc[b] - m).astype(BF16), vb[b])
+            acc += dot32(jnp.exp(sc[t % 2, b] - m).astype(BF16), vb[b])
         out = acc / pltpu.roll(acc, HEAD_DIM, 1)
-        o_ref[t] = jnp.where(
-            lane_h < HEAD_DIM, pltpu.roll(out[:halfrows], HEAD_DIM, 1), out[halfrows:]
-        ).astype(BF16)
-
-
-def out_kernel(pos_ref, own_ref, oth_ref, w0, w1, o_ref, *, other):
-    heads = own_ref.shape[0]
-    halfrows = own_ref.shape[1]
-    half = 2 * halfrows
-    cols = o_ref.shape[1]
+        left = pltpu.roll(out[:halfrows], HEAD_DIM, 1)
+        o_ref[t] = jnp.where(lane_h < HEAD_DIM, left, out[halfrows:]).astype(BF16)
+
+    tops = [scores(0)]
+    for t in range(ranks):
+        if t < ranks - 1:
+            tops.append(scores(t + 1))
+        values(t, tops[t])
+
+
+def out_kernel(pos_ref, att_ref, w0, w1, own_ref, *outs):
+    heads, quarter, _ = att_ref.shape
+    cols = own_ref.shape[1]
     core, ychip = pos_ref[0], pos_ref[1]
-    mine = jnp.bitwise_xor(core, pos_ref[3])
-    group = 2 * ((1 - ychip) if other else ychip) + core
-    lanes = pl.ds(pl.multiple_of(group * cols, cols), cols)
-    lane_h = lane_iota((halfrows, 128))
-    for src, part in ((own_ref, mine), (oth_ref, 1 - mine)):
-        total = None
-        for first, w in ((core, w0), (1 - core, w1)):
-            tops, bots = [], []
-            for j in range(0, heads // 2, 2):
-                a = src[first * (heads // 2) + j].astype(F32)
-                b = src[first * (heads // 2) + j + 1].astype(F32)
-                tops.append(jnp.where(lane_h < HEAD_DIM, a, pltpu.roll(b, HEAD_DIM, 1)))
-                bots.append(jnp.where(lane_h < HEAD_DIM, pltpu.roll(a, HEAD_DIM, 1), b))
-            feats = jnp.concatenate(
+    lane = lane_iota((quarter, 128))
+    feats = []
+    for first in (core, 1 - core):
+        tops, bots = [], []
+        for j in range(0, heads // 2, 2):
+            a = att_ref[first * (heads // 2) + j].astype(F32)
+            b = att_ref[first * (heads // 2) + j + 1].astype(F32)
+            tops.append(jnp.where(lane < HEAD_DIM, a, pltpu.roll(b, HEAD_DIM, 1)))
+            bots.append(jnp.where(lane < HEAD_DIM, pltpu.roll(a, HEAD_DIM, 1), b))
+        feats.append(
+            jnp.concatenate(
                 [jnp.concatenate(tops, axis=1), jnp.concatenate(bots, axis=1)], axis=0
             ).astype(BF16)
-            term = dot32(feats, w[:, lanes])
-            total = term if total is None else total + term
-        o_ref[pl.ds(pl.multiple_of(part * half, half), half), :] = total.astype(o_ref.dtype)
-
-
-def final_kernel(late_ref, early_ref, proj_ref, across_ref, o_ref):
-    half = o_ref.shape[0] // 2
-    for i, ref in enumerate((late_ref, early_ref)):
-        rows = slice(i * half, (i + 1) * half)
-        proj = proj_ref[rows] + across_ref[rows].astype(F32)
-        o_ref[rows] = (ref[0:half].astype(F32) + proj).astype(BF16)
-
-
-def call(kernel, outs, scalars, args, *, us, vmem=16, scratch=()):
-    spaces = [pltpu.SMEM] * scalars + [pltpu.VMEM] * (len(args) - scalars)
+        )
+    for step, ref in enumerate((own_ref, *outs)):
+        group = jnp.bitwise_xor(2 * ychip + core, step)
+        lanes = pl.ds(pl.multiple_of(group * cols, cols), cols)
+        total = dot32(feats[0], w0[:, lanes]) + dot32(feats[1], w1[:, lanes])
+        ref[...] = total.astype(ref.dtype)
+
+
+def final_kernel(pos_ref, late_ref, early_ref, own_ref, beside_ref, across_ref, corner_ref, o_ref):
+    half = own_ref.shape[0]
+    first = jnp.bitwise_xor(pos_ref[0], pos_ref[3]) == 0
+    own = own_ref[...] + across_ref[...].astype(F32)
+    other = beside_ref[...].astype(F32) + corner_ref[...].astype(F32)
+    pick = jnp.broadcast_to(first, own.shape)
+    o_ref[0:half] = (late_ref[0:half].astype(F32) + jnp.where(pick, own, other)).astype(BF16)
+    o_ref[half:] = (early_ref[0:half].astype(F32) + jnp.where(pick, other, own)).astype(BF16)
+
+
+def call(kernel, outs, scalars, args, *, us, vmem=16, scratch=(), space=pltpu.VMEM):
+    spaces = [pltpu.SMEM] * scalars + [space] * (len(args) - scalars)
     outs = [jax.ShapeDtypeStruct(*out) for out in outs]
     result = pl.pallas_call(
         kernel,
@@ -341,28 +375,42 @@
     half = tok // 2
     ranks = lax.axis_size("tm")
     head_at, shard = lax.axis_index("head"), lax.axis_index("tm")
-    pos = jnp.stack([head_at % 2, head_at // 2, shard % 4, shard // 4]).astype(jnp.int32)
-
-    halo = from_behind(tokens_in[tok - RIM :], "tm", 1)
-    late, early, band, base = call(
+    pos = jnp.stack([head_at & 1, head_at >> 1, shard & 3, shard >> 2]).astype(jnp.int32)
+
+    operands = (
+        tokens_in, jnp.swapaxes(conv_weight, 1, 2),
+        conv_bias.reshape(1, cols), norm_gain.reshape(cols // 128, 128),
+    )
+    late, early, band, base, edge = call(
         conv_kernel,
         [
             ((half + GAIN_ROWS, cols), BF16),
             ((half + GAIN_ROWS, cols), BF16),
-            ((KERNEL, cols, cols), BF16),
+            ((KERNEL - 1, cols, cols), BF16),
             ((2 * RIM, cols), F32),
+            ((RIM, cols), BF16),
         ],
         0,
-        (
-            tokens_in, jnp.swapaxes(conv_weight, 1, 2),
-            conv_bias.reshape(1, cols), norm_gain.reshape(1, cols),
-        ),
+        operands,
         us=2.0,
-    )
-
-    def project_half(x):
-        beside, across = swap(x, 1), swap(x, 2)
-        corner = swap(across, 1)
+        vmem=CONV_VMEM,
+        scratch=[pltpu.VMEM(x.shape, x.dtype) for x in operands]
+        + [pltpu.SemaphoreType.DMA((len(operands),))],
+        space=pltpu.HBM,
+    )
+    halo = from_behind(edge, "tm", 1)
+    base, band, late = call(
+        stage_kernel, [(x.shape, x.dtype) for x in (base, band, late)], 0, (base, band, late), us=1.0
+    )
+
+    def project_half(x, after=None):
+        across = swap(x, 2)
+        if after is not None:
+            corner = swap(x, 3)
+            x = lax.optimization_barrier((x, after))[0]
+        else:
+            corner = swap(across, 1)
+        beside = swap(x, 1)
         return call(
             qkv_kernel,
             [((half + half // 2, 2 * HEAD_DIM), BF16)] * 4,
@@ -374,40 +422,44 @@
 
     sends = list(project_half(early))
     late = call(
-        fix_kernel, [((half + GAIN_ROWS, cols), BF16)], 0, (halo, base, band, late), us=0.5
-    )
-    sends += list(project_half(late))
+        fix_kernel, [((half + GAIN_ROWS, cols), BF16)], 0, (halo, base, band, late), us=FIX_US
+    )
+    sends += list(project_half(late, sends[0]))
     own = [spread(value, i % 4, 1 - i // 4) for i, value in enumerate(sends)]
-    oth = [swap(value, 1) for value in own]
+    kv, qs = call(
+        pack_kernel,
+        [((8, half, 128), BF16), ((8, half, 128), BF16)],
+        1,
+        (pos, *own),
+        us=0.5,
+    )
     wo1 = swap(lax.optimization_barrier((w_out, sends[0]))[0], 1)
     attended = call(
         attend_kernel,
-        [((ranks, half // 2, 2 * HEAD_DIM), BF16)],
+        [((8, half // 2, 2 * HEAD_DIM), BF16)],
         2,
-        (pos, valid_count, *own, *oth),
+        (pos, valid_count, kv, swap(kv, 1), qs),
         us=8.0,
         vmem=24,
         scratch=[
-            pltpu.VMEM((2 * ranks, half, 128), BF16),
-            pltpu.VMEM((2 * ranks, half, 128), BF16),
-            pltpu.VMEM((ranks, half, 128), BF16),
-            pltpu.VMEM((2 * ranks, half, half), F32),
+            pltpu.VMEM((16, half, 128), BF16),
+            pltpu.VMEM((16, half, 128), BF16),
+            pltpu.VMEM((2, 16, half, half), F32),
         ],
     )
     back = lax.all_to_all(attended, "tm", 0, 0)
-    back_beside = swap(back, 1)
-
-    def project(other, dtype):
-        kernel = functools.partial(out_kernel, other=other)
-        args = (pos, back, back_beside, w_out, wo1)
-        return call(kernel, [((tok, cols), dtype)], 1, args, us=1.0)
-
-    proj_across = swap(project(True, BF16), 2)
+    own, beside, across, corner = call(
+        out_kernel,
+        [((half, cols), F32)] + [((half, cols), BF16)] * 3,
+        1,
+        (pos, back, w_out, wo1),
+        us=1.0,
+    )
     return call(
         final_kernel,
         [((tok, cols), BF16)],
-        0,
-        (late, early, project(False, F32), proj_across),
+        1,
+        (pos, late, early, own, swap(beside, 1), swap(across, 2), swap(corner, 3)),
         us=0.5,
     )
 

time: 76.7 us -> 73.3 us (0.956)
  waiting for transfers between devices: 25.8 us -> 22.6 us
  Pallas kernels: 15.4 us -> 16.5 us
    ppermute x17 -> x11, waiting for transfers between devices: 13.8 us -> 8.34 us  [swap(): lax.ppermute(value, 'head', [(i, i ^ bit) for i in range(lax.axis_size('h...]
    ppermute x8, waiting for transfers between devices: 2.71 us -> 4.64 us  [spread(): return lax.ppermute(value, ('tm', 'head'), pairs)]
    ppermute x1, starting transfers between devices: 4.83 us -> 3.38 us  [from_behind(): lax.ppermute(value, axis, [(source, source + steps) for source in range(f...]
    ppermute x17 -> x11, starting transfers between devices: 12.4 us -> 13.6 us  [swap(): lax.ppermute(value, 'head', [(i, i ^ bit) for i in range(lax.axis_size('h...]
    pallas_call x8 -> x9, Pallas kernels: 15.4 us -> 16.5 us  [call(): pl.pallas_call(kernel, out_shape=outs, in_specs=[pl.BlockSpec(memory_spac...]
  transfers between devices with their start and end apart: 27 -> 21, of which waited for: 11 -> 9; matrix products, arithmetic and copies ran while one was open for 0% -> 0% of each run, Pallas kernels for 6% -> 15%
where the time goes in v3:
time: 73.3 us; the launch traced here: 72.9 us
  starting transfers between devices  31.1 us (42%)
  waiting for transfers between devices  22.6 us (31%)
  Pallas kernels  16.5 us (23%)
  local copies, waits for them, and re-layouts  2.51 us (3%)
    pallas_call x9, Pallas kernels, call(): pl.pallas_call(kernel, out_shape=outs, in_specs=[pl.BlockSpec(memory_spac...  16.5 us
    ppermute x11, starting transfers between devices, swap(): lax.ppermute(value, 'head', [(i, i ^ bit) for i in range(lax.axis_size('h...  13.6 us
    ppermute x8, starting transfers between devices, spread(): return lax.ppermute(value, ('tm', 'head'), pairs)  10.7 us
    all_to_all x1, waiting for transfers between devices, on_device(): back = lax.all_to_all(attended, 'tm', 0, 0)  9.61 us
    ppermute x11, waiting for transfers between devices, swap(): lax.ppermute(value, 'head', [(i, i ^ bit) for i in range(lax.axis_size('h...  8.34 us
    ppermute x8, waiting for transfers between devices, spread(): return lax.ppermute(value, ('tm', 'head'), pairs)  4.64 us
    all_to_all x1, starting transfers between devices, on_device(): back = lax.all_to_all(attended, 'tm', 0, 0)  3.45 us
    ppermute x1, starting transfers between devices, from_behind(): lax.ppermute(value, axis, [(source, source + steps) for source in range(f...  3.38 us
  transfers between devices with their start and end apart: 21, of which 9 were waited for; matrix products, arithmetic and copies ran while one was open for 0% of the time, Pallas kernels for 15%

profile of v3, /device:TPU:0, one launch (start us, length us, event | category | flops | bytes accessed | tf_op | source)
XLA Modules:
  0.0 72.9 jit_solution(4479098933605661698)
XLA Ops:
  0.0 2.4 %shard_map.91 = (bf16[264,256]{1,0:T(8,128)(2,1)}, bf16[264,256]{1,0:T(8,128)(2,1)}, bf16[2,256,256]{2,1,0:T(8,128)(2,1)}, f32[16,256]{1,0:T(8,128)}, bf16[8,256]{1,0:T(8,128)(2,1)}) custom-call(bf16[512,256]{1,0:T(8,128)(2,1)} %x_hbm.1, bf16[4,64,192]{2,1,0:T(8,128)(2,1)} %bitcast.7, f32[1,256]{1,0:T(1,128)} %bitcast.8, bf16[2,128]{1,0:T(2,128)(2,1)} %bitcast.9), custom_call_target="tpu_custom_call" | custom-call | flops 2000000000 | bytes 7200000 | tf_op jit(solution)/shard_map/pallas_call | solution.py:357
  2.4 3.0 %collective-permute-start.2 = (bf16[264,256]{1,0:T(8,128)(2,1)}, bf16[264,256]{1,0:T(8,128)(2,1)S(1)}, u32[]{:S(2)}, u32[]{:S(2)}) collective-permute-start(bf16[264,256]{1,0:T(8,128)(2,1)} %get-tuple-element.36.a_ref.early_ref), channel_id=1, source_target_pairs={{0,2},{1,3},{2,0},{3,1},{4,6},{5,7},{6,4},{7,5},{8,10},{9,11},{10,... | collective-permute-start | bytes 405512 | tf_op jit(solution)/shard_map/ppermute | solution.py:126
  5.4 0.0 collective-permute-start.1
  5.4 3.4 %collective-permute-start = (bf16[8,256]{1,0:T(8,128)(2,1)}, bf16[8,256]{1,0:T(8,128)(2,1)S(1)}, u32[]{:S(2)}, u32[]{:S(2)}) collective-permute-start(bf16[8,256]{1,0:T(8,128)(2,1)} %get-tuple-element.29), channel_id=1, source_target_pairs={{0,4},{4,8},{8,12},{12,16},{16,20},{20,24},{24,28},{1,5},{5,9},{9,... | collective-permute-start | bytes 12296 | tf_op jit(solution)/shard_map/ppermute | solution.py:28
  8.8 0.1 pad_add_fusion.pos_ref
  8.9 0.6 copy-done.8
  9.5 0.9 %copy-done.6 = bf16[2,256,256]{2,1,0:T(8,128)(2,1)S(1)} copy-done((bf16[2,256,256]{2,1,0:T(8,128)(2,1)S(1)}, bf16[2,256,256]{2,1,0:T(8,128)(2,1)}, u32[]{:S(2)}) %copy-start.6) | copy-done | bytes 262168
  10.5 0.9 %copy-done.7 = bf16[264,256]{1,0:T(8,128)(2,1)S(1)} copy-done((bf16[264,256]{1,0:T(8,128)(2,1)S(1)}, bf16[264,256]{1,0:T(8,128)(2,1)}, u32[]{:S(2)}) %copy-start.7) | copy-done | bytes 135192
  11.4 0.0 collective-permute-done.2.y_ref
  11.4 0.3 collective-permute-start.3
  11.7 0.0 collective-permute-done.halo_ref
  11.7 0.2 shard_map.93.a_ref.late_ref
  11.9 0.5 collective-permute-start.10
  12.4 1.5 %collective-permute-start.9 = (bf16[264,256]{1,0:T(8,128)(2,1)S(1)}, bf16[264,256]{1,0:T(8,128)(2,1)S(1)}, u32[]{:S(2)}, u32[]{:S(2)}) collective-permute-start(bf16[264,256]{1,0:T(8,128)(2,1)S(1)} %shard_map.93.a_ref.late_ref), channel_id=1, source_target_pairs={{0,2},{1,3},{2,0},{3,1},{4,6},{5,7},{6,4},{7,5},{8,10},{9,11},{10,... | collective-permute-start | bytes 405512 | tf_op jit(solution)/shard_map/ppermute | solution.py:126
  13.9 0.0 collective-permute-done.1.b_ref
  14.0 1.4 %shard_map.94 = (bf16[384,128]{1,0:T(8,128)(2,1)S(1)}, bf16[384,128]{1,0:T(8,128)(2,1)S(1)}, bf16[384,128]{1,0:T(8,128)(2,1)S(1)}, bf16[384,128]{1,0:T(8,128)(2,1)S(1)}) custom-call(s32[4]{0:T(128)S(1)} %pad_add_fusion.pos_ref, bf16[264,256]{1,0:T(8,128)(2,1)S(1)} %copy-done.4, bf16[264,256]{1,0:T(8,128)(2,1)S(1)} %collective-permute-done.1.b_ref, ...), custom_call_target="tpu_custom_call" | custom-call | flops 1000000000 | bytes 3600000 | tf_op jit(solution)/shard_map/pallas_call | solution.py:357
  15.3 0.1 collective-permute-start.8
  15.4 1.7 %collective-permute-start.5 = (bf16[384,128]{1,0:T(8,128)(2,1)S(1)}, bf16[384,128]{1,0:T(8,128)(2,1)S(1)}, u32[]{:S(2)}, u32[]{:S(2)}) collective-permute-start(bf16[384,128]{1,0:T(8,128)(2,1)S(1)} %get-tuple-element.38), channel_id=1, source_target_pairs={{0,5},{1,21},{2,7},{3,23},{4,1},{5,17},{6,3},{7,19},{8,13},{9,29},... | collective-permute-start | bytes 294920 | tf_op jit(solution)/shard_map/ppermute | solution.py:136
  17.1 2.2 %collective-permute-start.6 = (bf16[384,128]{1,0:T(8,128)(2,1)S(1)}, bf16[384,128]{1,0:T(8,128)(2,1)S(1)}, u32[]{:S(2)}, u32[]{:S(2)}) collective-permute-start(bf16[384,128]{1,0:T(8,128)(2,1)S(1)} %get-tuple-element.39), channel_id=1, source_target_pairs={{0,9},{1,25},{2,11},{3,27},{4,13},{5,29},{6,15},{7,31},{8,1},{9,17... | collective-permute-start | bytes 294920 | tf_op jit(solution)/shard_map/ppermute | solution.py:136
  19.2 1.1 %collective-permute-start.7 = (bf16[384,128]{1,0:T(8,128)(2,1)S(1)}, bf16[384,128]{1,0:T(8,128)(2,1)S(1)}, u32[]{:S(2)}, u32[]{:S(2)}) collective-permute-start(bf16[384,128]{1,0:T(8,128)(2,1)S(1)} %get-tuple-element.40), channel_id=1, source_target_pairs={{0,13},{1,29},{2,15},{3,31},{4,9},{5,25},{6,11},{7,27},{8,5},{9,21... | collective-permute-start | bytes 294920 | tf_op jit(solution)/shard_map/ppermute | solution.py:136
  20.3 0.5 collective-permute-done.9.y_ref
  20.8 0.0 collective-permute-done.8.b_ref
  20.8 1.4 %shard_map.95 = (bf16[384,128]{1,0:T(8,128)(2,1)S(1)}, bf16[384,128]{1,0:T(8,128)(2,1)S(1)}, bf16[384,128]{1,0:T(8,128)(2,1)S(1)}, bf16[384,128]{1,0:T(8,128)(2,1)S(1)}) custom-call(s32[4]{0:T(128)S(1)} %pad_add_fusion.pos_ref, bf16[264,256]{1,0:T(8,128)(2,1)S(1)} %shard_map.93.a_ref.late_ref, bf16[264,256]{1,0:T(8,128)(2,1)S(1)} %collective-permute-done.8.b_ref, ...), custom_call_target="tpu_custom_call" | custom-call | flops 1000000000 | bytes 3600000 | tf_op jit(solution)/shard_map/pallas_call | solution.py:357
  22.2 0.7 collective-permute-start.11
  22.9 2.2 %collective-permute-start.12 = (bf16[384,128]{1,0:T(8,128)(2,1)S(1)}, bf16[384,128]{1,0:T(8,128)(2,1)S(1)}, u32[]{:S(2)}, u32[]{:S(2)}) collective-permute-start(bf16[384,128]{1,0:T(8,128)(2,1)S(1)} %get-tuple-element.43), channel_id=1, source_target_pairs={{0,4},{1,20},{2,6},{3,22},{4,0},{5,16},{6,2},{7,18},{8,12},{9,28},... | collective-permute-start | bytes 294920 | tf_op jit(solution)/shard_map/ppermute | solution.py:136
  25.1 1.0 %collective-permute-done.6.rest_2_ = bf16[384,128]{1,0:T(8,128)(2,1)S(1)} collective-permute-done((bf16[384,128]{1,0:T(8,128)(2,1)S(1)}, bf16[384,128]{1,0:T(8,128)(2,1)S(1)}, u32[]{:S(2)}, u32[]{:S(2)}) %collective-permute-start.6) | collective-permute-done | bytes 98336 | tf_op jit(solution)/shard_map/ppermute | solution.py:136
  26.1 0.0 collective-permute-start.13
  26.1 0.9 %collective-permute-done.7.rest_3_ = bf16[384,128]{1,0:T(8,128)(2,1)S(1)} collective-permute-done((bf16[384,128]{1,0:T(8,128)(2,1)S(1)}, bf16[384,128]{1,0:T(8,128)(2,1)S(1)}, u32[]{:S(2)}, u32[]{:S(2)}) %collective-permute-start.7) | collective-permute-done | bytes 98336 | tf_op jit(solution)/shard_map/ppermute | solution.py:136
  27.0 2.9 %collective-permute-start.14 = (bf16[384,128]{1,0:T(8,128)(2,1)S(1)}, bf16[384,128]{1,0:T(8,128)(2,1)S(1)}, u32[]{:S(2)}, u32[]{:S(2)}) collective-permute-start(bf16[384,128]{1,0:T(8,128)(2,1)S(1)} %get-tuple-element.45), channel_id=1, source_target_pairs={{0,12},{1,28},{2,14},{3,30},{4,8},{5,24},{6,10},{7,26},{8,4},{9,20... | collective-permute-start | bytes 294920 | tf_op jit(solution)/shard_map/ppermute | solution.py:136
  29.9 0.0 collective-permute-done.12.rest_5_
  29.9 0.9 %collective-permute-done.13.rest_6_ = bf16[384,128]{1,0:T(8,128)(2,1)S(1)} collective-permute-done((bf16[384,128]{1,0:T(8,128)(2,1)S(1)}, bf16[384,128]{1,0:T(8,128)(2,1)S(1)}, u32[]{:S(2)}, u32[]{:S(2)}) %collective-permute-start.13) | collective-permute-done | bytes 98336 | tf_op jit(solution)/shard_map/ppermute | solution.py:136
  30.8 1.8 %collective-permute-done.14.rest_7_ = bf16[384,128]{1,0:T(8,128)(2,1)S(1)} collective-permute-done((bf16[384,128]{1,0:T(8,128)(2,1)S(1)}, bf16[384,128]{1,0:T(8,128)(2,1)S(1)}, u32[]{:S(2)}, u32[]{:S(2)}) %collective-permute-start.14) | collective-permute-done | bytes 98336 | tf_op jit(solution)/shard_map/ppermute | solution.py:136
  32.6 0.7 shard_map.96
  33.3 0.0 copy-start.5
  33.3 6.2 %collective-permute-start.15 = (bf16[8,256,128]{2,1,0:T(8,128)(2,1)S(1)}, bf16[8,256,128]{2,1,0:T(8,128)(2,1)S(1)}, u32[]{:S(2)}, u32[]{:S(2)}) collective-permute-start(bf16[8,256,128]{2,1,0:T(8,128)(2,1)S(1)} %get-tuple-element.46.own_ref), channel_id=1, source_target_pairs={{0,1},{1,0},{2,3},{3,2},{4,5},{5,4},{6,7},{7,6},{8,9},{9,8},{10,11... | collective-permute-start | bytes 1572872 | tf_op jit(solution)/shard_map/ppermute | solution.py:126
  39.5 0.1 collective-permute-start.16
  39.6 1.4 %collective-permute-done.15.oth_ref = bf16[8,256,128]{2,1,0:T(8,128)(2,1)S(1)} collective-permute-done((bf16[8,256,128]{2,1,0:T(8,128)(2,1)S(1)}, bf16[8,256,128]{2,1,0:T(8,128)(2,1)S(1)}, u32[]{:S(2)}, u32[]{:S(2)}) %collective-permute-start.15) | collective-permute-done | bytes 524320 | tf_op jit(solution)/shard_map/ppermute | solution.py:126
  41.0 8.1 %shard_map.97 = bf16[8,128,128]{2,1,0:T(8,128)(2,1)} custom-call(s32[4]{0:T(128)S(1)} %pad_add_fusion.pos_ref, s32[4]{0:T(128)S(1)} %copy-done.5, bf16[8,256,128]{2,1,0:T(8,128)(2,1)S(1)} %get-tuple-element.46.own_ref, bf16[8,256,128]{2,1,0:T(8,128)(2,1)S(1)} %collective-permute-done.15.oth_ref, bf16[8,256,128]{2,1,0:T(8,128)(2,1)S(1)} %get-tuple-element.47.qs), custom_call_target="tpu_custom_call" | custom-call | flops 8000000000 | bytes 28800000 | tf_op jit(solution)/shard_map/pallas_call | solution.py:357
  49.1 3.5 %all-to-all-start = ((bf16[8,128,128]{2,1,0:T(8,128)(2,1)}), bf16[8,128,128]{2,1,0:T(8,128)(2,1)S(1)}, u32[]{:S(2)}, u32[]{:S(2)}) async-start(bf16[8,128,128]{2,1,0:T(8,128)(2,1)} %shard_map.97), calls=%async_computation | async-start | bytes 524288 | tf_op jit(solution)/shard_map/all_to_all | solution.py:450
  52.6 0.0 collective-permute-done.16.w1
  52.6 9.6 %all-to-all-done.att_ref = bf16[8,128,128]{2,1,0:T(8,128)(2,1)S(1)} async-done(((bf16[8,128,128]{2,1,0:T(8,128)(2,1)}), bf16[8,128,128]{2,1,0:T(8,128)(2,1)S(1)}, u32[]{:S(2)}, u32[]{:S(2)}) %all-to-all-start) | async-done | bytes 262176 | tf_op jit(solution)/shard_map/all_to_all | solution.py:450
  62.2 1.0 %shard_map.98 = (f32[256,256]{1,0:T(8,128)S(1)}, bf16[256,256]{1,0:T(8,128)(2,1)S(1)}, bf16[256,256]{1,0:T(8,128)(2,1)S(1)}, bf16[256,256]{1,0:T(8,128)(2,1)S(1)}) custom-call(s32[4]{0:T(128)S(1)} %pad_add_fusion.pos_ref, bf16[8,128,128]{2,1,0:T(8,128)(2,1)S(1)} %all-to-all-done.att_ref, bf16[256,1024]{1,0:T(8,128)(2,1)S(1)} %copy-done.3, ...), custom_call_target="tpu_custom_call" | custom-call | flops 1000000000 | bytes 3600000 | tf_op jit(solution)/shard_map/pallas_call | solution.py:357
  63.2 0.1 collective-permute-start.17
  63.3 0.6 collective-permute-start.18
  63.9 1.3 %collective-permute-start.19 = (bf16[256,256]{1,0:T(8,128)(2,1)S(1)}, bf16[256,256]{1,0:T(8,128)(2,1)S(1)}, u32[]{:S(2)}, u32[]{:S(2)}) collective-permute-start(bf16[256,256]{1,0:T(8,128)(2,1)S(1)} %get-tuple-element.52), channel_id=1, source_target_pairs={{0,3},{1,2},{2,1},{3,0},{4,7},{5,6},{6,5},{7,4},{8,11},{9,10},{10,... | collective-permute-start | bytes 393224 | tf_op jit(solution)/shard_map/ppermute | solution.py:126
  65.2 4.5 %collective-permute-done.18.across_ref = bf16[256,256]{1,0:T(8,128)(2,1)S(1)} collective-permute-done((bf16[256,256]{1,0:T(8,128)(2,1)S(1)}, bf16[256,256]{1,0:T(8,128)(2,1)S(1)}, u32[]{:S(2)}, u32[]{:S(2)}) %collective-permute-start.18) | collective-permute-done | bytes 131104 | tf_op jit(solution)/shard_map/ppermute | solution.py:126
  69.7 1.9 %collective-permute-done.19.corner_ref = bf16[256,256]{1,0:T(8,128)(2,1)S(1)} collective-permute-done((bf16[256,256]{1,0:T(8,128)(2,1)S(1)}, bf16[256,256]{1,0:T(8,128)(2,1)S(1)}, u32[]{:S(2)}, u32[]{:S(2)}) %collective-permute-start.19) | collective-permute-done | bytes 131104 | tf_op jit(solution)/shard_map/ppermute | solution.py:126
  71.6 1.4 %shard_map.99 = bf16[512,256]{1,0:T(8,128)(2,1)} custom-call(s32[4]{0:T(128)S(1)} %pad_add_fusion.pos_ref, bf16[264,256]{1,0:T(8,128)(2,1)S(1)} %shard_map.93.a_ref.late_ref, bf16[264,256]{1,0:T(8,128)(2,1)S(1)} %copy-done.4, f32[256,256]{1,0:T(8,128)S(1)} %get-tuple-element.49.own_ref, bf16[256,256]{1,0:T(8,128)(2,1)S(1)} %collective-permute-done.17.beside_ref, ...), custom_call_target="tpu_custom_call" | custom-call | flops 500000000 | bytes 1800000 | tf_op jit(solution)/shard_map/pallas_call | solution.py:357
  (22 shorter events, 0.1 us)
Async XLA Ops:
  2.4 9.0 %collective-permute-start.2 = (bf16[264,256]{1,0:T(8,128)(2,1)}, bf16[264,256]{1,0:T(8,128)(2,1)S(1)}, u32[]{:S(2)}, u32[]{:S(2)}) collective-permute-start(bf16[264,256]{1,0:T(8,128)(2,1)} %get-tuple-element.36.a_ref.early_ref), channel_id=1, source_target_pairs={{0,2},{1,3},{2,0},{3,1},{4,6},{5,7},{6,4},{7,5},{8,10},{9,11},{10,... | collective-permute-start | bytes 405512 | tf_op jit(solution)/shard_map/ppermute | solution.py:126
  5.4 8.5 %collective-permute-start.1 = (bf16[264,256]{1,0:T(8,128)(2,1)}, bf16[264,256]{1,0:T(8,128)(2,1)S(1)}, u32[]{:S(2)}, u32[]{:S(2)}) collective-permute-start(bf16[264,256]{1,0:T(8,128)(2,1)} %get-tuple-element.36.a_ref.early_ref), channel_id=1, source_target_pairs={{0,1},{1,0},{2,3},{3,2},{4,5},{5,4},{6,7},{7,6},{8,9},{9,8},{10,11... | collective-permute-start | bytes 405512 | tf_op jit(solution)/shard_map/ppermute | solution.py:126
  5.4 6.3 %collective-permute-start = (bf16[8,256]{1,0:T(8,128)(2,1)}, bf16[8,256]{1,0:T(8,128)(2,1)S(1)}, u32[]{:S(2)}, u32[]{:S(2)}) collective-permute-start(bf16[8,256]{1,0:T(8,128)(2,1)} %get-tuple-element.29), channel_id=1, source_target_pairs={{0,4},{4,8},{8,12},{12,16},{16,20},{20,24},{24,28},{1,5},{5,9},{9,... | collective-permute-start | bytes 12296 | tf_op jit(solution)/shard_map/ppermute | solution.py:28
  8.8 0.7 copy-start.8
  9.5 0.9 %copy-start.6 = (bf16[2,256,256]{2,1,0:T(8,128)(2,1)S(1)}, bf16[2,256,256]{2,1,0:T(8,128)(2,1)}, u32[]{:S(2)}) copy-start(bf16[2,256,256]{2,1,0:T(8,128)(2,1)} %get-tuple-element.31.refs_1_) | copy-start | bytes 786436
  10.5 0.9 %copy-start.7 = (bf16[264,256]{1,0:T(8,128)(2,1)S(1)}, bf16[264,256]{1,0:T(8,128)(2,1)}, u32[]{:S(2)}) copy-start(bf16[264,256]{1,0:T(8,128)(2,1)} %get-tuple-element.32.refs_2_) | copy-start | bytes 405508
  11.4 2.5 %collective-permute-start.3 = (bf16[264,256]{1,0:T(8,128)(2,1)S(1)}, bf16[264,256]{1,0:T(8,128)(2,1)S(1)}, u32[]{:S(2)}, u32[]{:S(2)}) collective-permute-start(bf16[264,256]{1,0:T(8,128)(2,1)S(1)} %collective-permute-done.2.y_ref), channel_id=1, source_target_pairs={{0,1},{1,0},{2,3},{3,2},{4,5},{5,4},{6,7},{7,6},{8,9},{9,8},{10,11... | collective-permute-start | bytes 405512 | tf_op jit(solution)/shard_map/ppermute | solution.py:126
  11.7 2.2 %copy-start = (bf16[1024,256]{1,0:T(8,128)(2,1)S(1)}, bf16[1024,256]{1,0:T(8,128)(2,1)}, u32[]{:S(2)}) copy-start(bf16[1024,256]{1,0:T(8,128)(2,1)} %wq.3) | copy-start | bytes 1572868
  11.7 2.2 %copy-start.1 = (bf16[1024,256]{1,0:T(8,128)(2,1)S(1)}, bf16[1024,256]{1,0:T(8,128)(2,1)}, u32[]{:S(2)}) copy-start(bf16[1024,256]{1,0:T(8,128)(2,1)} %wk.3) | copy-start | bytes 1572868
  11.7 2.2 %copy-start.2 = (bf16[1024,256]{1,0:T(8,128)(2,1)S(1)}, bf16[1024,256]{1,0:T(8,128)(2,1)}, u32[]{:S(2)}) copy-start(bf16[1024,256]{1,0:T(8,128)(2,1)} %wv.3) | copy-start | bytes 1572868
  11.7 2.2 %copy-start.4 = (bf16[264,256]{1,0:T(8,128)(2,1)S(1)}, bf16[264,256]{1,0:T(8,128)(2,1)}, u32[]{:S(2)}) copy-start(bf16[264,256]{1,0:T(8,128)(2,1)} %get-tuple-element.36.a_ref.early_ref) | copy-start | bytes 405508
  11.9 7.3 %collective-permute-start.10 = (bf16[264,256]{1,0:T(8,128)(2,1)S(1)}, bf16[264,256]{1,0:T(8,128)(2,1)S(1)}, u32[]{:S(2)}, u32[]{:S(2)}) collective-permute-start(bf16[264,256]{1,0:T(8,128)(2,1)S(1)} %shard_map.93.a_ref.late_ref), channel_id=1, source_target_pairs={{0,3},{1,2},{2,1},{3,0},{4,7},{5,6},{6,5},{7,4},{8,11},{9,10},{10,... | collective-permute-start | bytes 405512 | tf_op jit(solution)/shard_map/ppermute | solution.py:126
  12.4 8.4 %collective-permute-start.9 = (bf16[264,256]{1,0:T(8,128)(2,1)S(1)}, bf16[264,256]{1,0:T(8,128)(2,1)S(1)}, u32[]{:S(2)}, u32[]{:S(2)}) collective-permute-start(bf16[264,256]{1,0:T(8,128)(2,1)S(1)} %shard_map.93.a_ref.late_ref), channel_id=1, source_target_pairs={{0,2},{1,3},{2,0},{3,1},{4,6},{5,7},{6,4},{7,5},{8,10},{9,11},{10,... | collective-permute-start | bytes 405512 | tf_op jit(solution)/shard_map/ppermute | solution.py:126
  15.3 5.5 %collective-permute-start.8 = (bf16[264,256]{1,0:T(8,128)(2,1)S(1)}, bf16[264,256]{1,0:T(8,128)(2,1)S(1)}, u32[]{:S(2)}, u32[]{:S(2)}) collective-permute-start(bf16[264,256]{1,0:T(8,128)(2,1)S(1)} %shard_map.93.a_ref.late_ref), channel_id=1, source_target_pairs={{0,1},{1,0},{2,3},{3,2},{4,5},{5,4},{6,7},{7,6},{8,9},{9,8},{10,11... | collective-permute-start | bytes 405512 | tf_op jit(solution)/shard_map/ppermute | solution.py:126
  15.4 7.4 %collective-permute-start.5 = (bf16[384,128]{1,0:T(8,128)(2,1)S(1)}, bf16[384,128]{1,0:T(8,128)(2,1)S(1)}, u32[]{:S(2)}, u32[]{:S(2)}) collective-permute-start(bf16[384,128]{1,0:T(8,128)(2,1)S(1)} %get-tuple-element.38), channel_id=1, source_target_pairs={{0,5},{1,21},{2,7},{3,23},{4,1},{5,17},{6,3},{7,19},{8,13},{9,29},... | collective-permute-start | bytes 294920 | tf_op jit(solution)/shard_map/ppermute | solution.py:136
  17.1 9.1 %collective-permute-start.6 = (bf16[384,128]{1,0:T(8,128)(2,1)S(1)}, bf16[384,128]{1,0:T(8,128)(2,1)S(1)}, u32[]{:S(2)}, u32[]{:S(2)}) collective-permute-start(bf16[384,128]{1,0:T(8,128)(2,1)S(1)} %get-tuple-element.39), channel_id=1, source_target_pairs={{0,9},{1,25},{2,11},{3,27},{4,13},{5,29},{6,15},{7,31},{8,1},{9,17... | collective-permute-start | bytes 294920 | tf_op jit(solution)/shard_map/ppermute | solution.py:136
  19.2 7.8 %collective-permute-start.7 = (bf16[384,128]{1,0:T(8,128)(2,1)S(1)}, bf16[384,128]{1,0:T(8,128)(2,1)S(1)}, u32[]{:S(2)}, u32[]{:S(2)}) collective-permute-start(bf16[384,128]{1,0:T(8,128)(2,1)S(1)} %get-tuple-element.40), channel_id=1, source_target_pairs={{0,13},{1,29},{2,15},{3,31},{4,9},{5,25},{6,11},{7,27},{8,5},{9,21... | collective-permute-start | bytes 294920 | tf_op jit(solution)/shard_map/ppermute | solution.py:136
  20.8 9.1 %collective-permute-start.4 = (bf16[384,128]{1,0:T(8,128)(2,1)S(1)}, bf16[384,128]{1,0:T(8,128)(2,1)S(1)}, u32[]{:S(2)}, u32[]{:S(2)}) collective-permute-start(bf16[384,128]{1,0:T(8,128)(2,1)S(1)} %get-tuple-element.37), channel_id=1, source_target_pairs={{0,1},{1,17},{2,3},{3,19},{4,5},{5,21},{6,7},{7,23},{8,9},{9,25},{... | collective-permute-start | bytes 294920 | tf_op jit(solution)/shard_map/ppermute | solution.py:136
  22.2 7.7 %collective-permute-start.11 = (bf16[384,128]{1,0:T(8,128)(2,1)S(1)}, bf16[384,128]{1,0:T(8,128)(2,1)S(1)}, u32[]{:S(2)}, u32[]{:S(2)}) collective-permute-start(bf16[384,128]{1,0:T(8,128)(2,1)S(1)} %get-tuple-element.42), channel_id=1, source_target_pairs={{0,0},{1,16},{2,2},{3,18},{4,4},{5,20},{6,6},{7,22},{8,8},{9,24},{... | collective-permute-start | bytes 294920 | tf_op jit(solution)/shard_map/ppermute | solution.py:136
  22.9 7.0 %collective-permute-start.12 = (bf16[384,128]{1,0:T(8,128)(2,1)S(1)}, bf16[384,128]{1,0:T(8,128)(2,1)S(1)}, u32[]{:S(2)}, u32[]{:S(2)}) collective-permute-start(bf16[384,128]{1,0:T(8,128)(2,1)S(1)} %get-tuple-element.43), channel_id=1, source_target_pairs={{0,4},{1,20},{2,6},{3,22},{4,0},{5,16},{6,2},{7,18},{8,12},{9,28},... | collective-permute-start | bytes 294920 | tf_op jit(solution)/shard_map/ppermute | solution.py:136
  26.1 4.6 %collective-permute-start.13 = (bf16[384,128]{1,0:T(8,128)(2,1)S(1)}, bf16[384,128]{1,0:T(8,128)(2,1)S(1)}, u32[]{:S(2)}, u32[]{:S(2)}) collective-permute-start(bf16[384,128]{1,0:T(8,128)(2,1)S(1)} %get-tuple-element.44), channel_id=1, source_target_pairs={{0,8},{1,24},{2,10},{3,26},{4,12},{5,28},{6,14},{7,30},{8,0},{9,16... | collective-permute-start | bytes 294920 | tf_op jit(solution)/shard_map/ppermute | solution.py:136
  27.0 12.4 %copy-start.3 = (bf16[256,1024]{1,0:T(8,128)(2,1)S(1)}, bf16[256,1024]{1,0:T(8,128)(2,1)}, u32[]{:S(2)}) copy-start(bf16[256,1024]{1,0:T(8,128)(2,1)} %w0.1) | copy-start | bytes 1572868
  27.0 5.6 %collective-permute-start.14 = (bf16[384,128]{1,0:T(8,128)(2,1)S(1)}, bf16[384,128]{1,0:T(8,128)(2,1)S(1)}, u32[]{:S(2)}, u32[]{:S(2)}) collective-permute-start(bf16[384,128]{1,0:T(8,128)(2,1)S(1)} %get-tuple-element.45), channel_id=1, source_target_pairs={{0,12},{1,28},{2,14},{3,30},{4,8},{5,24},{6,10},{7,26},{8,4},{9,20... | collective-permute-start | bytes 294920 | tf_op jit(solution)/shard_map/ppermute | solution.py:136
  33.3 7.7 %copy-start.5 = (s32[4]{0:T(128)S(1)}, s32[4]{0:T(128)}, u32[]{:S(2)}) copy-start(s32[4]{0:T(128)} %valid_ref.1) | copy-start | bytes 52
  33.3 7.7 %collective-permute-start.15 = (bf16[8,256,128]{2,1,0:T(8,128)(2,1)S(1)}, bf16[8,256,128]{2,1,0:T(8,128)(2,1)S(1)}, u32[]{:S(2)}, u32[]{:S(2)}) collective-permute-start(bf16[8,256,128]{2,1,0:T(8,128)(2,1)S(1)} %get-tuple-element.46.own_ref), channel_id=1, source_target_pairs={{0,1},{1,0},{2,3},{3,2},{4,5},{5,4},{6,7},{7,6},{8,9},{9,8},{10,11... | collective-permute-start | bytes 1572872 | tf_op jit(solution)/shard_map/ppermute | solution.py:126
  39.5 13.1 %collective-permute-start.16 = (bf16[256,1024]{1,0:T(8,128)(2,1)S(1)}, bf16[256,1024]{1,0:T(8,128)(2,1)S(1)}, u32[]{:S(2)}, u32[]{:S(2)}) collective-permute-start(bf16[256,1024]{1,0:T(8,128)(2,1)S(1)} %copy-done.3), channel_id=1, source_target_pairs={{0,1},{1,0},{2,3},{3,2},{4,5},{5,4},{6,7},{7,6},{8,9},{9,8},{10,11... | collective-permute-start | bytes 1572872 | tf_op jit(solution)/shard_map/ppermute | solution.py:126
  49.1 13.1 %all-to-all-start = ((bf16[8,128,128]{2,1,0:T(8,128)(2,1)}), bf16[8,128,128]{2,1,0:T(8,128)(2,1)S(1)}, u32[]{:S(2)}, u32[]{:S(2)}) async-start(bf16[8,128,128]{2,1,0:T(8,128)(2,1)} %shard_map.97), calls=%async_computation | async-start | bytes 524288 | tf_op jit(solution)/shard_map/all_to_all | solution.py:450
  63.2 1.9 %collective-permute-start.17 = (bf16[256,256]{1,0:T(8,128)(2,1)S(1)}, bf16[256,256]{1,0:T(8,128)(2,1)S(1)}, u32[]{:S(2)}, u32[]{:S(2)}) collective-permute-start(bf16[256,256]{1,0:T(8,128)(2,1)S(1)} %get-tuple-element.50), channel_id=1, source_target_pairs={{0,1},{1,0},{2,3},{3,2},{4,5},{5,4},{6,7},{7,6},{8,9},{9,8},{10,11... | collective-permute-start | bytes 393224 | tf_op jit(solution)/shard_map/ppermute | solution.py:126
  63.3 6.4 %collective-permute-start.18 = (bf16[256,256]{1,0:T(8,128)(2,1)S(1)}, bf16[256,256]{1,0:T(8,128)(2,1)S(1)}, u32[]{:S(2)}, u32[]{:S(2)}) collective-permute-start(bf16[256,256]{1,0:T(8,128)(2,1)S(1)} %get-tuple-element.51), channel_id=1, source_target_pairs={{0,2},{1,3},{2,0},{3,1},{4,6},{5,7},{6,4},{7,5},{8,10},{9,11},{10,... | collective-permute-start | bytes 393224 | tf_op jit(solution)/shard_map/ppermute | solution.py:126
  63.9 7.7 %collective-permute-start.19 = (bf16[256,256]{1,0:T(8,128)(2,1)S(1)}, bf16[256,256]{1,0:T(8,128)(2,1)S(1)}, u32[]{:S(2)}, u32[]{:S(2)}) collective-permute-start(bf16[256,256]{1,0:T(8,128)(2,1)S(1)} %get-tuple-element.52), channel_id=1, source_target_pairs={{0,3},{1,2},{2,1},{3,0},{4,7},{5,6},{6,5},{7,4},{8,11},{9,10},{10,... | collective-permute-start | bytes 393224 | tf_op jit(solution)/shard_map/ppermute | solution.py:126

commit v4 on v3

--- a/solution.py
+++ b/solution.py
@@ -251,13 +251,37 @@
         out[...] = pack[m]
 
 
-def pack_kernel(pos_ref, *rest):
-    own_refs, kv_ref, qs_ref = rest[:8], rest[8], rest[9]
-    half = kv_ref.shape[1]
+def pack_kernel(*refs):
+    kv_ref = refs[-1]
+    for i, ref in enumerate(refs[:-1]):
+        kv_ref[i] = ref[0 : kv_ref.shape[1], :]
+
+
+def load_keys(pos_ref, valid_ref, kv_ref, kb, vb, side):
+    half = kb.shape[1]
+    lane = lane_iota((half, 128))
+    row = jnp.where(lane == HEAD_DIM, lax.broadcasted_iota(jnp.int32, (half, 128), 0), -1)
+    left = jnp.where(lane < HEAD_DIM, 1.0, 0.0).astype(BF16)
+    right = jnp.where(lane < HEAD_DIM, 0.0, 1.0).astype(BF16)
+    for i in range(kb.shape[0]):
+        part = 1 - i // 4
+        shard = 4 * jnp.bitwise_xor(side, part) + jnp.bitwise_xor(pos_ref[2], i % 4)
+        start = (2 * shard + part) * half
+        stretch = start // STRETCH
+        first_bad = jnp.maximum(valid_ref[stretch] - (start - stretch * STRETCH), 0)
+        bias = jnp.where(row >= first_bad, NEG, 0.0).astype(BF16)
+        kv = kv_ref[i]
+        kb[shard] = kv * left + bias
+        vb[shard] = kv * right + left
+
+
+def own_kernel(pos_ref, valid_ref, kv_ref, *rest):
+    own_refs, (kb, vb, qs_ref) = rest[:8], rest[8:]
+    load_keys(pos_ref, valid_ref, kv_ref, kb, vb, pos_ref[0])
+    half = kb.shape[1]
     lane = lane_iota((half // 2, 128))
     pad = jnp.where(lane == HEAD_DIM, 1.0, 0.0)
     for i, ref in enumerate(own_refs):
-        kv_ref[i] = ref[0:half, :]
         shard = 4 * jnp.bitwise_xor(pos_ref[0], 1 - i // 4) + jnp.bitwise_xor(pos_ref[2], i % 4)
         packed = ref[half:, :].astype(F32)
         rolled = pltpu.roll(packed, HEAD_DIM, 1)
@@ -265,37 +289,26 @@
         qs_ref[shard, half // 2 :] = jnp.where(lane < HEAD_DIM, rolled, pad).astype(BF16)
 
 
-def attend_kernel(pos_ref, valid_ref, own_ref, oth_ref, qs, o_ref, kb, vb, sc):
+def attend_kernel(pos_ref, valid_ref, oth_ref, k_own, v_own, qs, o_ref, k_oth, v_oth, sc):
     ranks = o_ref.shape[0]
     half = o_ref.shape[1] * 2
     halfrows = half // 2
-    core, low = pos_ref[0], pos_ref[2]
-    lane = lane_iota((half, 128))
-    row = lax.broadcasted_iota(jnp.int32, (half, 128), 0)
+    core = pos_ref[0]
     lane_h = lane_iota((halfrows, 128))
-    for i in range(8):
-        part = 1 - i // 4
-        for side, ref in ((core, own_ref), (1 - core, oth_ref)):
-            shard = 4 * jnp.bitwise_xor(side, part) + jnp.bitwise_xor(low, i % 4)
-            block = 2 * shard + part
-            start = block * half
-            stretch = start // STRETCH
-            ok = row + (start - stretch * STRETCH) < valid_ref[stretch]
-            bias = jnp.where(jnp.logical_and(lane == HEAD_DIM, jnp.logical_not(ok)), NEG, 0.0)
-            kv = ref[i].astype(F32)
-            kb[block] = jnp.where(lane < HEAD_DIM, kv, bias).astype(BF16)
-            vb[block] = jnp.where(lane < HEAD_DIM, 1.0, kv).astype(BF16)
-    qrow = lax.broadcasted_iota(jnp.int32, (half, half), 0)
-    kcol = lane_iota((half, half))
+    load_keys(pos_ref, valid_ref, oth_ref, k_oth, v_oth, 1 - core)
+    causal = lane_iota((half, half)) <= lax.broadcasted_iota(jnp.int32, (half, half), 0)
+    blocks = [(k_own, v_own), (k_oth, v_oth)]
 
     def scores(t):
-        part = jnp.bitwise_xor(core, t // 4)
+        ahead = jnp.where(jnp.bitwise_xor(core, t // 4) == 0, NEG, 0.0)
         q = qs[t]
         top = jnp.full((half, 128), NEG, F32)
         for b in range(2 * t + 2):
-            s = dot_nt(q, kb[b])
-            if b >= 2 * t:
-                s = jnp.where(kcol + (b - 2 * t) * half <= qrow + part * half, s, NEG)
+            s = dot_nt(q, blocks[b % 2][0][b // 2])
+            if b == 2 * t:
+                s = jnp.where(causal, s, NEG)
+            elif b == 2 * t + 1:
+                s = s + ahead
             sc[t % 2, b] = s
             for piece in range(half // 128):
                 top = jnp.maximum(top, s[:, piece * 128 : (piece + 1) * 128])
@@ -304,7 +317,7 @@
     def values(t, m):
         acc = jnp.zeros((half, 128), F32)
         for b in range(2 * t + 2):
-            acc += dot32(jnp.exp(sc[t % 2, b] - m).astype(BF16), vb[b])
+            acc += dot32(jnp.exp(sc[t % 2, b] - m).astype(BF16), blocks[b % 2][1][b // 2])
         out = acc / pltpu.roll(acc, HEAD_DIM, 1)
         left = pltpu.roll(out[:halfrows], HEAD_DIM, 1)
         o_ref[t] = jnp.where(lane_h < HEAD_DIM, left, out[halfrows:]).astype(BF16)
@@ -316,10 +329,8 @@
         values(t, tops[t])
 
 
-def out_kernel(pos_ref, att_ref, w0, w1, own_ref, *outs):
+def features(core, att_ref):
     heads, quarter, _ = att_ref.shape
-    cols = own_ref.shape[1]
-    core, ychip = pos_ref[0], pos_ref[1]
     lane = lane_iota((quarter, 128))
     feats = []
     for first in (core, 1 - core):
@@ -334,21 +345,41 @@
                 [jnp.concatenate(tops, axis=1), jnp.concatenate(bots, axis=1)], axis=0
             ).astype(BF16)
         )
-    for step, ref in enumerate((own_ref, *outs)):
-        group = jnp.bitwise_xor(2 * ychip + core, step)
-        lanes = pl.ds(pl.multiple_of(group * cols, cols), cols)
-        total = dot32(feats[0], w0[:, lanes]) + dot32(feats[1], w1[:, lanes])
-        ref[...] = total.astype(ref.dtype)
-
-
-def final_kernel(pos_ref, late_ref, early_ref, own_ref, beside_ref, across_ref, corner_ref, o_ref):
-    half = own_ref.shape[0]
-    first = jnp.bitwise_xor(pos_ref[0], pos_ref[3]) == 0
-    own = own_ref[...] + across_ref[...].astype(F32)
-    other = beside_ref[...].astype(F32) + corner_ref[...].astype(F32)
-    pick = jnp.broadcast_to(first, own.shape)
-    o_ref[0:half] = (late_ref[0:half].astype(F32) + jnp.where(pick, own, other)).astype(BF16)
-    o_ref[half:] = (early_ref[0:half].astype(F32) + jnp.where(pick, other, own)).astype(BF16)
+    return feats
+
+
+def partial_out(pos_ref, feats, w0, w1, step, cols):
+    group = jnp.bitwise_xor(2 * pos_ref[1] + pos_ref[0], step)
+    lanes = pl.ds(pl.multiple_of(group * cols, cols), cols)
+    return dot32(feats[0], w0[:, lanes]) + dot32(feats[1], w1[:, lanes])
+
+
+def far_kernel(pos_ref, att_ref, w0, w1, across_ref, corner_ref):
+    feats = features(pos_ref[0], att_ref)
+    for step, ref in ((2, across_ref), (3, corner_ref)):
+        ref[...] = partial_out(pos_ref, feats, w0, w1, step, ref.shape[1]).astype(BF16)
+
+
+def rows_of(pos_ref, half, other):
+    mine = jnp.bitwise_xor(jnp.bitwise_xor(pos_ref[0], pos_ref[3]), other)
+    return pl.ds(pl.multiple_of(mine * half, half), half)
+
+
+def near_kernel(pos_ref, att_ref, w0, w1, late_ref, early_ref, base_ref, beside_ref):
+    feats = features(pos_ref[0], att_ref)
+    half, cols = beside_ref.shape
+    beside_ref[...] = partial_out(pos_ref, feats, w0, w1, 1, cols).astype(BF16)
+    base_ref[0:half] = late_ref[0:half].astype(F32)
+    base_ref[half:] = early_ref[0:half].astype(F32)
+    base_ref[rows_of(pos_ref, half, 0)] += partial_out(pos_ref, feats, w0, w1, 0, cols)
+
+
+def final_kernel(pos_ref, base_ref, beside_ref, across_ref, corner_ref, o_ref):
+    half = beside_ref.shape[0]
+    mine, other = rows_of(pos_ref, half, 0), rows_of(pos_ref, half, 1)
+    o_ref[mine] = (base_ref[mine] + across_ref[...].astype(F32)).astype(BF16)
+    rest = beside_ref[...].astype(F32) + corner_ref[...].astype(F32)
+    o_ref[other] = (base_ref[other] + rest).astype(BF16)
 
 
 def call(kernel, outs, scalars, args, *, us, vmem=16, scratch=(), space=pltpu.VMEM):
@@ -426,42 +457,39 @@
     )
     sends += list(project_half(late, sends[0]))
     own = [spread(value, i % 4, 1 - i // 4) for i, value in enumerate(sends)]
-    kv, qs = call(
-        pack_kernel,
-        [((8, half, 128), BF16), ((8, half, 128), BF16)],
-        1,
-        (pos, *own),
-        us=0.5,
-    )
+    kv = call(pack_kernel, [((8, half, 128), BF16)], 0, own, us=0.4)
     wo1 = swap(lax.optimization_barrier((w_out, sends[0]))[0], 1)
+    kv_oth = swap(kv, 1)
+    k_own, v_own, qs = call(
+        own_kernel, [((8, half, 128), BF16)] * 3, 2, (pos, valid_count, kv, *own), us=0.8
+    )
     attended = call(
         attend_kernel,
         [((8, half // 2, 2 * HEAD_DIM), BF16)],
         2,
-        (pos, valid_count, kv, swap(kv, 1), qs),
+        (pos, valid_count, kv_oth, k_own, v_own, qs),
         us=8.0,
         vmem=24,
         scratch=[
-            pltpu.VMEM((16, half, 128), BF16),
-            pltpu.VMEM((16, half, 128), BF16),
+            pltpu.VMEM((8, half, 128), BF16),
+            pltpu.VMEM((8, half, 128), BF16),
             pltpu.VMEM((2, 16, half, half), F32),
         ],
     )
     back = lax.all_to_all(attended, "tm", 0, 0)
-    own, beside, across, corner = call(
-        out_kernel,
-        [((half, cols), F32)] + [((half, cols), BF16)] * 3,
+    across, corner = call(
+        far_kernel, [((half, cols), BF16)] * 2, 1, (pos, back, w_out, wo1), us=0.6
+    )
+    across, corner = swap(across, 2), swap(corner, 3)
+    base, beside = call(
+        near_kernel,
+        [((tok, cols), F32), ((half, cols), BF16)],
         1,
-        (pos, back, w_out, wo1),
+        (pos, back, w_out, wo1, late, early),
         us=1.0,
     )
-    return call(
-        final_kernel,
-        [((tok, cols), BF16)],
-        1,
-        (pos, late, early, own, swap(beside, 1), swap(across, 2), swap(corner, 3)),
-        us=0.5,
-    )
+    args = (pos, base, swap(beside, 1), across, corner)
+    return call(final_kernel, [((tok, cols), BF16)], 1, args, us=0.5)
 
 
 def solution(mesh):

time: 73.3 us -> 71 us (0.969)
  waiting for transfers between devices: 22.6 us -> 18.2 us
  starting transfers between devices: 31.1 us -> 32.4 us
    ppermute x11, waiting for transfers between devices: 8.34 us -> 5.03 us  [swap(): lax.ppermute(value, 'head', [(i, i ^ bit) for i in range(lax.axis_size('h...]
    all_to_all x1, starting transfers between devices: 3.45 us -> 4.61 us  [on_device(): back = lax.all_to_all(attended, 'tm', 0, 0)]
    pallas_call x9 -> x11, Pallas kernels: 16.5 us -> 16.7 us  [call(): pl.pallas_call(kernel, out_shape=outs, in_specs=[pl.BlockSpec(memory_spac...]
  transfers between devices with their start and end apart: 21 -> 21, of which waited for: 9 -> 9; matrix products, arithmetic and copies ran while one was open for 0% -> 0% of each run, Pallas kernels for 15% -> 17%
where the time goes in v4:
time: 71 us; the launch traced here: 70.1 us
  starting transfers between devices  32.4 us (46%)
  waiting for transfers between devices  18.2 us (26%)
  Pallas kernels  16.7 us (24%)
  local copies, waits for them, and re-layouts  2.51 us (4%)
    pallas_call x11, Pallas kernels, call(): pl.pallas_call(kernel, out_shape=outs, in_specs=[pl.BlockSpec(memory_spac...  16.7 us
    ppermute x11, starting transfers between devices, swap(): lax.ppermute(value, 'head', [(i, i ^ bit) for i in range(lax.axis_size('h...  14 us
    ppermute x8, starting transfers between devices, spread(): return lax.ppermute(value, ('tm', 'head'), pairs)  10.4 us
    all_to_all x1, waiting for transfers between devices, on_device(): back = lax.all_to_all(attended, 'tm', 0, 0)  9.21 us
    ppermute x11, waiting for transfers between devices, swap(): lax.ppermute(value, 'head', [(i, i ^ bit) for i in range(lax.axis_size('h...  5.03 us
    all_to_all x1, starting transfers between devices, on_device(): back = lax.all_to_all(attended, 'tm', 0, 0)  4.61 us
    ppermute x8, waiting for transfers between devices, spread(): return lax.ppermute(value, ('tm', 'head'), pairs)  3.95 us
    ppermute x1, starting transfers between devices, from_behind(): lax.ppermute(value, axis, [(source, source + steps) for source in range(f...  3.38 us
  transfers between devices with their start and end apart: 21, of which 9 were waited for; matrix products, arithmetic and copies ran while one was open for 0% of the time, Pallas kernels for 17%

profile of v4, /device:TPU:0, one launch (start us, length us, event | category | flops | bytes accessed | tf_op | source)
XLA Modules:
  0.0 70.1 jit_solution(16736778511415779998)
XLA Ops:
  0.0 2.4 %shard_map.91 = (bf16[264,256]{1,0:T(8,128)(2,1)}, bf16[264,256]{1,0:T(8,128)(2,1)}, bf16[2,256,256]{2,1,0:T(8,128)(2,1)}, f32[16,256]{1,0:T(8,128)}, bf16[8,256]{1,0:T(8,128)(2,1)}) custom-call(bf16[512,256]{1,0:T(8,128)(2,1)} %x_hbm.1, bf16[4,64,192]{2,1,0:T(8,128)(2,1)} %bitcast.7, f32[1,256]{1,0:T(1,128)} %bitcast.8, bf16[2,128]{1,0:T(2,128)(2,1)} %bitcast.9), custom_call_target="tpu_custom_call" | custom-call | flops 2000000000 | bytes 7200000 | tf_op jit(solution)/shard_map/pallas_call | solution.py:388
  2.4 3.0 %collective-permute-start.1 = (bf16[264,256]{1,0:T(8,128)(2,1)}, bf16[264,256]{1,0:T(8,128)(2,1)S(1)}, u32[]{:S(2)}, u32[]{:S(2)}) collective-permute-start(bf16[264,256]{1,0:T(8,128)(2,1)} %get-tuple-element.30.a_ref.early_ref), channel_id=1, source_target_pairs={{0,2},{1,3},{2,0},{3,1},{4,6},{5,7},{6,4},{7,5},{8,10},{9,11},{10,... | collective-permute-start | bytes 405512 | tf_op jit(solution)/shard_map/ppermute | solution.py:126
  5.4 0.0 collective-permute-start
  5.4 3.4 %collective-permute-start.7 = (bf16[8,256]{1,0:T(8,128)(2,1)}, bf16[8,256]{1,0:T(8,128)(2,1)S(1)}, u32[]{:S(2)}, u32[]{:S(2)}) collective-permute-start(bf16[8,256]{1,0:T(8,128)(2,1)} %get-tuple-element.35), channel_id=1, source_target_pairs={{0,4},{4,8},{8,12},{12,16},{16,20},{20,24},{24,28},{1,5},{5,9},{9,... | collective-permute-start | bytes 12296 | tf_op jit(solution)/shard_map/ppermute | solution.py:28
  8.8 0.1 pad_add_fusion.pos_ref
  8.9 0.6 copy-done.8
  9.5 0.9 %copy-done.6 = bf16[2,256,256]{2,1,0:T(8,128)(2,1)S(1)} copy-done((bf16[2,256,256]{2,1,0:T(8,128)(2,1)S(1)}, bf16[2,256,256]{2,1,0:T(8,128)(2,1)}, u32[]{:S(2)}) %copy-start.6) | copy-done | bytes 262168
  10.5 0.9 %copy-done.7 = bf16[264,256]{1,0:T(8,128)(2,1)S(1)} copy-done((bf16[264,256]{1,0:T(8,128)(2,1)S(1)}, bf16[264,256]{1,0:T(8,128)(2,1)}, u32[]{:S(2)}) %copy-start.7) | copy-done | bytes 135192
  11.4 0.0 collective-permute-done.1.y_ref
  11.4 0.3 collective-permute-start.2
  11.7 0.0 collective-permute-done.7.halo_ref
  11.7 0.2 shard_map.94.a_ref.late_ref
  11.9 0.5 collective-permute-start.10
  12.4 1.5 %collective-permute-start.9 = (bf16[264,256]{1,0:T(8,128)(2,1)S(1)}, bf16[264,256]{1,0:T(8,128)(2,1)S(1)}, u32[]{:S(2)}, u32[]{:S(2)}) collective-permute-start(bf16[264,256]{1,0:T(8,128)(2,1)S(1)} %shard_map.94.a_ref.late_ref), channel_id=1, source_target_pairs={{0,2},{1,3},{2,0},{3,1},{4,6},{5,7},{6,4},{7,5},{8,10},{9,11},{10,... | collective-permute-start | bytes 405512 | tf_op jit(solution)/shard_map/ppermute | solution.py:126
  13.9 0.0 collective-permute-done.b_ref
  13.9 0.0 collective-permute-done.2.z_ref
  14.0 1.4 %shard_map.92 = (bf16[384,128]{1,0:T(8,128)(2,1)S(1)}, bf16[384,128]{1,0:T(8,128)(2,1)S(1)}, bf16[384,128]{1,0:T(8,128)(2,1)S(1)}, bf16[384,128]{1,0:T(8,128)(2,1)S(1)}) custom-call(s32[4]{0:T(128)S(1)} %pad_add_fusion.pos_ref, bf16[264,256]{1,0:T(8,128)(2,1)S(1)} %copy-done.4, bf16[264,256]{1,0:T(8,128)(2,1)S(1)} %collective-permute-done.b_ref, ...), custom_call_target="tpu_custom_call" | custom-call | flops 1000000000 | bytes 3600000 | tf_op jit(solution)/shard_map/pallas_call | solution.py:388
  15.3 0.1 collective-permute-start.8
  15.4 0.5 collective-permute-start.3
  15.9 3.5 %collective-permute-start.4 = (bf16[384,128]{1,0:T(8,128)(2,1)S(1)}, bf16[384,128]{1,0:T(8,128)(2,1)S(1)}, u32[]{:S(2)}, u32[]{:S(2)}) collective-permute-start(bf16[384,128]{1,0:T(8,128)(2,1)S(1)} %get-tuple-element.32), channel_id=1, source_target_pairs={{0,5},{1,21},{2,7},{3,23},{4,1},{5,17},{6,3},{7,19},{8,13},{9,29},... | collective-permute-start | bytes 294920 | tf_op jit(solution)/shard_map/ppermute | solution.py:136
  19.4 0.0 collective-permute-done.10.z_ref
  19.4 0.3 collective-permute-start.5
  19.7 1.1 %collective-permute-done.9.y_ref = bf16[264,256]{1,0:T(8,128)(2,1)S(1)} collective-permute-done((bf16[264,256]{1,0:T(8,128)(2,1)S(1)}, bf16[264,256]{1,0:T(8,128)(2,1)S(1)}, u32[]{:S(2)}, u32[]{:S(2)}) %collective-permute-start.9) | collective-permute-done | bytes 135200 | tf_op jit(solution)/shard_map/ppermute | solution.py:126
  20.8 1.9 %collective-permute-start.6 = (bf16[384,128]{1,0:T(8,128)(2,1)S(1)}, bf16[384,128]{1,0:T(8,128)(2,1)S(1)}, u32[]{:S(2)}, u32[]{:S(2)}) collective-permute-start(bf16[384,128]{1,0:T(8,128)(2,1)S(1)} %get-tuple-element.34), channel_id=1, source_target_pairs={{0,13},{1,29},{2,15},{3,31},{4,9},{5,25},{6,11},{7,27},{8,5},{9,21... | collective-permute-start | bytes 294920 | tf_op jit(solution)/shard_map/ppermute | solution.py:136
  22.7 0.0 collective-permute-done.8.b_ref
  22.7 1.4 %shard_map.95 = (bf16[384,128]{1,0:T(8,128)(2,1)S(1)}, bf16[384,128]{1,0:T(8,128)(2,1)S(1)}, bf16[384,128]{1,0:T(8,128)(2,1)S(1)}, bf16[384,128]{1,0:T(8,128)(2,1)S(1)}) custom-call(s32[4]{0:T(128)S(1)} %pad_add_fusion.pos_ref, bf16[264,256]{1,0:T(8,128)(2,1)S(1)} %shard_map.94.a_ref.late_ref, bf16[264,256]{1,0:T(8,128)(2,1)S(1)} %collective-permute-done.8.b_ref, ...), custom_call_target="tpu_custom_call" | custom-call | flops 1000000000 | bytes 3600000 | tf_op jit(solution)/shard_map/pallas_call | solution.py:388
  24.1 0.7 collective-permute-start.11
  24.7 1.0 %collective-permute-start.12 = (bf16[384,128]{1,0:T(8,128)(2,1)S(1)}, bf16[384,128]{1,0:T(8,128)(2,1)S(1)}, u32[]{:S(2)}, u32[]{:S(2)}) collective-permute-start(bf16[384,128]{1,0:T(8,128)(2,1)S(1)} %get-tuple-element.44), channel_id=1, source_target_pairs={{0,4},{1,20},{2,6},{3,22},{4,0},{5,16},{6,2},{7,18},{8,12},{9,28},... | collective-permute-start | bytes 294920 | tf_op jit(solution)/shard_map/ppermute | solution.py:136
  25.8 0.9 %collective-permute-start.13 = (bf16[384,128]{1,0:T(8,128)(2,1)S(1)}, bf16[384,128]{1,0:T(8,128)(2,1)S(1)}, u32[]{:S(2)}, u32[]{:S(2)}) collective-permute-start(bf16[384,128]{1,0:T(8,128)(2,1)S(1)} %get-tuple-element.45), channel_id=1, source_target_pairs={{0,8},{1,24},{2,10},{3,26},{4,12},{5,28},{6,14},{7,30},{8,0},{9,16... | collective-permute-start | bytes 294920 | tf_op jit(solution)/shard_map/ppermute | solution.py:136
  26.7 1.6 %collective-permute-start.14 = (bf16[384,128]{1,0:T(8,128)(2,1)S(1)}, bf16[384,128]{1,0:T(8,128)(2,1)S(1)}, u32[]{:S(2)}, u32[]{:S(2)}) collective-permute-start(bf16[384,128]{1,0:T(8,128)(2,1)S(1)} %get-tuple-element.46), channel_id=1, source_target_pairs={{0,12},{1,28},{2,14},{3,30},{4,8},{5,24},{6,10},{7,26},{8,4},{9,20... | collective-permute-start | bytes 294920 | tf_op jit(solution)/shard_map/ppermute | solution.py:136
  28.3 0.9 %collective-permute-done.6.refs_3_.rest_3_ = bf16[384,128]{1,0:T(8,128)(2,1)S(1)} collective-permute-done((bf16[384,128]{1,0:T(8,128)(2,1)S(1)}, bf16[384,128]{1,0:T(8,128)(2,1)S(1)}, u32[]{:S(2)}, u32[]{:S(2)}) %collective-permute-start.6) | collective-permute-done | bytes 98336 | tf_op jit(solution)/shard_map/ppermute | solution.py:136
  29.2 0.6 collective-permute-done.12.refs_5_.rest_5_
  29.8 0.6 collective-permute-done.13.refs_6_.rest_6_
  30.4 1.9 %collective-permute-done.14.refs_7_.rest_7_ = bf16[384,128]{1,0:T(8,128)(2,1)S(1)} collective-permute-done((bf16[384,128]{1,0:T(8,128)(2,1)S(1)}, bf16[384,128]{1,0:T(8,128)(2,1)S(1)}, u32[]{:S(2)}, u32[]{:S(2)}) %collective-permute-start.14) | collective-permute-done | bytes 98336 | tf_op jit(solution)/shard_map/ppermute | solution.py:136
  32.3 6.3 %collective-permute-start.15 = (bf16[8,256,128]{2,1,0:T(8,128)(2,1)S(1)}, bf16[8,256,128]{2,1,0:T(8,128)(2,1)S(1)}, u32[]{:S(2)}, u32[]{:S(2)}) collective-permute-start(bf16[8,256,128]{2,1,0:T(8,128)(2,1)S(1)} %shard_map.96.kv_ref), channel_id=1, source_target_pairs={{0,1},{1,0},{2,3},{3,2},{4,5},{5,4},{6,7},{7,6},{8,9},{9,8},{10,11... | collective-permute-start | bytes 1572872 | tf_op jit(solution)/shard_map/ppermute | solution.py:126
  38.6 0.1 collective-permute-start.16
  38.6 1.0 %shard_map.97 = (bf16[8,256,128]{2,1,0:T(8,128)(2,1)S(1)}, bf16[8,256,128]{2,1,0:T(8,128)(2,1)S(1)}, bf16[8,256,128]{2,1,0:T(8,128)(2,1)S(1)}) custom-call(s32[4]{0:T(128)S(1)} %pad_add_fusion.pos_ref, s32[4]{0:T(128)S(1)} %copy-done.5, bf16[8,256,128]{2,1,0:T(8,128)(2,1)S(1)} %shard_map.96.kv_ref, ...), custom_call_target="tpu_custom_call" | custom-call | flops 800000000 | bytes 2880000 | tf_op jit(solution)/shard_map/pallas_call | solution.py:388
  39.6 0.5 collective-permute-done.15.oth_ref
  40.1 7.3 %shard_map.98 = bf16[8,128,128]{2,1,0:T(8,128)(2,1)} custom-call(s32[4]{0:T(128)S(1)} %pad_add_fusion.pos_ref, s32[4]{0:T(128)S(1)} %copy-done.5, bf16[8,256,128]{2,1,0:T(8,128)(2,1)S(1)} %collective-permute-done.15.oth_ref, bf16[8,256,128]{2,1,0:T(8,128)(2,1)S(1)} %get-tuple-element.47.k_own, bf16[8,256,128]{2,1,0:T(8,128)(2,1)S(1)} %get-tuple-element.48.v_own, ...), custom_call_target="tpu_custom_call" | custom-call | flops 8000000000 | bytes 28800000 | tf_op jit(solution)/shard_map/pallas_call | solution.py:388
  47.4 4.6 %all-to-all-start = ((bf16[8,128,128]{2,1,0:T(8,128)(2,1)}), bf16[8,128,128]{2,1,0:T(8,128)(2,1)S(1)}, u32[]{:S(2)}, u32[]{:S(2)}) async-start(bf16[8,128,128]{2,1,0:T(8,128)(2,1)} %shard_map.98), calls=%async_computation | async-start | bytes 524288 | tf_op jit(solution)/shard_map/all_to_all | solution.py:479
  52.0 9.2 %all-to-all-done.att_ref = bf16[8,128,128]{2,1,0:T(8,128)(2,1)S(1)} async-done(((bf16[8,128,128]{2,1,0:T(8,128)(2,1)}), bf16[8,128,128]{2,1,0:T(8,128)(2,1)S(1)}, u32[]{:S(2)}, u32[]{:S(2)}) %all-to-all-start) | async-done | bytes 262176 | tf_op jit(solution)/shard_map/all_to_all | solution.py:479
  61.2 0.9 %shard_map.100 = (bf16[256,256]{1,0:T(8,128)(2,1)S(1)}, bf16[256,256]{1,0:T(8,128)(2,1)S(1)}) custom-call(s32[4]{0:T(128)S(1)} %pad_add_fusion.pos_ref, bf16[8,128,128]{2,1,0:T(8,128)(2,1)S(1)} %all-to-all-done.att_ref, bf16[256,1024]{1,0:T(8,128)(2,1)S(1)} %copy-done.3, bf16[256,1024]{1,0:T(8,128)(2,1)S(1)} %collective-permute-done.16.w1), custom_call_target="tpu_custom_call" | custom-call | flops 600000000 | bytes 2160000 | tf_op jit(solution)/shard_map/pallas_call | solution.py:388
  62.1 0.8 %collective-permute-start.18 = (bf16[256,256]{1,0:T(8,128)(2,1)S(1)}, bf16[256,256]{1,0:T(8,128)(2,1)S(1)}, u32[]{:S(2)}, u32[]{:S(2)}) collective-permute-start(bf16[256,256]{1,0:T(8,128)(2,1)S(1)} %get-tuple-element.53), channel_id=1, source_target_pairs={{0,2},{1,3},{2,0},{3,1},{4,6},{5,7},{6,4},{7,5},{8,10},{9,11},{10,... | collective-permute-start | bytes 393224 | tf_op jit(solution)/shard_map/ppermute | solution.py:126
  63.0 0.9 %shard_map.99 = (f32[512,256]{1,0:T(8,128)S(1)}, bf16[256,256]{1,0:T(8,128)(2,1)S(1)}) custom-call(s32[4]{0:T(128)S(1)} %pad_add_fusion.pos_ref, bf16[8,128,128]{2,1,0:T(8,128)(2,1)S(1)} %all-to-all-done.att_ref, bf16[256,1024]{1,0:T(8,128)(2,1)S(1)} %copy-done.3, bf16[256,1024]{1,0:T(8,128)(2,1)S(1)} %collective-permute-done.16.w1, ...), custom_call_target="tpu_custom_call" | custom-call | flops 1000000000 | bytes 3600000 | tf_op jit(solution)/shard_map/pallas_call | solution.py:388
  63.9 1.5 %collective-permute-start.17 = (bf16[256,256]{1,0:T(8,128)(2,1)S(1)}, bf16[256,256]{1,0:T(8,128)(2,1)S(1)}, u32[]{:S(2)}, u32[]{:S(2)}) collective-permute-start(bf16[256,256]{1,0:T(8,128)(2,1)S(1)} %get-tuple-element.52), channel_id=1, source_target_pairs={{0,1},{1,0},{2,3},{3,2},{4,5},{5,4},{6,7},{7,6},{8,9},{9,8},{10,11... | collective-permute-start | bytes 393224 | tf_op jit(solution)/shard_map/ppermute | solution.py:126
  65.3 3.1 %collective-permute-done.18.across_ref = bf16[256,256]{1,0:T(8,128)(2,1)S(1)} collective-permute-done((bf16[256,256]{1,0:T(8,128)(2,1)S(1)}, bf16[256,256]{1,0:T(8,128)(2,1)S(1)}, u32[]{:S(2)}, u32[]{:S(2)}) %collective-permute-start.18) | collective-permute-done | bytes 131104 | tf_op jit(solution)/shard_map/ppermute | solution.py:126
  68.4 0.4 collective-permute-done.19.corner_ref
  68.7 1.3 %shard_map.101 = bf16[512,256]{1,0:T(8,128)(2,1)} custom-call(s32[4]{0:T(128)S(1)} %pad_add_fusion.pos_ref, f32[512,256]{1,0:T(8,128)S(1)} %get-tuple-element.51.base_ref, bf16[256,256]{1,0:T(8,128)(2,1)S(1)} %collective-permute-done.17.beside_ref, bf16[256,256]{1,0:T(8,128)(2,1)S(1)} %collective-permute-done.18.across_ref, ...), custom_call_target="tpu_custom_call" | custom-call | flops 500000000 | bytes 1800000 | tf_op jit(solution)/shard_map/pallas_call | solution.py:388
  (24 shorter events, 0.1 us)
Async XLA Ops:
  2.4 9.0 %collective-permute-start.1 = (bf16[264,256]{1,0:T(8,128)(2,1)}, bf16[264,256]{1,0:T(8,128)(2,1)S(1)}, u32[]{:S(2)}, u32[]{:S(2)}) collective-permute-start(bf16[264,256]{1,0:T(8,128)(2,1)} %get-tuple-element.30.a_ref.early_ref), channel_id=1, source_target_pairs={{0,2},{1,3},{2,0},{3,1},{4,6},{5,7},{6,4},{7,5},{8,10},{9,11},{10,... | collective-permute-start | bytes 405512 | tf_op jit(solution)/shard_map/ppermute | solution.py:126
  5.4 8.5 %collective-permute-start = (bf16[264,256]{1,0:T(8,128)(2,1)}, bf16[264,256]{1,0:T(8,128)(2,1)S(1)}, u32[]{:S(2)}, u32[]{:S(2)}) collective-permute-start(bf16[264,256]{1,0:T(8,128)(2,1)} %get-tuple-element.30.a_ref.early_ref), channel_id=1, source_target_pairs={{0,1},{1,0},{2,3},{3,2},{4,5},{5,4},{6,7},{7,6},{8,9},{9,8},{10,11... | collective-permute-start | bytes 405512 | tf_op jit(solution)/shard_map/ppermute | solution.py:126
  5.4 6.3 %collective-permute-start.7 = (bf16[8,256]{1,0:T(8,128)(2,1)}, bf16[8,256]{1,0:T(8,128)(2,1)S(1)}, u32[]{:S(2)}, u32[]{:S(2)}) collective-permute-start(bf16[8,256]{1,0:T(8,128)(2,1)} %get-tuple-element.35), channel_id=1, source_target_pairs={{0,4},{4,8},{8,12},{12,16},{16,20},{20,24},{24,28},{1,5},{5,9},{9,... | collective-permute-start | bytes 12296 | tf_op jit(solution)/shard_map/ppermute | solution.py:28
  8.8 0.7 %copy-start.8 = (f32[16,256]{1,0:T(8,128)S(1)}, f32[16,256]{1,0:T(8,128)}, u32[]{:S(2)}) copy-start(f32[16,256]{1,0:T(8,128)} %get-tuple-element.36.refs_0_) | copy-start | bytes 49156
  9.5 0.9 %copy-start.6 = (bf16[2,256,256]{2,1,0:T(8,128)(2,1)S(1)}, bf16[2,256,256]{2,1,0:T(8,128)(2,1)}, u32[]{:S(2)}) copy-start(bf16[2,256,256]{2,1,0:T(8,128)(2,1)} %get-tuple-element.37.refs_1_) | copy-start | bytes 786436
  10.5 0.9 %copy-start.7 = (bf16[264,256]{1,0:T(8,128)(2,1)S(1)}, bf16[264,256]{1,0:T(8,128)(2,1)}, u32[]{:S(2)}) copy-start(bf16[264,256]{1,0:T(8,128)(2,1)} %get-tuple-element.38.refs_2_) | copy-start | bytes 405508
  11.4 2.5 %collective-permute-start.2 = (bf16[264,256]{1,0:T(8,128)(2,1)S(1)}, bf16[264,256]{1,0:T(8,128)(2,1)S(1)}, u32[]{:S(2)}, u32[]{:S(2)}) collective-permute-start(bf16[264,256]{1,0:T(8,128)(2,1)S(1)} %collective-permute-done.1.y_ref), channel_id=1, source_target_pairs={{0,1},{1,0},{2,3},{3,2},{4,5},{5,4},{6,7},{7,6},{8,9},{9,8},{10,11... | collective-permute-start | bytes 405512 | tf_op jit(solution)/shard_map/ppermute | solution.py:126
  11.7 2.2 %copy-start = (bf16[1024,256]{1,0:T(8,128)(2,1)S(1)}, bf16[1024,256]{1,0:T(8,128)(2,1)}, u32[]{:S(2)}) copy-start(bf16[1024,256]{1,0:T(8,128)(2,1)} %wq.3) | copy-start | bytes 1572868
  11.7 2.2 %copy-start.1 = (bf16[1024,256]{1,0:T(8,128)(2,1)S(1)}, bf16[1024,256]{1,0:T(8,128)(2,1)}, u32[]{:S(2)}) copy-start(bf16[1024,256]{1,0:T(8,128)(2,1)} %wk.3) | copy-start | bytes 1572868
  11.7 2.2 %copy-start.2 = (bf16[1024,256]{1,0:T(8,128)(2,1)S(1)}, bf16[1024,256]{1,0:T(8,128)(2,1)}, u32[]{:S(2)}) copy-start(bf16[1024,256]{1,0:T(8,128)(2,1)} %wv.3) | copy-start | bytes 1572868
  11.7 2.2 %copy-start.4 = (bf16[264,256]{1,0:T(8,128)(2,1)S(1)}, bf16[264,256]{1,0:T(8,128)(2,1)}, u32[]{:S(2)}) copy-start(bf16[264,256]{1,0:T(8,128)(2,1)} %get-tuple-element.30.a_ref.early_ref) | copy-start | bytes 405508
  11.9 7.4 %collective-permute-start.10 = (bf16[264,256]{1,0:T(8,128)(2,1)S(1)}, bf16[264,256]{1,0:T(8,128)(2,1)S(1)}, u32[]{:S(2)}, u32[]{:S(2)}) collective-permute-start(bf16[264,256]{1,0:T(8,128)(2,1)S(1)} %shard_map.94.a_ref.late_ref), channel_id=1, source_target_pairs={{0,3},{1,2},{2,1},{3,0},{4,7},{5,6},{6,5},{7,4},{8,11},{9,10},{10,... | collective-permute-start | bytes 405512 | tf_op jit(solution)/shard_map/ppermute | solution.py:126
  12.4 8.4 %collective-permute-start.9 = (bf16[264,256]{1,0:T(8,128)(2,1)S(1)}, bf16[264,256]{1,0:T(8,128)(2,1)S(1)}, u32[]{:S(2)}, u32[]{:S(2)}) collective-permute-start(bf16[264,256]{1,0:T(8,128)(2,1)S(1)} %shard_map.94.a_ref.late_ref), channel_id=1, source_target_pairs={{0,2},{1,3},{2,0},{3,1},{4,6},{5,7},{6,4},{7,5},{8,10},{9,11},{10,... | collective-permute-start | bytes 405512 | tf_op jit(solution)/shard_map/ppermute | solution.py:126
  15.3 7.4 %collective-permute-start.8 = (bf16[264,256]{1,0:T(8,128)(2,1)S(1)}, bf16[264,256]{1,0:T(8,128)(2,1)S(1)}, u32[]{:S(2)}, u32[]{:S(2)}) collective-permute-start(bf16[264,256]{1,0:T(8,128)(2,1)S(1)} %shard_map.94.a_ref.late_ref), channel_id=1, source_target_pairs={{0,1},{1,0},{2,3},{3,2},{4,5},{5,4},{6,7},{7,6},{8,9},{9,8},{10,11... | collective-permute-start | bytes 405512 | tf_op jit(solution)/shard_map/ppermute | solution.py:126
  15.4 9.3 %collective-permute-start.3 = (bf16[384,128]{1,0:T(8,128)(2,1)S(1)}, bf16[384,128]{1,0:T(8,128)(2,1)S(1)}, u32[]{:S(2)}, u32[]{:S(2)}) collective-permute-start(bf16[384,128]{1,0:T(8,128)(2,1)S(1)} %get-tuple-element.31), channel_id=1, source_target_pairs={{0,1},{1,17},{2,3},{3,19},{4,5},{5,21},{6,7},{7,23},{8,9},{9,25},{... | collective-permute-start | bytes 294920 | tf_op jit(solution)/shard_map/ppermute | solution.py:136
  15.9 9.9 %collective-permute-start.4 = (bf16[384,128]{1,0:T(8,128)(2,1)S(1)}, bf16[384,128]{1,0:T(8,128)(2,1)S(1)}, u32[]{:S(2)}, u32[]{:S(2)}) collective-permute-start(bf16[384,128]{1,0:T(8,128)(2,1)S(1)} %get-tuple-element.32), channel_id=1, source_target_pairs={{0,5},{1,21},{2,7},{3,23},{4,1},{5,17},{6,3},{7,19},{8,13},{9,29},... | collective-permute-start | bytes 294920 | tf_op jit(solution)/shard_map/ppermute | solution.py:136
  19.4 7.4 %collective-permute-start.5 = (bf16[384,128]{1,0:T(8,128)(2,1)S(1)}, bf16[384,128]{1,0:T(8,128)(2,1)S(1)}, u32[]{:S(2)}, u32[]{:S(2)}) collective-permute-start(bf16[384,128]{1,0:T(8,128)(2,1)S(1)} %get-tuple-element.33), channel_id=1, source_target_pairs={{0,9},{1,25},{2,11},{3,27},{4,13},{5,29},{6,15},{7,31},{8,1},{9,17... | collective-permute-start | bytes 294920 | tf_op jit(solution)/shard_map/ppermute | solution.py:136
  20.8 8.4 %collective-permute-start.6 = (bf16[384,128]{1,0:T(8,128)(2,1)S(1)}, bf16[384,128]{1,0:T(8,128)(2,1)S(1)}, u32[]{:S(2)}, u32[]{:S(2)}) collective-permute-start(bf16[384,128]{1,0:T(8,128)(2,1)S(1)} %get-tuple-element.34), channel_id=1, source_target_pairs={{0,13},{1,29},{2,15},{3,31},{4,9},{5,25},{6,11},{7,27},{8,5},{9,21... | collective-permute-start | bytes 294920 | tf_op jit(solution)/shard_map/ppermute | solution.py:136
  24.1 5.1 %collective-permute-start.11 = (bf16[384,128]{1,0:T(8,128)(2,1)S(1)}, bf16[384,128]{1,0:T(8,128)(2,1)S(1)}, u32[]{:S(2)}, u32[]{:S(2)}) collective-permute-start(bf16[384,128]{1,0:T(8,128)(2,1)S(1)} %get-tuple-element.43), channel_id=1, source_target_pairs={{0,0},{1,16},{2,2},{3,18},{4,4},{5,20},{6,6},{7,22},{8,8},{9,24},{... | collective-permute-start | bytes 294920 | tf_op jit(solution)/shard_map/ppermute | solution.py:136
  24.7 5.1 %collective-permute-start.12 = (bf16[384,128]{1,0:T(8,128)(2,1)S(1)}, bf16[384,128]{1,0:T(8,128)(2,1)S(1)}, u32[]{:S(2)}, u32[]{:S(2)}) collective-permute-start(bf16[384,128]{1,0:T(8,128)(2,1)S(1)} %get-tuple-element.44), channel_id=1, source_target_pairs={{0,4},{1,20},{2,6},{3,22},{4,0},{5,16},{6,2},{7,18},{8,12},{9,28},... | collective-permute-start | bytes 294920 | tf_op jit(solution)/shard_map/ppermute | solution.py:136
  25.8 4.6 %collective-permute-start.13 = (bf16[384,128]{1,0:T(8,128)(2,1)S(1)}, bf16[384,128]{1,0:T(8,128)(2,1)S(1)}, u32[]{:S(2)}, u32[]{:S(2)}) collective-permute-start(bf16[384,128]{1,0:T(8,128)(2,1)S(1)} %get-tuple-element.45), channel_id=1, source_target_pairs={{0,8},{1,24},{2,10},{3,26},{4,12},{5,28},{6,14},{7,30},{8,0},{9,16... | collective-permute-start | bytes 294920 | tf_op jit(solution)/shard_map/ppermute | solution.py:136
  26.7 11.8 %copy-start.3 = (bf16[256,1024]{1,0:T(8,128)(2,1)S(1)}, bf16[256,1024]{1,0:T(8,128)(2,1)}, u32[]{:S(2)}) copy-start(bf16[256,1024]{1,0:T(8,128)(2,1)} %w0.3) | copy-start | bytes 1572868
  26.7 11.9 %copy-start.5 = (s32[4]{0:T(128)S(1)}, s32[4]{0:T(128)}, u32[]{:S(2)}) copy-start(s32[4]{0:T(128)} %valid_ref.3) | copy-start | bytes 52
  26.7 5.5 %collective-permute-start.14 = (bf16[384,128]{1,0:T(8,128)(2,1)S(1)}, bf16[384,128]{1,0:T(8,128)(2,1)S(1)}, u32[]{:S(2)}, u32[]{:S(2)}) collective-permute-start(bf16[384,128]{1,0:T(8,128)(2,1)S(1)} %get-tuple-element.46), channel_id=1, source_target_pairs={{0,12},{1,28},{2,14},{3,30},{4,8},{5,24},{6,10},{7,26},{8,4},{9,20... | collective-permute-start | bytes 294920 | tf_op jit(solution)/shard_map/ppermute | solution.py:136
  32.3 7.8 %collective-permute-start.15 = (bf16[8,256,128]{2,1,0:T(8,128)(2,1)S(1)}, bf16[8,256,128]{2,1,0:T(8,128)(2,1)S(1)}, u32[]{:S(2)}, u32[]{:S(2)}) collective-permute-start(bf16[8,256,128]{2,1,0:T(8,128)(2,1)S(1)} %shard_map.96.kv_ref), channel_id=1, source_target_pairs={{0,1},{1,0},{2,3},{3,2},{4,5},{5,4},{6,7},{7,6},{8,9},{9,8},{10,11... | collective-permute-start | bytes 1572872 | tf_op jit(solution)/shard_map/ppermute | solution.py:126
  38.6 13.5 %collective-permute-start.16 = (bf16[256,1024]{1,0:T(8,128)(2,1)S(1)}, bf16[256,1024]{1,0:T(8,128)(2,1)S(1)}, u32[]{:S(2)}, u32[]{:S(2)}) collective-permute-start(bf16[256,1024]{1,0:T(8,128)(2,1)S(1)} %copy-done.3), channel_id=1, source_target_pairs={{0,1},{1,0},{2,3},{3,2},{4,5},{5,4},{6,7},{7,6},{8,9},{9,8},{10,11... | collective-permute-start | bytes 1572872 | tf_op jit(solution)/shard_map/ppermute | solution.py:126
  47.4 13.8 %all-to-all-start = ((bf16[8,128,128]{2,1,0:T(8,128)(2,1)}), bf16[8,128,128]{2,1,0:T(8,128)(2,1)S(1)}, u32[]{:S(2)}, u32[]{:S(2)}) async-start(bf16[8,128,128]{2,1,0:T(8,128)(2,1)} %shard_map.98), calls=%async_computation | async-start | bytes 524288 | tf_op jit(solution)/shard_map/all_to_all | solution.py:479
  62.1 6.3 %collective-permute-start.18 = (bf16[256,256]{1,0:T(8,128)(2,1)S(1)}, bf16[256,256]{1,0:T(8,128)(2,1)S(1)}, u32[]{:S(2)}, u32[]{:S(2)}) collective-permute-start(bf16[256,256]{1,0:T(8,128)(2,1)S(1)} %get-tuple-element.53), channel_id=1, source_target_pairs={{0,2},{1,3},{2,0},{3,1},{4,6},{5,7},{6,4},{7,5},{8,10},{9,11},{10,... | collective-permute-start | bytes 393224 | tf_op jit(solution)/shard_map/ppermute | solution.py:126
  63.0 5.8 %collective-permute-start.19 = (bf16[256,256]{1,0:T(8,128)(2,1)S(1)}, bf16[256,256]{1,0:T(8,128)(2,1)S(1)}, u32[]{:S(2)}, u32[]{:S(2)}) collective-permute-start(bf16[256,256]{1,0:T(8,128)(2,1)S(1)} %get-tuple-element.54), channel_id=1, source_target_pairs={{0,3},{1,2},{2,1},{3,0},{4,7},{5,6},{6,5},{7,4},{8,11},{9,10},{10,... | collective-permute-start | bytes 393224 | tf_op jit(solution)/shard_map/ppermute | solution.py:126
  63.9 4.9 %collective-permute-start.17 = (bf16[256,256]{1,0:T(8,128)(2,1)S(1)}, bf16[256,256]{1,0:T(8,128)(2,1)S(1)}, u32[]{:S(2)}, u32[]{:S(2)}) collective-permute-start(bf16[256,256]{1,0:T(8,128)(2,1)S(1)} %get-tuple-element.52), channel_id=1, source_target_pairs={{0,1},{1,0},{2,3},{3,2},{4,5},{5,4},{6,7},{7,6},{8,9},{9,8},{10,11... | collective-permute-start | bytes 393224 | tf_op jit(solution)/shard_map/ppermute | solution.py:126

commit v5 on v4

--- a/solution.py
+++ b/solution.py
@@ -144,6 +144,11 @@
     return lax.dot_general(a, b, (((1,), (1,)), ((), ())), preferred_element_type=F32)
 
 
+def place():
+    head_at, shard = lax.axis_index("head"), lax.axis_index("tm")
+    return head_at & 1, head_at >> 1, shard & 3, shard >> 2
+
+
 def lane_iota(shape):
     return lax.broadcasted_iota(jnp.int32, shape, 1)
 
@@ -152,51 +157,59 @@
     return (x32 + jax.nn.gelu(term, approximate=True)).astype(BF16)
 
 
-def conv_kernel(
-    x_hbm, w_hbm, b_hbm, g_hbm, late_ref, early_ref, band_ref, base_ref, edge_ref,
-    x_ref, w_ref, b_ref, g_ref, sems,
-):
-    pairs = ((x_hbm, x_ref), (w_hbm, w_ref), (b_hbm, b_ref), (g_hbm, g_ref))
+def bands_of(w_ref, j):
+    groups, width, _ = w_ref.shape
+    bands = []
+    for g in range(groups):
+        parts = [w_ref[g, :, j * width : (j + 1) * width].astype(F32)]
+        if g > 0:
+            parts.insert(0, jnp.zeros((width, g * width), F32))
+        if g < groups - 1:
+            parts.append(jnp.zeros((width, (groups - 1 - g) * width), F32))
+        bands.append(jnp.concatenate(parts, axis=1))
+    return jnp.concatenate(bands, axis=0).astype(BF16)
+
+
+def gain_rows(g_ref):
+    pieces = g_ref[...].astype(F32)
+    gain = jnp.concatenate([pieces[i : i + 1] for i in range(pieces.shape[0])], axis=1)
+    return jnp.broadcast_to(gain, (GAIN_ROWS, gain.shape[1])).astype(BF16)
+
+
+def early_kernel(x_hbm, w_hbm, b_hbm, g_hbm, early_ref, edge_ref, x_ref, w_ref, b_ref, g_ref, sems):
+    half = early_ref.shape[0] - GAIN_ROWS
+    pairs = (
+        (x_hbm.at[half - 2 * RIM :], x_ref), (w_hbm, w_ref), (b_hbm, b_ref), (g_hbm, g_ref)
+    )
     copies = [pltpu.make_async_copy(src, dst, sems.at[i]) for i, (src, dst) in enumerate(pairs)]
     for copy in copies:
         copy.start()
     for copy in copies:
         copy.wait()
-    rows = x_ref.shape[0]
-    edge_ref[...] = x_ref[rows - RIM :]
-    groups, width, _ = w_ref.shape
-    x32 = x_ref[...].astype(F32)
+    edge_ref[...] = x_ref[half + RIM :]
+    ext = x_ref[...].astype(F32)
+    acc = jnp.zeros((half, ext.shape[1]), F32) + b_ref[...]
+    for j in range(KERNEL):
+        start = RIM + j * DILATION
+        acc += dot_nt(ext[start : start + half].astype(BF16), bands_of(w_ref, j))
+    early_ref[0:half] = gelu_mix(ext[2 * RIM :], acc)
+    early_ref[half:] = gain_rows(g_ref)
+
+
+def late_kernel(x_ref, w_ref, b_ref, g_ref, late_ref, band_ref, base_ref):
+    half = late_ref.shape[0] - GAIN_ROWS
+    x32 = x_ref[0:half].astype(F32)
     ext = jnp.concatenate([jnp.zeros((RIM, x32.shape[1]), F32), x32], axis=0)
     acc = jnp.zeros(x32.shape, F32) + b_ref[...]
     for j in range(KERNEL):
-        bands = []
-        for g in range(groups):
-            parts = [w_ref[g, :, j * width : (j + 1) * width].astype(F32)]
-            if g > 0:
-                parts.insert(0, jnp.zeros((width, g * width), F32))
-            if g < groups - 1:
-                parts.append(jnp.zeros((width, (groups - 1 - g) * width), F32))
-            bands.append(jnp.concatenate(parts, axis=1))
-        band = jnp.concatenate(bands, axis=0).astype(BF16)
+        band = bands_of(w_ref, j)
         if j < KERNEL - 1:
             band_ref[j] = band
-        acc += dot_nt(ext[j * DILATION : j * DILATION + rows].astype(BF16), band)
+        acc += dot_nt(ext[j * DILATION : j * DILATION + half].astype(BF16), band)
     base_ref[0:RIM] = acc[0:RIM]
     base_ref[RIM:] = x32[0:RIM]
-    mix = gelu_mix(x32, acc)
-    pieces = g_ref[...].astype(F32)
-    gain = jnp.concatenate([pieces[i : i + 1] for i in range(pieces.shape[0])], axis=1)
-    gain = jnp.broadcast_to(gain, (GAIN_ROWS, gain.shape[1])).astype(BF16)
-    half = rows // 2
-    late_ref[0:half] = mix[0:half]
-    late_ref[half:] = gain
-    early_ref[0:half] = mix[half:]
-    early_ref[half:] = gain
-
-
-def stage_kernel(*refs):
-    for ref, out in zip(refs[:3], refs[3:]):
-        out[...] = ref[...]
+    late_ref[0:half] = gelu_mix(x32, acc)
+    late_ref[half:] = gain_rows(g_ref)
 
 
 def fix_kernel(halo_ref, base_ref, band_ref, late_ref, o_ref):
@@ -209,7 +222,8 @@
     o_ref[0:RIM] = gelu_mix(base_ref[RIM:], acc)
 
 
-def qkv_kernel(pos_ref, a_ref, b_ref, y_ref, z_ref, wq, wk, wv, *rest):
+def qkv_kernel(a_ref, b_ref, y_ref, z_ref, wq, wk, wv, *rest):
+    pos_ref = place()
     outs, pack = rest[:-1], rest[-1]
     half = a_ref.shape[0] - GAIN_ROWS
     cols = a_ref.shape[1]
@@ -257,45 +271,55 @@
         kv_ref[i] = ref[0 : kv_ref.shape[1], :]
 
 
-def load_keys(pos_ref, valid_ref, kv_ref, kb, vb, side):
-    half = kb.shape[1]
+def halves():
+    lane = lane_iota((1, 128))
+    left = jnp.where(lane < HEAD_DIM, 1.0, 0.0)
+    return left.astype(BF16), (1.0 - left).astype(BF16)
+
+
+def shard_of(pos, side, i):
+    return 4 * jnp.bitwise_xor(side, 1 - i // 4) + jnp.bitwise_xor(pos[2], i % 4)
+
+
+def key_bias(valid_ref, shard, i, half):
     lane = lane_iota((half, 128))
     row = jnp.where(lane == HEAD_DIM, lax.broadcasted_iota(jnp.int32, (half, 128), 0), -1)
-    left = jnp.where(lane < HEAD_DIM, 1.0, 0.0).astype(BF16)
-    right = jnp.where(lane < HEAD_DIM, 0.0, 1.0).astype(BF16)
-    for i in range(kb.shape[0]):
-        part = 1 - i // 4
-        shard = 4 * jnp.bitwise_xor(side, part) + jnp.bitwise_xor(pos_ref[2], i % 4)
-        start = (2 * shard + part) * half
-        stretch = start // STRETCH
-        first_bad = jnp.maximum(valid_ref[stretch] - (start - stretch * STRETCH), 0)
-        bias = jnp.where(row >= first_bad, NEG, 0.0).astype(BF16)
-        kv = kv_ref[i]
-        kb[shard] = kv * left + bias
-        vb[shard] = kv * right + left
-
-
-def own_kernel(pos_ref, valid_ref, kv_ref, *rest):
-    own_refs, (kb, vb, qs_ref) = rest[:8], rest[8:]
-    load_keys(pos_ref, valid_ref, kv_ref, kb, vb, pos_ref[0])
+    start = (2 * shard + 1 - i // 4) * half
+    stretch = start // STRETCH
+    first_bad = jnp.maximum(valid_ref[stretch] - (start - stretch * STRETCH), 0)
+    return jnp.where(row >= first_bad, NEG, 0.0).astype(BF16)
+
+
+def own_kernel(valid_ref, kv_ref, *rest):
+    pos_ref = place()
+    own_refs, (kb, vb, qs_ref, bias_ref) = rest[:8], rest[8:]
+    left, right = halves()
     half = kb.shape[1]
     lane = lane_iota((half // 2, 128))
     pad = jnp.where(lane == HEAD_DIM, 1.0, 0.0)
     for i, ref in enumerate(own_refs):
-        shard = 4 * jnp.bitwise_xor(pos_ref[0], 1 - i // 4) + jnp.bitwise_xor(pos_ref[2], i % 4)
+        shard = shard_of(pos_ref, pos_ref[0], i)
+        kb[shard] = kv_ref[i] * left + key_bias(valid_ref, shard, i, half)
+        vb[shard] = kv_ref[i] * right + left
+        bias_ref[i] = key_bias(valid_ref, shard_of(pos_ref, 1 - pos_ref[0], i), i, half)
         packed = ref[half:, :].astype(F32)
         rolled = pltpu.roll(packed, HEAD_DIM, 1)
         qs_ref[shard, 0 : half // 2] = jnp.where(lane < HEAD_DIM, packed, pad).astype(BF16)
         qs_ref[shard, half // 2 :] = jnp.where(lane < HEAD_DIM, rolled, pad).astype(BF16)
 
 
-def attend_kernel(pos_ref, valid_ref, oth_ref, k_own, v_own, qs, o_ref, k_oth, v_oth, sc):
+def attend_kernel(oth_ref, bias_ref, k_own, v_own, qs, o_ref, k_oth, v_oth, sc):
     ranks = o_ref.shape[0]
     half = o_ref.shape[1] * 2
     halfrows = half // 2
+    pos_ref = place()
     core = pos_ref[0]
     lane_h = lane_iota((halfrows, 128))
-    load_keys(pos_ref, valid_ref, oth_ref, k_oth, v_oth, 1 - core)
+    left, right = halves()
+    for i in range(8):
+        shard = shard_of(pos_ref, 1 - core, i)
+        k_oth[shard] = oth_ref[i] * left + bias_ref[i]
+        v_oth[shard] = oth_ref[i] * right + left
     causal = lane_iota((half, half)) <= lax.broadcasted_iota(jnp.int32, (half, half), 0)
     blocks = [(k_own, v_own), (k_oth, v_oth)]
 
@@ -354,7 +378,8 @@
     return dot32(feats[0], w0[:, lanes]) + dot32(feats[1], w1[:, lanes])
 
 
-def far_kernel(pos_ref, att_ref, w0, w1, across_ref, corner_ref):
+def far_kernel(att_ref, w0, w1, across_ref, corner_ref):
+    pos_ref = place()
     feats = features(pos_ref[0], att_ref)
     for step, ref in ((2, across_ref), (3, corner_ref)):
         ref[...] = partial_out(pos_ref, feats, w0, w1, step, ref.shape[1]).astype(BF16)
@@ -365,7 +390,8 @@
     return pl.ds(pl.multiple_of(mine * half, half), half)
 
 
-def near_kernel(pos_ref, att_ref, w0, w1, late_ref, early_ref, base_ref, beside_ref):
+def near_kernel(att_ref, w0, w1, late_ref, early_ref, base_ref, beside_ref):
+    pos_ref = place()
     feats = features(pos_ref[0], att_ref)
     half, cols = beside_ref.shape
     beside_ref[...] = partial_out(pos_ref, feats, w0, w1, 1, cols).astype(BF16)
@@ -374,7 +400,8 @@
     base_ref[rows_of(pos_ref, half, 0)] += partial_out(pos_ref, feats, w0, w1, 0, cols)
 
 
-def final_kernel(pos_ref, base_ref, beside_ref, across_ref, corner_ref, o_ref):
+def final_kernel(base_ref, beside_ref, across_ref, corner_ref, o_ref):
+    pos_ref = place()
     half = beside_ref.shape[0]
     mine, other = rows_of(pos_ref, half, 0), rows_of(pos_ref, half, 1)
     o_ref[mine] = (base_ref[mine] + across_ref[...].astype(F32)).astype(BF16)
@@ -405,33 +432,34 @@
     tok, cols = tokens_in.shape
     half = tok // 2
     ranks = lax.axis_size("tm")
-    head_at, shard = lax.axis_index("head"), lax.axis_index("tm")
-    pos = jnp.stack([head_at & 1, head_at >> 1, shard & 3, shard >> 2]).astype(jnp.int32)
-
     operands = (
         tokens_in, jnp.swapaxes(conv_weight, 1, 2),
         conv_bias.reshape(1, cols), norm_gain.reshape(cols // 128, 128),
     )
-    late, early, band, base, edge = call(
-        conv_kernel,
+    early, edge = call(
+        early_kernel,
+        [((half + GAIN_ROWS, cols), BF16), ((RIM, cols), BF16)],
+        0,
+        operands,
+        us=1.5,
+        vmem=CONV_VMEM,
+        scratch=[pltpu.VMEM((half + 2 * RIM, cols), BF16)]
+        + [pltpu.VMEM(x.shape, x.dtype) for x in operands[1:]]
+        + [pltpu.SemaphoreType.DMA((len(operands),))],
+        space=pltpu.HBM,
+    )
+    halo = from_behind(edge, "tm", 1)
+    operands = lax.optimization_barrier((*operands, edge))[:4]
+    late, band, base = call(
+        late_kernel,
         [
-            ((half + GAIN_ROWS, cols), BF16),
             ((half + GAIN_ROWS, cols), BF16),
             ((KERNEL - 1, cols, cols), BF16),
             ((2 * RIM, cols), F32),
-            ((RIM, cols), BF16),
         ],
         0,
         operands,
-        us=2.0,
-        vmem=CONV_VMEM,
-        scratch=[pltpu.VMEM(x.shape, x.dtype) for x in operands]
-        + [pltpu.SemaphoreType.DMA((len(operands),))],
-        space=pltpu.HBM,
-    )
-    halo = from_behind(edge, "tm", 1)
-    base, band, late = call(
-        stage_kernel, [(x.shape, x.dtype) for x in (base, band, late)], 0, (base, band, late), us=1.0
+        us=1.0,
     )
 
     def project_half(x, after=None):
@@ -445,8 +473,8 @@
         return call(
             qkv_kernel,
             [((half + half // 2, 2 * HEAD_DIM), BF16)] * 4,
-            1,
-            (pos, x, beside, across, corner, w_query, w_key, w_value),
+            0,
+            (x, beside, across, corner, w_query, w_key, w_value),
             us=1.0,
             scratch=[pltpu.VMEM((4, half + half // 2, 2 * HEAD_DIM), BF16)],
         )
@@ -460,14 +488,14 @@
     kv = call(pack_kernel, [((8, half, 128), BF16)], 0, own, us=0.4)
     wo1 = swap(lax.optimization_barrier((w_out, sends[0]))[0], 1)
     kv_oth = swap(kv, 1)
-    k_own, v_own, qs = call(
-        own_kernel, [((8, half, 128), BF16)] * 3, 2, (pos, valid_count, kv, *own), us=0.8
+    k_own, v_own, qs, bias = call(
+        own_kernel, [((8, half, 128), BF16)] * 4, 1, (valid_count, kv, *own), us=0.8
     )
     attended = call(
         attend_kernel,
         [((8, half // 2, 2 * HEAD_DIM), BF16)],
-        2,
-        (pos, valid_count, kv_oth, k_own, v_own, qs),
+        0,
+        (kv_oth, bias, k_own, v_own, qs),
         us=8.0,
         vmem=24,
         scratch=[
@@ -478,18 +506,18 @@
     )
     back = lax.all_to_all(attended, "tm", 0, 0)
     across, corner = call(
-        far_kernel, [((half, cols), BF16)] * 2, 1, (pos, back, w_out, wo1), us=0.6
+        far_kernel, [((half, cols), BF16)] * 2, 0, (back, w_out, wo1), us=0.6
     )
     across, corner = swap(across, 2), swap(corner, 3)
     base, beside = call(
         near_kernel,
         [((tok, cols), F32), ((half, cols), BF16)],
-        1,
-        (pos, back, w_out, wo1, late, early),
+        0,
+        (back, w_out, wo1, late, early),
         us=1.0,
     )
-    args = (pos, base, swap(beside, 1), across, corner)
-    return call(final_kernel, [((tok, cols), BF16)], 1, args, us=0.5)
+    args = (base, swap(beside, 1), across, corner)
+    return call(final_kernel, [((tok, cols), BF16)], 0, args, us=0.5)
 
 
 def solution(mesh):

time: 71 us -> 67.7 us (0.954)
  Pallas kernels: 16.7 us -> 13.5 us
  starting transfers between devices: 32.4 us -> 35.4 us
  local copies, waits for them, and re-layouts: 2.51 us -> 0.04 us
    pallas_call x11, Pallas kernels: 16.7 us -> 13.5 us  [call(): pl.pallas_call(kernel, out_shape=outs, in_specs=[pl.BlockSpec(memory_spac...]
    ppermute x8, starting transfers between devices: 10.4 us -> 13.2 us  [spread(): return lax.ppermute(value, ('tm', 'head'), pairs)]
    unnamed x18 -> x20, local copies, waits for them, and re-layouts: 2.51 us -> 0.04 us
    ppermute x1, waiting for transfers between devices: 0.01 us -> 0.74 us  [from_behind(): lax.ppermute(value, axis, [(source, source + steps) for source in range(f...]
  transfers between devices with their start and end apart: 21 -> 21, of which waited for: 9 -> 8; matrix products, arithmetic and copies ran while one was open for 0% -> 0% of each run, Pallas kernels for 17% -> 15%
where the time goes in v5:
time: 67.7 us; the launch traced here: 67.2 us
  starting transfers between devices  35.4 us (52%)
  waiting for transfers between devices  18.1 us (27%)
  Pallas kernels  13.5 us (20%)
    ppermute x11, starting transfers between devices, swap(): lax.ppermute(value, 'head', [(i, i ^ bit) for i in range(lax.axis_size('h...  13.9 us
    pallas_call x11, Pallas kernels, call(): pl.pallas_call(kernel, out_shape=outs, in_specs=[pl.BlockSpec(memory_spac...  13.5 us
    ppermute x8, starting transfers between devices, spread(): return lax.ppermute(value, ('tm', 'head'), pairs)  13.2 us
    all_to_all x1, waiting for transfers between devices, on_device(): back = lax.all_to_all(attended, 'tm', 0, 0)  9.21 us
    all_to_all x1, starting transfers between devices, on_device(): back = lax.all_to_all(attended, 'tm', 0, 0)  4.83 us
    ppermute x11, waiting for transfers between devices, swap(): lax.ppermute(value, 'head', [(i, i ^ bit) for i in range(lax.axis_size('h...  4.71 us
    ppermute x8, waiting for transfers between devices, spread(): return lax.ppermute(value, ('tm', 'head'), pairs)  3.47 us
    ppermute x1, starting transfers between devices, from_behind(): lax.ppermute(value, axis, [(source, source + steps) for source in range(f...  3.38 us
  transfers between devices with their start and end apart: 21, of which 8 were waited for; matrix products, arithmetic and copies ran while one was open for 0% of the time, Pallas kernels for 15%

profile of v5, /device:TPU:0, one launch (start us, length us, event | category | flops | bytes accessed | tf_op | source)
XLA Modules:
  0.0 67.2 jit_solution(16698219328986876915)
XLA Ops:
  0.0 2.1 %shard_map.91 = (bf16[264,256]{1,0:T(8,128)(2,1)}, bf16[8,256]{1,0:T(8,128)(2,1)}) custom-call(bf16[512,256]{1,0:T(8,128)(2,1)} %x_ref, bf16[4,64,192]{2,1,0:T(8,128)(2,1)} %bitcast.3, f32[1,256]{1,0:T(1,128)} %bitcast.5, bf16[2,128]{1,0:T(2,128)(2,1)} %bitcast.7), custom_call_target="tpu_custom_call" | custom-call | flops 1500000000 | bytes 5400000 | tf_op jit(solution)/shard_map/pallas_call | solution.py:415
  2.2 0.0 copy-start.7
  2.2 0.0 copy-start.8
  2.2 3.0 %collective-permute-start.1 = (bf16[264,256]{1,0:T(8,128)(2,1)}, bf16[264,256]{1,0:T(8,128)(2,1)S(1)}, u32[]{:S(2)}, u32[]{:S(2)}) collective-permute-start(bf16[264,256]{1,0:T(8,128)(2,1)} %get-tuple-element.32.a_ref.early_ref), channel_id=1, source_target_pairs={{0,2},{1,3},{2,0},{3,1},{4,6},{5,7},{6,4},{7,5},{8,10},{9,11},{10,... | collective-permute-start | bytes 405512 | tf_op jit(solution)/shard_map/ppermute | solution.py:126
  5.2 0.0 collective-permute-start
  5.2 3.4 %collective-permute-start.7 = (bf16[8,256]{1,0:T(8,128)(2,1)}, bf16[8,256]{1,0:T(8,128)(2,1)S(1)}, u32[]{:S(2)}, u32[]{:S(2)}) collective-permute-start(bf16[8,256]{1,0:T(8,128)(2,1)} %get-tuple-element.37), channel_id=1, source_target_pairs={{0,4},{4,8},{8,12},{12,16},{16,20},{20,24},{24,28},{1,5},{5,9},{9,... | collective-permute-start | bytes 12296 | tf_op jit(solution)/shard_map/ppermute | solution.py:28
  8.7 0.4 shard_map.93
  9.1 0.0 collective-permute-done.1.y_ref
  9.1 0.3 collective-permute-start.2
  9.4 0.7 %collective-permute-done.7.halo_ref = bf16[8,256]{1,0:T(8,128)(2,1)S(1)} collective-permute-done((bf16[8,256]{1,0:T(8,128)(2,1)}, bf16[8,256]{1,0:T(8,128)(2,1)S(1)}, u32[]{:S(2)}, u32[]{:S(2)}) %collective-permute-start.7) | collective-permute-done | bytes 4128 | tf_op jit(solution)/shard_map/ppermute | solution.py:28
  10.1 0.2 shard_map.94.a_ref.late_ref
  10.3 0.8 %collective-permute-start.10 = (bf16[264,256]{1,0:T(8,128)(2,1)S(1)}, bf16[264,256]{1,0:T(8,128)(2,1)S(1)}, u32[]{:S(2)}, u32[]{:S(2)}) collective-permute-start(bf16[264,256]{1,0:T(8,128)(2,1)S(1)} %shard_map.94.a_ref.late_ref), channel_id=1, source_target_pairs={{0,3},{1,2},{2,1},{3,0},{4,7},{5,6},{6,5},{7,4},{8,11},{9,10},{10,... | collective-permute-start | bytes 405512 | tf_op jit(solution)/shard_map/ppermute | solution.py:126
  11.2 0.5 collective-permute-start.9
  11.7 0.0 collective-permute-done.b_ref
  11.7 0.8 %shard_map.92 = (bf16[384,128]{1,0:T(8,128)(2,1)S(1)}, bf16[384,128]{1,0:T(8,128)(2,1)S(1)}, bf16[384,128]{1,0:T(8,128)(2,1)S(1)}, bf16[384,128]{1,0:T(8,128)(2,1)S(1)}) custom-call(bf16[264,256]{1,0:T(8,128)(2,1)S(1)} %copy-done.5, bf16[264,256]{1,0:T(8,128)(2,1)S(1)} %collective-permute-done.b_ref, bf16[264,256]{1,0:T(8,128)(2,1)S(1)} %collective-permute-done.1.y_ref, ...), custom_call_target="tpu_custom_call" | custom-call | flops 1000000000 | bytes 3600000 | tf_op jit(solution)/shard_map/pallas_call | solution.py:415
  12.6 0.6 collective-permute-start.8
  13.2 0.1 collective-permute-start.3
  13.3 4.2 %collective-permute-start.4 = (bf16[384,128]{1,0:T(8,128)(2,1)S(1)}, bf16[384,128]{1,0:T(8,128)(2,1)S(1)}, u32[]{:S(2)}, u32[]{:S(2)}) collective-permute-start(bf16[384,128]{1,0:T(8,128)(2,1)S(1)} %get-tuple-element.34), channel_id=1, source_target_pairs={{0,5},{1,21},{2,7},{3,23},{4,1},{5,17},{6,3},{7,19},{8,13},{9,29},... | collective-permute-start | bytes 294920 | tf_op jit(solution)/shard_map/ppermute | solution.py:136
  17.5 0.0 collective-permute-done.10.z_ref
  17.5 1.4 %collective-permute-start.5 = (bf16[384,128]{1,0:T(8,128)(2,1)S(1)}, bf16[384,128]{1,0:T(8,128)(2,1)S(1)}, u32[]{:S(2)}, u32[]{:S(2)}) collective-permute-start(bf16[384,128]{1,0:T(8,128)(2,1)S(1)} %get-tuple-element.35), channel_id=1, source_target_pairs={{0,9},{1,25},{2,11},{3,27},{4,13},{5,29},{6,15},{7,31},{8,1},{9,17... | collective-permute-start | bytes 294920 | tf_op jit(solution)/shard_map/ppermute | solution.py:136
  18.9 0.0 collective-permute-done.9.y_ref
  18.9 2.8 %collective-permute-start.6 = (bf16[384,128]{1,0:T(8,128)(2,1)S(1)}, bf16[384,128]{1,0:T(8,128)(2,1)S(1)}, u32[]{:S(2)}, u32[]{:S(2)}) collective-permute-start(bf16[384,128]{1,0:T(8,128)(2,1)S(1)} %get-tuple-element.36), channel_id=1, source_target_pairs={{0,13},{1,29},{2,15},{3,31},{4,9},{5,25},{6,11},{7,27},{8,5},{9,21... | collective-permute-start | bytes 294920 | tf_op jit(solution)/shard_map/ppermute | solution.py:136
  21.7 0.0 collective-permute-done.8.b_ref
  21.7 0.8 %shard_map.95 = (bf16[384,128]{1,0:T(8,128)(2,1)S(1)}, bf16[384,128]{1,0:T(8,128)(2,1)S(1)}, bf16[384,128]{1,0:T(8,128)(2,1)S(1)}, bf16[384,128]{1,0:T(8,128)(2,1)S(1)}) custom-call(bf16[264,256]{1,0:T(8,128)(2,1)S(1)} %shard_map.94.a_ref.late_ref, bf16[264,256]{1,0:T(8,128)(2,1)S(1)} %collective-permute-done.8.b_ref, ...), custom_call_target="tpu_custom_call" | custom-call | flops 1000000000 | bytes 3600000 | tf_op jit(solution)/shard_map/pallas_call | solution.py:415
  22.6 0.7 collective-permute-start.11
  23.3 0.0 collective-permute-done.3.refs_0_.rest_0_
  23.3 1.5 %collective-permute-start.12 = (bf16[384,128]{1,0:T(8,128)(2,1)S(1)}, bf16[384,128]{1,0:T(8,128)(2,1)S(1)}, u32[]{:S(2)}, u32[]{:S(2)}) collective-permute-start(bf16[384,128]{1,0:T(8,128)(2,1)S(1)} %get-tuple-element.47), channel_id=1, source_target_pairs={{0,4},{1,20},{2,6},{3,22},{4,0},{5,16},{6,2},{7,18},{8,12},{9,28},... | collective-permute-start | bytes 294920 | tf_op jit(solution)/shard_map/ppermute | solution.py:136
  24.8 0.0 collective-permute-done.4.refs_1_.rest_1_
  24.8 0.5 collective-permute-start.13
  25.3 2.0 %collective-permute-start.14 = (bf16[384,128]{1,0:T(8,128)(2,1)S(1)}, bf16[384,128]{1,0:T(8,128)(2,1)S(1)}, u32[]{:S(2)}, u32[]{:S(2)}) collective-permute-start(bf16[384,128]{1,0:T(8,128)(2,1)S(1)} %get-tuple-element.49), channel_id=1, source_target_pairs={{0,12},{1,28},{2,14},{3,30},{4,8},{5,24},{6,10},{7,26},{8,4},{9,20... | collective-permute-start | bytes 294920 | tf_op jit(solution)/shard_map/ppermute | solution.py:136
  27.3 0.9 %collective-permute-done.12.refs_5_.rest_5_ = bf16[384,128]{1,0:T(8,128)(2,1)S(1)} collective-permute-done((bf16[384,128]{1,0:T(8,128)(2,1)S(1)}, bf16[384,128]{1,0:T(8,128)(2,1)S(1)}, u32[]{:S(2)}, u32[]{:S(2)}) %collective-permute-start.12) | collective-permute-done | bytes 98336 | tf_op jit(solution)/shard_map/ppermute | solution.py:136
  28.2 1.1 %collective-permute-done.13.refs_6_.rest_6_ = bf16[384,128]{1,0:T(8,128)(2,1)S(1)} collective-permute-done((bf16[384,128]{1,0:T(8,128)(2,1)S(1)}, bf16[384,128]{1,0:T(8,128)(2,1)S(1)}, u32[]{:S(2)}, u32[]{:S(2)}) %collective-permute-start.13) | collective-permute-done | bytes 98336 | tf_op jit(solution)/shard_map/ppermute | solution.py:136
  29.4 1.4 %collective-permute-done.14.refs_7_.rest_7_ = bf16[384,128]{1,0:T(8,128)(2,1)S(1)} collective-permute-done((bf16[384,128]{1,0:T(8,128)(2,1)S(1)}, bf16[384,128]{1,0:T(8,128)(2,1)S(1)}, u32[]{:S(2)}, u32[]{:S(2)}) %collective-permute-start.14) | collective-permute-done | bytes 98336 | tf_op jit(solution)/shard_map/ppermute | solution.py:136
  30.8 6.2 %collective-permute-start.15 = (bf16[8,256,128]{2,1,0:T(8,128)(2,1)S(1)}, bf16[8,256,128]{2,1,0:T(8,128)(2,1)S(1)}, u32[]{:S(2)}, u32[]{:S(2)}) collective-permute-start(bf16[8,256,128]{2,1,0:T(8,128)(2,1)S(1)} %shard_map.96.kv_ref), channel_id=1, source_target_pairs={{0,1},{1,0},{2,3},{3,2},{4,5},{5,4},{6,7},{7,6},{8,9},{9,8},{10,11... | collective-permute-start | bytes 1572872 | tf_op jit(solution)/shard_map/ppermute | solution.py:126
  37.1 0.1 collective-permute-start.16
  37.2 1.1 %shard_map.97 = (bf16[8,256,128]{2,1,0:T(8,128)(2,1)S(1)}, bf16[8,256,128]{2,1,0:T(8,128)(2,1)S(1)}, bf16[8,256,128]{2,1,0:T(8,128)(2,1)S(1)}, bf16[8,256,128]{2,1,0:T(8,128)(2,1)S(1)}) custom-call(s32[4]{0:T(128)S(1)} %copy-done.9, bf16[8,256,128]{2,1,0:T(8,128)(2,1)S(1)} %shard_map.96.kv_ref, bf16[384,128]{1,0:T(8,128)(2,1)S(1)} %collective-permute-done.3.refs_0_.rest_0_, ...), custom_call_target="tpu_custom_call" | custom-call | flops 800000000 | bytes 2880000 | tf_op jit(solution)/shard_map/pallas_call | solution.py:415
  38.3 0.3 collective-permute-done.15.oth_ref
  38.6 6.5 %shard_map.98 = bf16[8,128,128]{2,1,0:T(8,128)(2,1)} custom-call(bf16[8,256,128]{2,1,0:T(8,128)(2,1)S(1)} %collective-permute-done.15.oth_ref, bf16[8,256,128]{2,1,0:T(8,128)(2,1)S(1)} %get-tuple-element.50.bias_ref, bf16[8,256,128]{2,1,0:T(8,128)(2,1)S(1)} %get-tuple-element.51.k_own, bf16[8,256,128]{2,1,0:T(8,128)(2,1)S(1)} %get-tuple-element.52.v_own, ...), custom_call_target="tpu_custom_call" | custom-call | flops 8000000000 | bytes 28800000 | tf_op jit(solution)/shard_map/pallas_call | solution.py:415
  45.1 4.8 %all-to-all-start = ((bf16[8,128,128]{2,1,0:T(8,128)(2,1)}), bf16[8,128,128]{2,1,0:T(8,128)(2,1)S(1)}, u32[]{:S(2)}, u32[]{:S(2)}) async-start(bf16[8,128,128]{2,1,0:T(8,128)(2,1)} %shard_map.98), calls=%async_computation | async-start | bytes 524288 | tf_op jit(solution)/shard_map/all_to_all | solution.py:507
  49.9 9.2 %all-to-all-done.att_ref = bf16[8,128,128]{2,1,0:T(8,128)(2,1)S(1)} async-done(((bf16[8,128,128]{2,1,0:T(8,128)(2,1)}), bf16[8,128,128]{2,1,0:T(8,128)(2,1)S(1)}, u32[]{:S(2)}, u32[]{:S(2)}) %all-to-all-start) | async-done | bytes 262176 | tf_op jit(solution)/shard_map/all_to_all | solution.py:507
  59.1 0.3 shard_map.100
  59.5 1.3 %collective-permute-start.18 = (bf16[256,256]{1,0:T(8,128)(2,1)S(1)}, bf16[256,256]{1,0:T(8,128)(2,1)S(1)}, u32[]{:S(2)}, u32[]{:S(2)}) collective-permute-start(bf16[256,256]{1,0:T(8,128)(2,1)S(1)} %get-tuple-element.57), channel_id=1, source_target_pairs={{0,2},{1,3},{2,0},{3,1},{4,6},{5,7},{6,4},{7,5},{8,10},{9,11},{10,... | collective-permute-start | bytes 393224 | tf_op jit(solution)/shard_map/ppermute | solution.py:126
  60.7 0.0 collective-permute-start.19
  60.7 0.3 shard_map.99
  61.1 1.0 %collective-permute-start.17 = (bf16[256,256]{1,0:T(8,128)(2,1)S(1)}, bf16[256,256]{1,0:T(8,128)(2,1)S(1)}, u32[]{:S(2)}, u32[]{:S(2)}) collective-permute-start(bf16[256,256]{1,0:T(8,128)(2,1)S(1)} %get-tuple-element.56), channel_id=1, source_target_pairs={{0,1},{1,0},{2,3},{3,2},{4,5},{5,4},{6,7},{7,6},{8,9},{9,8},{10,11... | collective-permute-start | bytes 393224 | tf_op jit(solution)/shard_map/ppermute | solution.py:126
  62.1 3.2 %collective-permute-done.18.across_ref = bf16[256,256]{1,0:T(8,128)(2,1)S(1)} collective-permute-done((bf16[256,256]{1,0:T(8,128)(2,1)S(1)}, bf16[256,256]{1,0:T(8,128)(2,1)S(1)}, u32[]{:S(2)}, u32[]{:S(2)}) %collective-permute-start.18) | collective-permute-done | bytes 131104 | tf_op jit(solution)/shard_map/ppermute | solution.py:126
  65.3 1.1 %collective-permute-done.19.corner_ref = bf16[256,256]{1,0:T(8,128)(2,1)S(1)} collective-permute-done((bf16[256,256]{1,0:T(8,128)(2,1)S(1)}, bf16[256,256]{1,0:T(8,128)(2,1)S(1)}, u32[]{:S(2)}, u32[]{:S(2)}) %collective-permute-start.19) | collective-permute-done | bytes 131104 | tf_op jit(solution)/shard_map/ppermute | solution.py:126
  66.5 0.8 %shard_map.101 = bf16[512,256]{1,0:T(8,128)(2,1)} custom-call(f32[512,256]{1,0:T(8,128)S(1)} %get-tuple-element.55.base_ref, bf16[256,256]{1,0:T(8,128)(2,1)S(1)} %collective-permute-done.17.beside_ref, bf16[256,256]{1,0:T(8,128)(2,1)S(1)} %collective-permute-done.18.across_ref, bf16[256,256]{1,0:T(8,128)(2,1)S(1)} %collective-permute-done.19.corner_ref), custom_call_target="tpu_custom_call" | custom-call | flops 500000000 | bytes 1800000 | tf_op jit(solution)/shard_map/pallas_call | solution.py:415
  (25 shorter events, 0.1 us)
Async XLA Ops:
  0.0 8.6 %copy-start.4 = (bf16[512,256]{1,0:T(8,128)(2,1)S(1)}, bf16[512,256]{1,0:T(8,128)(2,1)}, u32[]{:S(2)}) copy-start(bf16[512,256]{1,0:T(8,128)(2,1)} %x_ref) | copy-start | bytes 786436
  0.0 8.6 %copy-start.6 = (bf16[4,192,64]{1,2,0:T(8,128)(2,1)S(1)}, bf16[4,192,64]{1,2,0:T(8,128)(2,1)}, u32[]{:S(2)}) copy-start(bf16[4,192,64]{1,2,0:T(8,128)(2,1)} %param.10) | copy-start | bytes 294916
  2.2 6.5 %copy-start.7 = (f32[256]{0:T(256)S(1)}, f32[256]{0:T(256)}, u32[]{:S(2)}) copy-start(f32[256]{0:T(256)} %param.11) | copy-start | bytes 3076
  2.2 6.5 %copy-start.8 = (bf16[256]{0:T(256)(128)(2,1)S(1)}, bf16[256]{0:T(256)(128)(2,1)}, u32[]{:S(2)}) copy-start(bf16[256]{0:T(256)(128)(2,1)} %param.12) | copy-start | bytes 1540
  2.2 6.9 %collective-permute-start.1 = (bf16[264,256]{1,0:T(8,128)(2,1)}, bf16[264,256]{1,0:T(8,128)(2,1)S(1)}, u32[]{:S(2)}, u32[]{:S(2)}) collective-permute-start(bf16[264,256]{1,0:T(8,128)(2,1)} %get-tuple-element.32.a_ref.early_ref), channel_id=1, source_target_pairs={{0,2},{1,3},{2,0},{3,1},{4,6},{5,7},{6,4},{7,5},{8,10},{9,11},{10,... | collective-permute-start | bytes 405512 | tf_op jit(solution)/shard_map/ppermute | solution.py:126
  5.2 6.5 %collective-permute-start = (bf16[264,256]{1,0:T(8,128)(2,1)}, bf16[264,256]{1,0:T(8,128)(2,1)S(1)}, u32[]{:S(2)}, u32[]{:S(2)}) collective-permute-start(bf16[264,256]{1,0:T(8,128)(2,1)} %get-tuple-element.32.a_ref.early_ref), channel_id=1, source_target_pairs={{0,1},{1,0},{2,3},{3,2},{4,5},{5,4},{6,7},{7,6},{8,9},{9,8},{10,11... | collective-permute-start | bytes 405512 | tf_op jit(solution)/shard_map/ppermute | solution.py:126
  5.2 4.9 %collective-permute-start.7 = (bf16[8,256]{1,0:T(8,128)(2,1)}, bf16[8,256]{1,0:T(8,128)(2,1)S(1)}, u32[]{:S(2)}, u32[]{:S(2)}) collective-permute-start(bf16[8,256]{1,0:T(8,128)(2,1)} %get-tuple-element.37), channel_id=1, source_target_pairs={{0,4},{4,8},{8,12},{12,16},{16,20},{20,24},{24,28},{1,5},{5,9},{9,... | collective-permute-start | bytes 12296 | tf_op jit(solution)/shard_map/ppermute | solution.py:28
  9.1 2.6 %collective-permute-start.2 = (bf16[264,256]{1,0:T(8,128)(2,1)S(1)}, bf16[264,256]{1,0:T(8,128)(2,1)S(1)}, u32[]{:S(2)}, u32[]{:S(2)}) collective-permute-start(bf16[264,256]{1,0:T(8,128)(2,1)S(1)} %collective-permute-done.1.y_ref), channel_id=1, source_target_pairs={{0,1},{1,0},{2,3},{3,2},{4,5},{5,4},{6,7},{7,6},{8,9},{9,8},{10,11... | collective-permute-start | bytes 405512 | tf_op jit(solution)/shard_map/ppermute | solution.py:126
  10.1 1.6 %copy-start = (bf16[1024,256]{1,0:T(8,128)(2,1)S(1)}, bf16[1024,256]{1,0:T(8,128)(2,1)}, u32[]{:S(2)}) copy-start(bf16[1024,256]{1,0:T(8,128)(2,1)} %wq.3) | copy-start | bytes 1572868
  10.1 1.6 %copy-start.1 = (bf16[1024,256]{1,0:T(8,128)(2,1)S(1)}, bf16[1024,256]{1,0:T(8,128)(2,1)}, u32[]{:S(2)}) copy-start(bf16[1024,256]{1,0:T(8,128)(2,1)} %wk.3) | copy-start | bytes 1572868
  10.1 1.6 %copy-start.2 = (bf16[1024,256]{1,0:T(8,128)(2,1)S(1)}, bf16[1024,256]{1,0:T(8,128)(2,1)}, u32[]{:S(2)}) copy-start(bf16[1024,256]{1,0:T(8,128)(2,1)} %wv.3) | copy-start | bytes 1572868
  10.1 1.6 %copy-start.5 = (bf16[264,256]{1,0:T(8,128)(2,1)S(1)}, bf16[264,256]{1,0:T(8,128)(2,1)}, u32[]{:S(2)}) copy-start(bf16[264,256]{1,0:T(8,128)(2,1)} %get-tuple-element.32.a_ref.early_ref) | copy-start | bytes 405508
  10.3 7.1 %collective-permute-start.10 = (bf16[264,256]{1,0:T(8,128)(2,1)S(1)}, bf16[264,256]{1,0:T(8,128)(2,1)S(1)}, u32[]{:S(2)}, u32[]{:S(2)}) collective-permute-start(bf16[264,256]{1,0:T(8,128)(2,1)S(1)} %shard_map.94.a_ref.late_ref), channel_id=1, source_target_pairs={{0,3},{1,2},{2,1},{3,0},{4,7},{5,6},{6,5},{7,4},{8,11},{9,10},{10,... | collective-permute-start | bytes 405512 | tf_op jit(solution)/shard_map/ppermute | solution.py:126
  11.2 7.8 %collective-permute-start.9 = (bf16[264,256]{1,0:T(8,128)(2,1)S(1)}, bf16[264,256]{1,0:T(8,128)(2,1)S(1)}, u32[]{:S(2)}, u32[]{:S(2)}) collective-permute-start(bf16[264,256]{1,0:T(8,128)(2,1)S(1)} %shard_map.94.a_ref.late_ref), channel_id=1, source_target_pairs={{0,2},{1,3},{2,0},{3,1},{4,6},{5,7},{6,4},{7,5},{8,10},{9,11},{10,... | collective-permute-start | bytes 405512 | tf_op jit(solution)/shard_map/ppermute | solution.py:126
  12.6 9.2 %collective-permute-start.8 = (bf16[264,256]{1,0:T(8,128)(2,1)S(1)}, bf16[264,256]{1,0:T(8,128)(2,1)S(1)}, u32[]{:S(2)}, u32[]{:S(2)}) collective-permute-start(bf16[264,256]{1,0:T(8,128)(2,1)S(1)} %shard_map.94.a_ref.late_ref), channel_id=1, source_target_pairs={{0,1},{1,0},{2,3},{3,2},{4,5},{5,4},{6,7},{7,6},{8,9},{9,8},{10,11... | collective-permute-start | bytes 405512 | tf_op jit(solution)/shard_map/ppermute | solution.py:126
  13.2 10.1 %collective-permute-start.3 = (bf16[384,128]{1,0:T(8,128)(2,1)S(1)}, bf16[384,128]{1,0:T(8,128)(2,1)S(1)}, u32[]{:S(2)}, u32[]{:S(2)}) collective-permute-start(bf16[384,128]{1,0:T(8,128)(2,1)S(1)} %get-tuple-element.33), channel_id=1, source_target_pairs={{0,1},{1,17},{2,3},{3,19},{4,5},{5,21},{6,7},{7,23},{8,9},{9,25},{... | collective-permute-start | bytes 294920 | tf_op jit(solution)/shard_map/ppermute | solution.py:136
  13.3 11.5 %collective-permute-start.4 = (bf16[384,128]{1,0:T(8,128)(2,1)S(1)}, bf16[384,128]{1,0:T(8,128)(2,1)S(1)}, u32[]{:S(2)}, u32[]{:S(2)}) collective-permute-start(bf16[384,128]{1,0:T(8,128)(2,1)S(1)} %get-tuple-element.34), channel_id=1, source_target_pairs={{0,5},{1,21},{2,7},{3,23},{4,1},{5,17},{6,3},{7,19},{8,13},{9,29},... | collective-permute-start | bytes 294920 | tf_op jit(solution)/shard_map/ppermute | solution.py:136
  17.5 7.8 %collective-permute-start.5 = (bf16[384,128]{1,0:T(8,128)(2,1)S(1)}, bf16[384,128]{1,0:T(8,128)(2,1)S(1)}, u32[]{:S(2)}, u32[]{:S(2)}) collective-permute-start(bf16[384,128]{1,0:T(8,128)(2,1)S(1)} %get-tuple-element.35), channel_id=1, source_target_pairs={{0,9},{1,25},{2,11},{3,27},{4,13},{5,29},{6,15},{7,31},{8,1},{9,17... | collective-permute-start | bytes 294920 | tf_op jit(solution)/shard_map/ppermute | solution.py:136
  18.9 8.4 %collective-permute-start.6 = (bf16[384,128]{1,0:T(8,128)(2,1)S(1)}, bf16[384,128]{1,0:T(8,128)(2,1)S(1)}, u32[]{:S(2)}, u32[]{:S(2)}) collective-permute-start(bf16[384,128]{1,0:T(8,128)(2,1)S(1)} %get-tuple-element.36), channel_id=1, source_target_pairs={{0,13},{1,29},{2,15},{3,31},{4,9},{5,25},{6,11},{7,27},{8,5},{9,21... | collective-permute-start | bytes 294920 | tf_op jit(solution)/shard_map/ppermute | solution.py:136
  22.6 4.7 %collective-permute-start.11 = (bf16[384,128]{1,0:T(8,128)(2,1)S(1)}, bf16[384,128]{1,0:T(8,128)(2,1)S(1)}, u32[]{:S(2)}, u32[]{:S(2)}) collective-permute-start(bf16[384,128]{1,0:T(8,128)(2,1)S(1)} %get-tuple-element.46), channel_id=1, source_target_pairs={{0,0},{1,16},{2,2},{3,18},{4,4},{5,20},{6,6},{7,22},{8,8},{9,24},{... | collective-permute-start | bytes 294920 | tf_op jit(solution)/shard_map/ppermute | solution.py:136
  23.3 5.0 %collective-permute-start.12 = (bf16[384,128]{1,0:T(8,128)(2,1)S(1)}, bf16[384,128]{1,0:T(8,128)(2,1)S(1)}, u32[]{:S(2)}, u32[]{:S(2)}) collective-permute-start(bf16[384,128]{1,0:T(8,128)(2,1)S(1)} %get-tuple-element.47), channel_id=1, source_target_pairs={{0,4},{1,20},{2,6},{3,22},{4,0},{5,16},{6,2},{7,18},{8,12},{9,28},... | collective-permute-start | bytes 294920 | tf_op jit(solution)/shard_map/ppermute | solution.py:136
  24.8 4.6 %collective-permute-start.13 = (bf16[384,128]{1,0:T(8,128)(2,1)S(1)}, bf16[384,128]{1,0:T(8,128)(2,1)S(1)}, u32[]{:S(2)}, u32[]{:S(2)}) collective-permute-start(bf16[384,128]{1,0:T(8,128)(2,1)S(1)} %get-tuple-element.48), channel_id=1, source_target_pairs={{0,8},{1,24},{2,10},{3,26},{4,12},{5,28},{6,14},{7,30},{8,0},{9,16... | collective-permute-start | bytes 294920 | tf_op jit(solution)/shard_map/ppermute | solution.py:136
  25.3 11.8 %copy-start.3 = (bf16[256,1024]{1,0:T(8,128)(2,1)S(1)}, bf16[256,1024]{1,0:T(8,128)(2,1)}, u32[]{:S(2)}) copy-start(bf16[256,1024]{1,0:T(8,128)(2,1)} %w0.3) | copy-start | bytes 1572868
  25.3 11.9 %copy-start.9 = (s32[4]{0:T(128)S(1)}, s32[4]{0:T(128)}, u32[]{:S(2)}) copy-start(s32[4]{0:T(128)} %valid_ref.1) | copy-start | bytes 52
  25.3 5.5 %collective-permute-start.14 = (bf16[384,128]{1,0:T(8,128)(2,1)S(1)}, bf16[384,128]{1,0:T(8,128)(2,1)S(1)}, u32[]{:S(2)}, u32[]{:S(2)}) collective-permute-start(bf16[384,128]{1,0:T(8,128)(2,1)S(1)} %get-tuple-element.49), channel_id=1, source_target_pairs={{0,12},{1,28},{2,14},{3,30},{4,8},{5,24},{6,10},{7,26},{8,4},{9,20... | collective-permute-start | bytes 294920 | tf_op jit(solution)/shard_map/ppermute | solution.py:136
  30.8 7.8 %collective-permute-start.15 = (bf16[8,256,128]{2,1,0:T(8,128)(2,1)S(1)}, bf16[8,256,128]{2,1,0:T(8,128)(2,1)S(1)}, u32[]{:S(2)}, u32[]{:S(2)}) collective-permute-start(bf16[8,256,128]{2,1,0:T(8,128)(2,1)S(1)} %shard_map.96.kv_ref), channel_id=1, source_target_pairs={{0,1},{1,0},{2,3},{3,2},{4,5},{5,4},{6,7},{7,6},{8,9},{9,8},{10,11... | collective-permute-start | bytes 1572872 | tf_op jit(solution)/shard_map/ppermute | solution.py:126
  37.1 12.8 %collective-permute-start.16 = (bf16[256,1024]{1,0:T(8,128)(2,1)S(1)}, bf16[256,1024]{1,0:T(8,128)(2,1)S(1)}, u32[]{:S(2)}, u32[]{:S(2)}) collective-permute-start(bf16[256,1024]{1,0:T(8,128)(2,1)S(1)} %copy-done.3), channel_id=1, source_target_pairs={{0,1},{1,0},{2,3},{3,2},{4,5},{5,4},{6,7},{7,6},{8,9},{9,8},{10,11... | collective-permute-start | bytes 1572872 | tf_op jit(solution)/shard_map/ppermute | solution.py:126
  45.1 14.0 %all-to-all-start = ((bf16[8,128,128]{2,1,0:T(8,128)(2,1)}), bf16[8,128,128]{2,1,0:T(8,128)(2,1)S(1)}, u32[]{:S(2)}, u32[]{:S(2)}) async-start(bf16[8,128,128]{2,1,0:T(8,128)(2,1)} %shard_map.98), calls=%async_computation | async-start | bytes 524288 | tf_op jit(solution)/shard_map/all_to_all | solution.py:507
  59.5 5.9 %collective-permute-start.18 = (bf16[256,256]{1,0:T(8,128)(2,1)S(1)}, bf16[256,256]{1,0:T(8,128)(2,1)S(1)}, u32[]{:S(2)}, u32[]{:S(2)}) collective-permute-start(bf16[256,256]{1,0:T(8,128)(2,1)S(1)} %get-tuple-element.57), channel_id=1, source_target_pairs={{0,2},{1,3},{2,0},{3,1},{4,6},{5,7},{6,4},{7,5},{8,10},{9,11},{10,... | collective-permute-start | bytes 393224 | tf_op jit(solution)/shard_map/ppermute | solution.py:126
  60.7 5.7 %collective-permute-start.19 = (bf16[256,256]{1,0:T(8,128)(2,1)S(1)}, bf16[256,256]{1,0:T(8,128)(2,1)S(1)}, u32[]{:S(2)}, u32[]{:S(2)}) collective-permute-start(bf16[256,256]{1,0:T(8,128)(2,1)S(1)} %get-tuple-element.58), channel_id=1, source_target_pairs={{0,3},{1,2},{2,1},{3,0},{4,7},{5,6},{6,5},{7,4},{8,11},{9,10},{10,... | collective-permute-start | bytes 393224 | tf_op jit(solution)/shard_map/ppermute | solution.py:126
  61.1 5.4 %collective-permute-start.17 = (bf16[256,256]{1,0:T(8,128)(2,1)S(1)}, bf16[256,256]{1,0:T(8,128)(2,1)S(1)}, u32[]{:S(2)}, u32[]{:S(2)}) collective-permute-start(bf16[256,256]{1,0:T(8,128)(2,1)S(1)} %get-tuple-element.56), channel_id=1, source_target_pairs={{0,1},{1,0},{2,3},{3,2},{4,5},{5,4},{6,7},{7,6},{8,9},{9,8},{10,11... | collective-permute-start | bytes 393224 | tf_op jit(solution)/shard_map/ppermute | solution.py:126

commit v6 on v5

--- a/solution.py
+++ b/solution.py
@@ -184,14 +184,16 @@
     copies = [pltpu.make_async_copy(src, dst, sems.at[i]) for i, (src, dst) in enumerate(pairs)]
     for copy in copies:
         copy.start()
-    for copy in copies:
+    copies[1].wait()
+    bands = [bands_of(w_ref, j) for j in range(KERNEL)]
+    for copy in (copies[0], *copies[2:]):
         copy.wait()
     edge_ref[...] = x_ref[half + RIM :]
     ext = x_ref[...].astype(F32)
     acc = jnp.zeros((half, ext.shape[1]), F32) + b_ref[...]
     for j in range(KERNEL):
         start = RIM + j * DILATION
-        acc += dot_nt(ext[start : start + half].astype(BF16), bands_of(w_ref, j))
+        acc += dot_nt(ext[start : start + half].astype(BF16), bands[j])
     early_ref[0:half] = gelu_mix(ext[2 * RIM :], acc)
     early_ref[half:] = gain_rows(g_ref)
 

time: 67.7 us -> 67.8 us (level)
  no operation moved by 1% of the time
where the time goes in v6:
time: 67.8 us; the launch traced here: 67.3 us
  starting transfers between devices  35.4 us (52%)
  waiting for transfers between devices  18.1 us (27%)
  Pallas kernels  13.6 us (20%)
    ppermute x11, starting transfers between devices, swap(): lax.ppermute(value, 'head', [(i, i ^ bit) for i in range(lax.axis_size('h...  13.9 us
    pallas_call x11, Pallas kernels, call(): pl.pallas_call(kernel, out_shape=outs, in_specs=[pl.BlockSpec(memory_spac...  13.6 us
    ppermute x8, starting transfers between devices, spread(): return lax.ppermute(value, ('tm', 'head'), pairs)  13.2 us
    all_to_all x1, waiting for transfers between devices, on_device(): back = lax.all_to_all(attended, 'tm', 0, 0)  9.21 us
    all_to_all x1, starting transfers between devices, on_device(): back = lax.all_to_all(attended, 'tm', 0, 0)  4.82 us
    ppermute x11, waiting for transfers between devices, swap(): lax.ppermute(value, 'head', [(i, i ^ bit) for i in range(lax.axis_size('h...  4.68 us
    ppermute x8, waiting for transfers between devices, spread(): return lax.ppermute(value, ('tm', 'head'), pairs)  3.46 us
    ppermute x1, starting transfers between devices, from_behind(): lax.ppermute(value, axis, [(source, source + steps) for source in range(f...  3.38 us
  transfers between devices with their start and end apart: 21, of which 8 were waited for; matrix products, arithmetic and copies ran while one was open for 0% of the time, Pallas kernels for 15%

profile of v6, /device:TPU:0, one launch (start us, length us, event | category | flops | bytes accessed | tf_op | source)
XLA Modules:
  0.0 67.3 jit_solution(8482934452502523652)
XLA Ops:
  0.0 2.2 %shard_map.91 = (bf16[264,256]{1,0:T(8,128)(2,1)}, bf16[8,256]{1,0:T(8,128)(2,1)}) custom-call(bf16[512,256]{1,0:T(8,128)(2,1)} %x_ref, bf16[4,64,192]{2,1,0:T(8,128)(2,1)} %bitcast.3, f32[1,256]{1,0:T(1,128)} %bitcast.5, bf16[2,128]{1,0:T(2,128)(2,1)} %bitcast.7), custom_call_target="tpu_custom_call" | custom-call | flops 1500000000 | bytes 5400000 | tf_op jit(solution)/shard_map/pallas_call | solution.py:417
  2.2 0.0 copy-start.7
  2.2 0.0 copy-start.8
  2.2 3.0 %collective-permute-start.1 = (bf16[264,256]{1,0:T(8,128)(2,1)}, bf16[264,256]{1,0:T(8,128)(2,1)S(1)}, u32[]{:S(2)}, u32[]{:S(2)}) collective-permute-start(bf16[264,256]{1,0:T(8,128)(2,1)} %get-tuple-element.32.a_ref.early_ref), channel_id=1, source_target_pairs={{0,2},{1,3},{2,0},{3,1},{4,6},{5,7},{6,4},{7,5},{8,10},{9,11},{10,... | collective-permute-start | bytes 405512 | tf_op jit(solution)/shard_map/ppermute | solution.py:126
  5.3 3.4 %collective-permute-start.7 = (bf16[8,256]{1,0:T(8,128)(2,1)}, bf16[8,256]{1,0:T(8,128)(2,1)S(1)}, u32[]{:S(2)}, u32[]{:S(2)}) collective-permute-start(bf16[8,256]{1,0:T(8,128)(2,1)} %get-tuple-element.37), channel_id=1, source_target_pairs={{0,4},{4,8},{8,12},{12,16},{16,20},{20,24},{24,28},{1,5},{5,9},{9,... | collective-permute-start | bytes 12296 | tf_op jit(solution)/shard_map/ppermute | solution.py:28
  8.7 0.4 shard_map.93
  9.1 0.3 collective-permute-start.2
  9.4 0.7 %collective-permute-done.7.halo_ref = bf16[8,256]{1,0:T(8,128)(2,1)S(1)} collective-permute-done((bf16[8,256]{1,0:T(8,128)(2,1)}, bf16[8,256]{1,0:T(8,128)(2,1)S(1)}, u32[]{:S(2)}, u32[]{:S(2)}) %collective-permute-start.7) | collective-permute-done | bytes 4128 | tf_op jit(solution)/shard_map/ppermute | solution.py:28
  10.2 0.2 shard_map.94.a_ref.late_ref
  10.4 0.8 %collective-permute-start.10 = (bf16[264,256]{1,0:T(8,128)(2,1)S(1)}, bf16[264,256]{1,0:T(8,128)(2,1)S(1)}, u32[]{:S(2)}, u32[]{:S(2)}) collective-permute-start(bf16[264,256]{1,0:T(8,128)(2,1)S(1)} %shard_map.94.a_ref.late_ref), channel_id=1, source_target_pairs={{0,3},{1,2},{2,1},{3,0},{4,7},{5,6},{6,5},{7,4},{8,11},{9,10},{10,... | collective-permute-start | bytes 405512 | tf_op jit(solution)/shard_map/ppermute | solution.py:126
  11.2 0.5 collective-permute-start.9
  11.7 0.0 collective-permute-done.b_ref
  11.7 0.0 collective-permute-done.2.z_ref
  11.8 0.8 %shard_map.92 = (bf16[384,128]{1,0:T(8,128)(2,1)S(1)}, bf16[384,128]{1,0:T(8,128)(2,1)S(1)}, bf16[384,128]{1,0:T(8,128)(2,1)S(1)}, bf16[384,128]{1,0:T(8,128)(2,1)S(1)}) custom-call(bf16[264,256]{1,0:T(8,128)(2,1)S(1)} %copy-done.5, bf16[264,256]{1,0:T(8,128)(2,1)S(1)} %collective-permute-done.b_ref, bf16[264,256]{1,0:T(8,128)(2,1)S(1)} %collective-permute-done.1.y_ref, ...), custom_call_target="tpu_custom_call" | custom-call | flops 1000000000 | bytes 3600000 | tf_op jit(solution)/shard_map/pallas_call | solution.py:417
  12.6 0.6 collective-permute-start.8
  13.3 0.1 collective-permute-start.3
  13.3 4.2 %collective-permute-start.4 = (bf16[384,128]{1,0:T(8,128)(2,1)S(1)}, bf16[384,128]{1,0:T(8,128)(2,1)S(1)}, u32[]{:S(2)}, u32[]{:S(2)}) collective-permute-start(bf16[384,128]{1,0:T(8,128)(2,1)S(1)} %get-tuple-element.34), channel_id=1, source_target_pairs={{0,5},{1,21},{2,7},{3,23},{4,1},{5,17},{6,3},{7,19},{8,13},{9,29},... | collective-permute-start | bytes 294920 | tf_op jit(solution)/shard_map/ppermute | solution.py:136
  17.5 1.4 %collective-permute-start.5 = (bf16[384,128]{1,0:T(8,128)(2,1)S(1)}, bf16[384,128]{1,0:T(8,128)(2,1)S(1)}, u32[]{:S(2)}, u32[]{:S(2)}) collective-permute-start(bf16[384,128]{1,0:T(8,128)(2,1)S(1)} %get-tuple-element.35), channel_id=1, source_target_pairs={{0,9},{1,25},{2,11},{3,27},{4,13},{5,29},{6,15},{7,31},{8,1},{9,17... | collective-permute-start | bytes 294920 | tf_op jit(solution)/shard_map/ppermute | solution.py:136
  19.0 2.8 %collective-permute-start.6 = (bf16[384,128]{1,0:T(8,128)(2,1)S(1)}, bf16[384,128]{1,0:T(8,128)(2,1)S(1)}, u32[]{:S(2)}, u32[]{:S(2)}) collective-permute-start(bf16[384,128]{1,0:T(8,128)(2,1)S(1)} %get-tuple-element.36), channel_id=1, source_target_pairs={{0,13},{1,29},{2,15},{3,31},{4,9},{5,25},{6,11},{7,27},{8,5},{9,21... | collective-permute-start | bytes 294920 | tf_op jit(solution)/shard_map/ppermute | solution.py:136
  21.8 0.0 collective-permute-done.8.b_ref
  21.8 0.8 %shard_map.95 = (bf16[384,128]{1,0:T(8,128)(2,1)S(1)}, bf16[384,128]{1,0:T(8,128)(2,1)S(1)}, bf16[384,128]{1,0:T(8,128)(2,1)S(1)}, bf16[384,128]{1,0:T(8,128)(2,1)S(1)}) custom-call(bf16[264,256]{1,0:T(8,128)(2,1)S(1)} %shard_map.94.a_ref.late_ref, bf16[264,256]{1,0:T(8,128)(2,1)S(1)} %collective-permute-done.8.b_ref, ...), custom_call_target="tpu_custom_call" | custom-call | flops 1000000000 | bytes 3600000 | tf_op jit(solution)/shard_map/pallas_call | solution.py:417
  22.6 0.7 collective-permute-start.11
  23.3 0.0 collective-permute-done.3.refs_0_.rest_0_
  23.3 1.5 %collective-permute-start.12 = (bf16[384,128]{1,0:T(8,128)(2,1)S(1)}, bf16[384,128]{1,0:T(8,128)(2,1)S(1)}, u32[]{:S(2)}, u32[]{:S(2)}) collective-permute-start(bf16[384,128]{1,0:T(8,128)(2,1)S(1)} %get-tuple-element.47), channel_id=1, source_target_pairs={{0,4},{1,20},{2,6},{3,22},{4,0},{5,16},{6,2},{7,18},{8,12},{9,28},... | collective-permute-start | bytes 294920 | tf_op jit(solution)/shard_map/ppermute | solution.py:136
  24.8 0.5 collective-permute-start.13
  25.3 0.0 collective-permute-done.5.refs_2_.rest_2_
  25.3 2.1 %collective-permute-start.14 = (bf16[384,128]{1,0:T(8,128)(2,1)S(1)}, bf16[384,128]{1,0:T(8,128)(2,1)S(1)}, u32[]{:S(2)}, u32[]{:S(2)}) collective-permute-start(bf16[384,128]{1,0:T(8,128)(2,1)S(1)} %get-tuple-element.49), channel_id=1, source_target_pairs={{0,12},{1,28},{2,14},{3,30},{4,8},{5,24},{6,10},{7,26},{8,4},{9,20... | collective-permute-start | bytes 294920 | tf_op jit(solution)/shard_map/ppermute | solution.py:136
  27.4 0.0 collective-permute-done.6.refs_3_.rest_3_
  27.4 0.0 collective-permute-done.11.refs_4_.rest_4_
  27.4 0.9 %collective-permute-done.12.refs_5_.rest_5_ = bf16[384,128]{1,0:T(8,128)(2,1)S(1)} collective-permute-done((bf16[384,128]{1,0:T(8,128)(2,1)S(1)}, bf16[384,128]{1,0:T(8,128)(2,1)S(1)}, u32[]{:S(2)}, u32[]{:S(2)}) %collective-permute-start.12) | collective-permute-done | bytes 98336 | tf_op jit(solution)/shard_map/ppermute | solution.py:136
  28.3 1.1 %collective-permute-done.13.refs_6_.rest_6_ = bf16[384,128]{1,0:T(8,128)(2,1)S(1)} collective-permute-done((bf16[384,128]{1,0:T(8,128)(2,1)S(1)}, bf16[384,128]{1,0:T(8,128)(2,1)S(1)}, u32[]{:S(2)}, u32[]{:S(2)}) %collective-permute-start.13) | collective-permute-done | bytes 98336 | tf_op jit(solution)/shard_map/ppermute | solution.py:136
  29.4 1.4 %collective-permute-done.14.refs_7_.rest_7_ = bf16[384,128]{1,0:T(8,128)(2,1)S(1)} collective-permute-done((bf16[384,128]{1,0:T(8,128)(2,1)S(1)}, bf16[384,128]{1,0:T(8,128)(2,1)S(1)}, u32[]{:S(2)}, u32[]{:S(2)}) %collective-permute-start.14) | collective-permute-done | bytes 98336 | tf_op jit(solution)/shard_map/ppermute | solution.py:136
  30.9 6.2 %collective-permute-start.15 = (bf16[8,256,128]{2,1,0:T(8,128)(2,1)S(1)}, bf16[8,256,128]{2,1,0:T(8,128)(2,1)S(1)}, u32[]{:S(2)}, u32[]{:S(2)}) collective-permute-start(bf16[8,256,128]{2,1,0:T(8,128)(2,1)S(1)} %shard_map.96.kv_ref), channel_id=1, source_target_pairs={{0,1},{1,0},{2,3},{3,2},{4,5},{5,4},{6,7},{7,6},{8,9},{9,8},{10,11... | collective-permute-start | bytes 1572872 | tf_op jit(solution)/shard_map/ppermute | solution.py:126
  37.1 0.1 collective-permute-start.16
  37.2 1.1 %shard_map.97 = (bf16[8,256,128]{2,1,0:T(8,128)(2,1)S(1)}, bf16[8,256,128]{2,1,0:T(8,128)(2,1)S(1)}, bf16[8,256,128]{2,1,0:T(8,128)(2,1)S(1)}, bf16[8,256,128]{2,1,0:T(8,128)(2,1)S(1)}) custom-call(s32[4]{0:T(128)S(1)} %copy-done.9, bf16[8,256,128]{2,1,0:T(8,128)(2,1)S(1)} %shard_map.96.kv_ref, bf16[384,128]{1,0:T(8,128)(2,1)S(1)} %collective-permute-done.3.refs_0_.rest_0_, ...), custom_call_target="tpu_custom_call" | custom-call | flops 800000000 | bytes 2880000 | tf_op jit(solution)/shard_map/pallas_call | solution.py:417
  38.3 0.3 collective-permute-done.15.oth_ref
  38.7 6.5 %shard_map.98 = bf16[8,128,128]{2,1,0:T(8,128)(2,1)} custom-call(bf16[8,256,128]{2,1,0:T(8,128)(2,1)S(1)} %collective-permute-done.15.oth_ref, bf16[8,256,128]{2,1,0:T(8,128)(2,1)S(1)} %get-tuple-element.50.bias_ref, bf16[8,256,128]{2,1,0:T(8,128)(2,1)S(1)} %get-tuple-element.51.k_own, bf16[8,256,128]{2,1,0:T(8,128)(2,1)S(1)} %get-tuple-element.52.v_own, ...), custom_call_target="tpu_custom_call" | custom-call | flops 8000000000 | bytes 28800000 | tf_op jit(solution)/shard_map/pallas_call | solution.py:417
  45.1 4.8 %all-to-all-start = ((bf16[8,128,128]{2,1,0:T(8,128)(2,1)}), bf16[8,128,128]{2,1,0:T(8,128)(2,1)S(1)}, u32[]{:S(2)}, u32[]{:S(2)}) async-start(bf16[8,128,128]{2,1,0:T(8,128)(2,1)} %shard_map.98), calls=%async_computation | async-start | bytes 524288 | tf_op jit(solution)/shard_map/all_to_all | solution.py:509
  49.9 0.0 collective-permute-done.16.w1
  49.9 9.2 %all-to-all-done.att_ref = bf16[8,128,128]{2,1,0:T(8,128)(2,1)S(1)} async-done(((bf16[8,128,128]{2,1,0:T(8,128)(2,1)}), bf16[8,128,128]{2,1,0:T(8,128)(2,1)S(1)}, u32[]{:S(2)}, u32[]{:S(2)}) %all-to-all-start) | async-done | bytes 262176 | tf_op jit(solution)/shard_map/all_to_all | solution.py:509
  59.2 0.4 shard_map.100
  59.5 1.2 %collective-permute-start.18 = (bf16[256,256]{1,0:T(8,128)(2,1)S(1)}, bf16[256,256]{1,0:T(8,128)(2,1)S(1)}, u32[]{:S(2)}, u32[]{:S(2)}) collective-permute-start(bf16[256,256]{1,0:T(8,128)(2,1)S(1)} %get-tuple-element.57), channel_id=1, source_target_pairs={{0,2},{1,3},{2,0},{3,1},{4,6},{5,7},{6,4},{7,5},{8,10},{9,11},{10,... | collective-permute-start | bytes 393224 | tf_op jit(solution)/shard_map/ppermute | solution.py:126
  60.8 0.3 shard_map.99
  61.1 1.0 %collective-permute-start.17 = (bf16[256,256]{1,0:T(8,128)(2,1)S(1)}, bf16[256,256]{1,0:T(8,128)(2,1)S(1)}, u32[]{:S(2)}, u32[]{:S(2)}) collective-permute-start(bf16[256,256]{1,0:T(8,128)(2,1)S(1)} %get-tuple-element.56), channel_id=1, source_target_pairs={{0,1},{1,0},{2,3},{3,2},{4,5},{5,4},{6,7},{7,6},{8,9},{9,8},{10,11... | collective-permute-start | bytes 393224 | tf_op jit(solution)/shard_map/ppermute | solution.py:126
  62.2 3.2 %collective-permute-done.18.across_ref = bf16[256,256]{1,0:T(8,128)(2,1)S(1)} collective-permute-done((bf16[256,256]{1,0:T(8,128)(2,1)S(1)}, bf16[256,256]{1,0:T(8,128)(2,1)S(1)}, u32[]{:S(2)}, u32[]{:S(2)}) %collective-permute-start.18) | collective-permute-done | bytes 131104 | tf_op jit(solution)/shard_map/ppermute | solution.py:126
  65.4 1.1 %collective-permute-done.19.corner_ref = bf16[256,256]{1,0:T(8,128)(2,1)S(1)} collective-permute-done((bf16[256,256]{1,0:T(8,128)(2,1)S(1)}, bf16[256,256]{1,0:T(8,128)(2,1)S(1)}, u32[]{:S(2)}, u32[]{:S(2)}) %collective-permute-start.19) | collective-permute-done | bytes 131104 | tf_op jit(solution)/shard_map/ppermute | solution.py:126
  66.5 0.0 collective-permute-done.17.beside_ref
  66.5 0.8 %shard_map.101 = bf16[512,256]{1,0:T(8,128)(2,1)} custom-call(f32[512,256]{1,0:T(8,128)S(1)} %get-tuple-element.55.base_ref, bf16[256,256]{1,0:T(8,128)(2,1)S(1)} %collective-permute-done.17.beside_ref, bf16[256,256]{1,0:T(8,128)(2,1)S(1)} %collective-permute-done.18.across_ref, bf16[256,256]{1,0:T(8,128)(2,1)S(1)} %collective-permute-done.19.corner_ref), custom_call_target="tpu_custom_call" | custom-call | flops 500000000 | bytes 1800000 | tf_op jit(solution)/shard_map/pallas_call | solution.py:417
  (25 shorter events, 0.1 us)
Async XLA Ops:
  0.0 8.7 %copy-start.4 = (bf16[512,256]{1,0:T(8,128)(2,1)S(1)}, bf16[512,256]{1,0:T(8,128)(2,1)}, u32[]{:S(2)}) copy-start(bf16[512,256]{1,0:T(8,128)(2,1)} %x_ref) | copy-start | bytes 786436
  0.0 8.7 %copy-start.6 = (bf16[4,192,64]{1,2,0:T(8,128)(2,1)S(1)}, bf16[4,192,64]{1,2,0:T(8,128)(2,1)}, u32[]{:S(2)}) copy-start(bf16[4,192,64]{1,2,0:T(8,128)(2,1)} %param.10) | copy-start | bytes 294916
  2.2 6.5 %copy-start.7 = (f32[256]{0:T(256)S(1)}, f32[256]{0:T(256)}, u32[]{:S(2)}) copy-start(f32[256]{0:T(256)} %param.11) | copy-start | bytes 3076
  2.2 6.5 %copy-start.8 = (bf16[256]{0:T(256)(128)(2,1)S(1)}, bf16[256]{0:T(256)(128)(2,1)}, u32[]{:S(2)}) copy-start(bf16[256]{0:T(256)(128)(2,1)} %param.12) | copy-start | bytes 1540
  2.2 6.9 %collective-permute-start.1 = (bf16[264,256]{1,0:T(8,128)(2,1)}, bf16[264,256]{1,0:T(8,128)(2,1)S(1)}, u32[]{:S(2)}, u32[]{:S(2)}) collective-permute-start(bf16[264,256]{1,0:T(8,128)(2,1)} %get-tuple-element.32.a_ref.early_ref), channel_id=1, source_target_pairs={{0,2},{1,3},{2,0},{3,1},{4,6},{5,7},{6,4},{7,5},{8,10},{9,11},{10,... | collective-permute-start | bytes 405512 | tf_op jit(solution)/shard_map/ppermute | solution.py:126
  5.3 6.5 %collective-permute-start = (bf16[264,256]{1,0:T(8,128)(2,1)}, bf16[264,256]{1,0:T(8,128)(2,1)S(1)}, u32[]{:S(2)}, u32[]{:S(2)}) collective-permute-start(bf16[264,256]{1,0:T(8,128)(2,1)} %get-tuple-element.32.a_ref.early_ref), channel_id=1, source_target_pairs={{0,1},{1,0},{2,3},{3,2},{4,5},{5,4},{6,7},{7,6},{8,9},{9,8},{10,11... | collective-permute-start | bytes 405512 | tf_op jit(solution)/shard_map/ppermute | solution.py:126
  5.3 4.9 %collective-permute-start.7 = (bf16[8,256]{1,0:T(8,128)(2,1)}, bf16[8,256]{1,0:T(8,128)(2,1)S(1)}, u32[]{:S(2)}, u32[]{:S(2)}) collective-permute-start(bf16[8,256]{1,0:T(8,128)(2,1)} %get-tuple-element.37), channel_id=1, source_target_pairs={{0,4},{4,8},{8,12},{12,16},{16,20},{20,24},{24,28},{1,5},{5,9},{9,... | collective-permute-start | bytes 12296 | tf_op jit(solution)/shard_map/ppermute | solution.py:28
  9.1 2.6 %collective-permute-start.2 = (bf16[264,256]{1,0:T(8,128)(2,1)S(1)}, bf16[264,256]{1,0:T(8,128)(2,1)S(1)}, u32[]{:S(2)}, u32[]{:S(2)}) collective-permute-start(bf16[264,256]{1,0:T(8,128)(2,1)S(1)} %collective-permute-done.1.y_ref), channel_id=1, source_target_pairs={{0,1},{1,0},{2,3},{3,2},{4,5},{5,4},{6,7},{7,6},{8,9},{9,8},{10,11... | collective-permute-start | bytes 405512 | tf_op jit(solution)/shard_map/ppermute | solution.py:126
  10.2 1.6 %copy-start = (bf16[1024,256]{1,0:T(8,128)(2,1)S(1)}, bf16[1024,256]{1,0:T(8,128)(2,1)}, u32[]{:S(2)}) copy-start(bf16[1024,256]{1,0:T(8,128)(2,1)} %wq.3) | copy-start | bytes 1572868
  10.2 1.6 %copy-start.1 = (bf16[1024,256]{1,0:T(8,128)(2,1)S(1)}, bf16[1024,256]{1,0:T(8,128)(2,1)}, u32[]{:S(2)}) copy-start(bf16[1024,256]{1,0:T(8,128)(2,1)} %wk.3) | copy-start | bytes 1572868
  10.2 1.6 %copy-start.2 = (bf16[1024,256]{1,0:T(8,128)(2,1)S(1)}, bf16[1024,256]{1,0:T(8,128)(2,1)}, u32[]{:S(2)}) copy-start(bf16[1024,256]{1,0:T(8,128)(2,1)} %wv.3) | copy-start | bytes 1572868
  10.2 1.6 %copy-start.5 = (bf16[264,256]{1,0:T(8,128)(2,1)S(1)}, bf16[264,256]{1,0:T(8,128)(2,1)}, u32[]{:S(2)}) copy-start(bf16[264,256]{1,0:T(8,128)(2,1)} %get-tuple-element.32.a_ref.early_ref) | copy-start | bytes 405508
  10.4 7.1 %collective-permute-start.10 = (bf16[264,256]{1,0:T(8,128)(2,1)S(1)}, bf16[264,256]{1,0:T(8,128)(2,1)S(1)}, u32[]{:S(2)}, u32[]{:S(2)}) collective-permute-start(bf16[264,256]{1,0:T(8,128)(2,1)S(1)} %shard_map.94.a_ref.late_ref), channel_id=1, source_target_pairs={{0,3},{1,2},{2,1},{3,0},{4,7},{5,6},{6,5},{7,4},{8,11},{9,10},{10,... | collective-permute-start | bytes 405512 | tf_op jit(solution)/shard_map/ppermute | solution.py:126
  11.2 7.8 %collective-permute-start.9 = (bf16[264,256]{1,0:T(8,128)(2,1)S(1)}, bf16[264,256]{1,0:T(8,128)(2,1)S(1)}, u32[]{:S(2)}, u32[]{:S(2)}) collective-permute-start(bf16[264,256]{1,0:T(8,128)(2,1)S(1)} %shard_map.94.a_ref.late_ref), channel_id=1, source_target_pairs={{0,2},{1,3},{2,0},{3,1},{4,6},{5,7},{6,4},{7,5},{8,10},{9,11},{10,... | collective-permute-start | bytes 405512 | tf_op jit(solution)/shard_map/ppermute | solution.py:126
  12.6 9.2 %collective-permute-start.8 = (bf16[264,256]{1,0:T(8,128)(2,1)S(1)}, bf16[264,256]{1,0:T(8,128)(2,1)S(1)}, u32[]{:S(2)}, u32[]{:S(2)}) collective-permute-start(bf16[264,256]{1,0:T(8,128)(2,1)S(1)} %shard_map.94.a_ref.late_ref), channel_id=1, source_target_pairs={{0,1},{1,0},{2,3},{3,2},{4,5},{5,4},{6,7},{7,6},{8,9},{9,8},{10,11... | collective-permute-start | bytes 405512 | tf_op jit(solution)/shard_map/ppermute | solution.py:126
  13.3 10.1 %collective-permute-start.3 = (bf16[384,128]{1,0:T(8,128)(2,1)S(1)}, bf16[384,128]{1,0:T(8,128)(2,1)S(1)}, u32[]{:S(2)}, u32[]{:S(2)}) collective-permute-start(bf16[384,128]{1,0:T(8,128)(2,1)S(1)} %get-tuple-element.33), channel_id=1, source_target_pairs={{0,1},{1,17},{2,3},{3,19},{4,5},{5,21},{6,7},{7,23},{8,9},{9,25},{... | collective-permute-start | bytes 294920 | tf_op jit(solution)/shard_map/ppermute | solution.py:136
  13.3 11.5 %collective-permute-start.4 = (bf16[384,128]{1,0:T(8,128)(2,1)S(1)}, bf16[384,128]{1,0:T(8,128)(2,1)S(1)}, u32[]{:S(2)}, u32[]{:S(2)}) collective-permute-start(bf16[384,128]{1,0:T(8,128)(2,1)S(1)} %get-tuple-element.34), channel_id=1, source_target_pairs={{0,5},{1,21},{2,7},{3,23},{4,1},{5,17},{6,3},{7,19},{8,13},{9,29},... | collective-permute-start | bytes 294920 | tf_op jit(solution)/shard_map/ppermute | solution.py:136
  17.5 7.8 %collective-permute-start.5 = (bf16[384,128]{1,0:T(8,128)(2,1)S(1)}, bf16[384,128]{1,0:T(8,128)(2,1)S(1)}, u32[]{:S(2)}, u32[]{:S(2)}) collective-permute-start(bf16[384,128]{1,0:T(8,128)(2,1)S(1)} %get-tuple-element.35), channel_id=1, source_target_pairs={{0,9},{1,25},{2,11},{3,27},{4,13},{5,29},{6,15},{7,31},{8,1},{9,17... | collective-permute-start | bytes 294920 | tf_op jit(solution)/shard_map/ppermute | solution.py:136
  19.0 8.4 %collective-permute-start.6 = (bf16[384,128]{1,0:T(8,128)(2,1)S(1)}, bf16[384,128]{1,0:T(8,128)(2,1)S(1)}, u32[]{:S(2)}, u32[]{:S(2)}) collective-permute-start(bf16[384,128]{1,0:T(8,128)(2,1)S(1)} %get-tuple-element.36), channel_id=1, source_target_pairs={{0,13},{1,29},{2,15},{3,31},{4,9},{5,25},{6,11},{7,27},{8,5},{9,21... | collective-permute-start | bytes 294920 | tf_op jit(solution)/shard_map/ppermute | solution.py:136
  22.6 4.7 %collective-permute-start.11 = (bf16[384,128]{1,0:T(8,128)(2,1)S(1)}, bf16[384,128]{1,0:T(8,128)(2,1)S(1)}, u32[]{:S(2)}, u32[]{:S(2)}) collective-permute-start(bf16[384,128]{1,0:T(8,128)(2,1)S(1)} %get-tuple-element.46), channel_id=1, source_target_pairs={{0,0},{1,16},{2,2},{3,18},{4,4},{5,20},{6,6},{7,22},{8,8},{9,24},{... | collective-permute-start | bytes 294920 | tf_op jit(solution)/shard_map/ppermute | solution.py:136
  23.3 5.0 %collective-permute-start.12 = (bf16[384,128]{1,0:T(8,128)(2,1)S(1)}, bf16[384,128]{1,0:T(8,128)(2,1)S(1)}, u32[]{:S(2)}, u32[]{:S(2)}) collective-permute-start(bf16[384,128]{1,0:T(8,128)(2,1)S(1)} %get-tuple-element.47), channel_id=1, source_target_pairs={{0,4},{1,20},{2,6},{3,22},{4,0},{5,16},{6,2},{7,18},{8,12},{9,28},... | collective-permute-start | bytes 294920 | tf_op jit(solution)/shard_map/ppermute | solution.py:136
  24.8 4.6 %collective-permute-start.13 = (bf16[384,128]{1,0:T(8,128)(2,1)S(1)}, bf16[384,128]{1,0:T(8,128)(2,1)S(1)}, u32[]{:S(2)}, u32[]{:S(2)}) collective-permute-start(bf16[384,128]{1,0:T(8,128)(2,1)S(1)} %get-tuple-element.48), channel_id=1, source_target_pairs={{0,8},{1,24},{2,10},{3,26},{4,12},{5,28},{6,14},{7,30},{8,0},{9,16... | collective-permute-start | bytes 294920 | tf_op jit(solution)/shard_map/ppermute | solution.py:136
  25.3 11.8 %copy-start.3 = (bf16[256,1024]{1,0:T(8,128)(2,1)S(1)}, bf16[256,1024]{1,0:T(8,128)(2,1)}, u32[]{:S(2)}) copy-start(bf16[256,1024]{1,0:T(8,128)(2,1)} %w0.3) | copy-start | bytes 1572868
  25.3 11.9 %copy-start.9 = (s32[4]{0:T(128)S(1)}, s32[4]{0:T(128)}, u32[]{:S(2)}) copy-start(s32[4]{0:T(128)} %valid_ref.1) | copy-start | bytes 52
  25.3 5.5 %collective-permute-start.14 = (bf16[384,128]{1,0:T(8,128)(2,1)S(1)}, bf16[384,128]{1,0:T(8,128)(2,1)S(1)}, u32[]{:S(2)}, u32[]{:S(2)}) collective-permute-start(bf16[384,128]{1,0:T(8,128)(2,1)S(1)} %get-tuple-element.49), channel_id=1, source_target_pairs={{0,12},{1,28},{2,14},{3,30},{4,8},{5,24},{6,10},{7,26},{8,4},{9,20... | collective-permute-start | bytes 294920 | tf_op jit(solution)/shard_map/ppermute | solution.py:136
  30.9 7.8 %collective-permute-start.15 = (bf16[8,256,128]{2,1,0:T(8,128)(2,1)S(1)}, bf16[8,256,128]{2,1,0:T(8,128)(2,1)S(1)}, u32[]{:S(2)}, u32[]{:S(2)}) collective-permute-start(bf16[8,256,128]{2,1,0:T(8,128)(2,1)S(1)} %shard_map.96.kv_ref), channel_id=1, source_target_pairs={{0,1},{1,0},{2,3},{3,2},{4,5},{5,4},{6,7},{7,6},{8,9},{9,8},{10,11... | collective-permute-start | bytes 1572872 | tf_op jit(solution)/shard_map/ppermute | solution.py:126
  37.1 12.8 %collective-permute-start.16 = (bf16[256,1024]{1,0:T(8,128)(2,1)S(1)}, bf16[256,1024]{1,0:T(8,128)(2,1)S(1)}, u32[]{:S(2)}, u32[]{:S(2)}) collective-permute-start(bf16[256,1024]{1,0:T(8,128)(2,1)S(1)} %copy-done.3), channel_id=1, source_target_pairs={{0,1},{1,0},{2,3},{3,2},{4,5},{5,4},{6,7},{7,6},{8,9},{9,8},{10,11... | collective-permute-start | bytes 1572872 | tf_op jit(solution)/shard_map/ppermute | solution.py:126
  45.1 14.0 %all-to-all-start = ((bf16[8,128,128]{2,1,0:T(8,128)(2,1)}), bf16[8,128,128]{2,1,0:T(8,128)(2,1)S(1)}, u32[]{:S(2)}, u32[]{:S(2)}) async-start(bf16[8,128,128]{2,1,0:T(8,128)(2,1)} %shard_map.98), calls=%async_computation | async-start | bytes 524288 | tf_op jit(solution)/shard_map/all_to_all | solution.py:509
  59.5 5.9 %collective-permute-start.18 = (bf16[256,256]{1,0:T(8,128)(2,1)S(1)}, bf16[256,256]{1,0:T(8,128)(2,1)S(1)}, u32[]{:S(2)}, u32[]{:S(2)}) collective-permute-start(bf16[256,256]{1,0:T(8,128)(2,1)S(1)} %get-tuple-element.57), channel_id=1, source_target_pairs={{0,2},{1,3},{2,0},{3,1},{4,6},{5,7},{6,4},{7,5},{8,10},{9,11},{10,... | collective-permute-start | bytes 393224 | tf_op jit(solution)/shard_map/ppermute | solution.py:126
  60.8 5.7 %collective-permute-start.19 = (bf16[256,256]{1,0:T(8,128)(2,1)S(1)}, bf16[256,256]{1,0:T(8,128)(2,1)S(1)}, u32[]{:S(2)}, u32[]{:S(2)}) collective-permute-start(bf16[256,256]{1,0:T(8,128)(2,1)S(1)} %get-tuple-element.58), channel_id=1, source_target_pairs={{0,3},{1,2},{2,1},{3,0},{4,7},{5,6},{6,5},{7,4},{8,11},{9,10},{10,... | collective-permute-start | bytes 393224 | tf_op jit(solution)/shard_map/ppermute | solution.py:126
  61.1 5.4 %collective-permute-start.17 = (bf16[256,256]{1,0:T(8,128)(2,1)S(1)}, bf16[256,256]{1,0:T(8,128)(2,1)S(1)}, u32[]{:S(2)}, u32[]{:S(2)}) collective-permute-start(bf16[256,256]{1,0:T(8,128)(2,1)S(1)} %get-tuple-element.56), channel_id=1, source_target_pairs={{0,1},{1,0},{2,3},{3,2},{4,5},{5,4},{6,7},{7,6},{8,9},{9,8},{10,11... | collective-permute-start | bytes 393224 | tf_op jit(solution)/shard_map/ppermute | solution.py:126
